TPU v7x, 32 devices: a whole 2x2x4 slice. The times are simulated.
32 devices in a mesh: section: 2 (over core), expert: 16 (over z, y, x).
Axes of the slice: x: 2, y: 2, z: 4, core: 2. Of those that a mesh axis runs over, the one named last changes fastest.
Arguments:
- sent_forward: bfloat16 [2, 2048, 2048], P('section', 'expert'), may hold values from -6 to 6
- grad_sent: bfloat16 [2, 2048, 2048], P('section', 'expert'), may hold values from -1.796875 to 1.796875
- saved_inputs: bfloat16 [2, 2048, 2048], P('section', 'expert'), may hold values from -6 to 6
- routes_forward: int32 [2, 2048, 2], P('section', 'expert'), may hold values from 0 to 7, all different within a row; in each aligned block of 128 rows (0 to 127, 128 to 255, ..., all dimensions but the last counted through in order) at most 48 rows name the same one
- gates_forward: float32 [2, 2048, 2], P('section', 'expert'), may hold values from 0.1 to 1
- routes_backward: int32 [2, 2048, 2], P('section', 'expert'), may hold values from 0 to 7, all different within a row; in each aligned block of 128 rows (0 to 127, 128 to 255, ..., all dimensions but the last counted through in order) at most 48 rows name the same one
- gates_backward: float32 [2, 2048, 2], P('section', 'expert'), may hold values from 0.1 to 1
- w_gate: bfloat16 [2, 16, 2048, 384], P('section', 'expert'), may hold values from -0.125 to 0.125
- w_up: bfloat16 [2, 16, 2048, 384], P('section', 'expert'), may hold values from -0.125 to 0.125
- w_down: bfloat16 [2, 16, 384, 2048], P('section', 'expert'), may hold values from -0.21875 to 0.21875
Outputs:
- layer_out: bfloat16 [2, 2048, 2048], P('section', 'expert')
- grad_in: bfloat16 [2, 2048, 2048], P('section', 'expert')
- grad_gate: bfloat16 [2, 16, 2048, 384], P('section', 'expert')
- grad_up: bfloat16 [2, 16, 2048, 384], P('section', 'expert')
- grad_down: bfloat16 [2, 16, 384, 2048], P('section', 'expert')
Inputs may be any that keep to these rules, and one draw needn't show every extreme that they name: `routes_forward`: each row names 2 different experts; among the 128 rows of one device no expert is named by more than 48 rows, and in some device's rows one expert is named by exactly 48. `routes_backward`: each row names 2 different experts; among the 128 rows of one device no expert is named by more than 48 rows, and in some device's rows one expert is named by exactly 48.
All inputs are finite; a program needn't handle non-finite values.
Results may differ from a plain program's by a relative error of at most 0.0065.
Values may be sent and summed in bfloat16 or wider, within the bound.
No kernel may reach another device: no remote copies, remote signals or barrier semaphores. Data moves between devices by JAX's collectives and lax.ppermute only.
A program may use at most 128 MiB of HBM per device.

v0:
```python
import jax
import jax.numpy as jnp
from jax import lax
from jax.sharding import PartitionSpec as P


def passed_along(array, axis, by):
    size = lax.axis_size(axis)
    return lax.ppermute(array, axis, [(i, (i + by) % size) for i in range(size)])


def route_tables(routes, gates, experts, capacity):
    flat_ids = routes.reshape(-1)
    hits = (flat_ids[:, None] == jnp.arange(experts, dtype=jnp.int32)[None, :]).astype(jnp.int32)
    earlier = jnp.cumsum(hits, axis=0) - hits
    slot_ids = jnp.sum(earlier * hits, axis=1)
    target = flat_ids * capacity + slot_ids
    placed = (target[:, None] == jnp.arange(experts * capacity, dtype=jnp.int32)[None, :]).astype(
        jnp.float32
    )
    placed = placed.reshape(routes.shape[0], routes.shape[1], experts * capacity)
    dispatch = jnp.sum(placed, axis=1)
    slot_gate = jnp.sum(placed * gates[:, :, None], axis=(0, 1))
    return (dispatch, slot_gate, target.reshape(routes.shape))


def gather_rows(dispatch, values):
    return lax.dot_general(
        dispatch.astype(jnp.bfloat16),
        values,
        (((0,), (0,)), ((), ())),
        preferred_element_type=jnp.float32,
    ).astype(jnp.bfloat16)


def pick_rows(target, slot_values):
    picked = jnp.take(slot_values, target.reshape(-1), axis=0)
    return picked.reshape(target.shape[0], target.shape[1], slot_values.shape[1])


def half_forward(inputs, gate_matrix, up_matrix, down_matrix):
    gate_act = jnp.dot(inputs, gate_matrix, preferred_element_type=jnp.float32)
    up_act = jnp.dot(inputs, up_matrix, preferred_element_type=jnp.float32)
    hidden = (gate_act * jax.nn.sigmoid(gate_act) * up_act).astype(jnp.bfloat16)
    return jnp.dot(hidden, down_matrix, preferred_element_type=jnp.float32).astype(jnp.bfloat16)


def weight_terms(inputs, upstream, hidden, d_gate, d_up):
    outer = (((0,), (0,)), ((), ()))
    return jnp.stack(
        [
            lax.dot_general(inputs, d_gate, outer, preferred_element_type=jnp.float32),
            lax.dot_general(inputs, d_up, outer, preferred_element_type=jnp.float32),
            lax.dot_general(upstream, hidden, outer, preferred_element_type=jnp.float32),
        ]
    )


def rounded_pair(lower, upper):
    lower_r = lax.optimization_barrier(lower.astype(jnp.bfloat16)).astype(jnp.float32)
    upper_r = lax.optimization_barrier(upper.astype(jnp.bfloat16)).astype(jnp.float32)
    return lower_r + upper_r


def half_backward(inputs, upstream, gate_matrix, up_matrix, down_matrix, sources, capacity):
    gate_act = jnp.dot(inputs, gate_matrix, preferred_element_type=jnp.float32)
    up_act = jnp.dot(inputs, up_matrix, preferred_element_type=jnp.float32)
    sigma = jax.nn.sigmoid(gate_act)
    swish = gate_act * sigma
    hidden = (swish * up_act).astype(jnp.bfloat16)
    inner = (((1,), (1,)), ((), ()))
    d_hidden = lax.dot_general(upstream, down_matrix, inner, preferred_element_type=jnp.float32)
    d_gate = (d_hidden * up_act * sigma * (1.0 + gate_act * (1.0 - sigma))).astype(jnp.bfloat16)
    d_up = (d_hidden * swish).astype(jnp.bfloat16)
    back = lax.dot_general(d_gate, gate_matrix, inner, preferred_element_type=jnp.float32)
    back = back + lax.dot_general(d_up, up_matrix, inner, preferred_element_type=jnp.float32)

    def slot_half(values, half):
        width = values.shape[-1]
        return values.reshape(sources, 2, capacity // 2, width)[:, half].reshape(-1, width)

    lower = weight_terms(
        slot_half(inputs, 0),
        slot_half(upstream, 0),
        slot_half(hidden, 0),
        slot_half(d_gate, 0),
        slot_half(d_up, 0),
    )
    upper = weight_terms(
        slot_half(inputs, 1),
        slot_half(upstream, 1),
        slot_half(hidden, 1),
        slot_half(d_gate, 1),
        slot_half(d_up, 1),
    )
    return (back.astype(jnp.bfloat16), rounded_pair(lower, upper))


def per_device(
    sent_forward,
    grad_sent,
    saved_inputs,
    routes_forward,
    gates_forward,
    routes_backward,
    gates_backward,
    w_gate,
    w_up,
    w_down,
):
    devices = lax.axis_size("expert")
    experts = devices // 2
    tokens = sent_forward.shape[1]
    model_width = sent_forward.shape[2]
    hidden_half = w_gate.shape[3]
    chosen = routes_forward.shape[2]
    capacity = 3 * tokens * chosen // (2 * experts)
    arrived = passed_along(sent_forward, "section", 1)[0]
    returned = passed_along(grad_sent, "section", -1)[0]
    dispatch_forward, slot_gate_forward, target_forward = route_tables(
        routes_forward[0], gates_forward[0], experts, capacity
    )
    dispatch_backward, slot_gate_backward, target_backward = route_tables(
        routes_backward[0], gates_backward[0], experts, capacity
    )
    slots_forward = gather_rows(dispatch_forward, arrived)
    slots_backward = gather_rows(dispatch_backward, saved_inputs[0])
    picked_grad = gather_rows(dispatch_backward, returned)
    slots_grad = (picked_grad.astype(jnp.float32) * slot_gate_backward[:, None]).astype(
        jnp.bfloat16
    )
    own_gate = w_gate[0, 0]
    own_up = w_up[0, 0]
    own_down = w_down[0, 0]

    def outbound(slot_values):
        return jnp.repeat(slot_values.reshape(experts, capacity, model_width), 2, axis=0)

    def inbound(received):
        return received.reshape(-1, model_width)

    def collect(coming_back):
        halves = coming_back.reshape(experts, 2, capacity, model_width).astype(jnp.float32)
        return jnp.sum(halves, axis=1).reshape(experts * capacity, model_width)

    got_forward, got_backward, got_grad = (
        lax.all_to_all(outbound(slots_forward), "expert", split_axis=0, concat_axis=0, tiled=True),
        lax.all_to_all(outbound(slots_backward), "expert", split_axis=0, concat_axis=0, tiled=True),
        lax.all_to_all(outbound(slots_grad), "expert", split_axis=0, concat_axis=0, tiled=True),
    )
    forward_local = half_forward(inbound(got_forward), own_gate, own_up, own_down).reshape(
        devices, capacity, model_width
    )
    back_rows, local_grads = half_backward(
        inbound(got_backward), inbound(got_grad), own_gate, own_up, own_down, devices, capacity
    )
    back_local = back_rows.reshape(devices, capacity, model_width)
    part_forward, part_backward = (
        lax.all_to_all(forward_local, "expert", split_axis=0, concat_axis=0, tiled=True),
        lax.all_to_all(back_local, "expert", split_axis=0, concat_axis=0, tiled=True),
    )
    picked_out = pick_rows(target_forward, collect(part_forward))
    layer_out = jnp.sum(picked_out * gates_forward[0][:, :, None], axis=1).astype(jnp.bfloat16)
    picked_back = pick_rows(target_backward, collect(part_backward))
    grad_in = jnp.sum(picked_back, axis=1).astype(jnp.bfloat16)
    grad_gate = local_grads[0].astype(jnp.bfloat16).reshape(1, 1, model_width, hidden_half)
    grad_up = local_grads[1].astype(jnp.bfloat16).reshape(1, 1, model_width, hidden_half)
    grad_down = (
        jnp.transpose(local_grads[2]).astype(jnp.bfloat16).reshape(1, 1, hidden_half, model_width)
    )
    return (layer_out[None], grad_in[None], grad_gate, grad_up, grad_down)


def solution(mesh):
    return jax.shard_map(
        per_device,
        mesh=mesh,
        in_specs=(
            P("section", "expert", None),
            P("section", "expert", None),
            P("section", "expert", None),
            P("section", "expert", None),
            P("section", "expert", None),
            P("section", "expert", None),
            P("section", "expert", None),
            P("section", "expert", None, None),
            P("section", "expert", None, None),
            P("section", "expert", None, None),
        ),
        out_specs=(
            P("section", "expert", None),
            P("section", "expert", None),
            P("section", "expert", None, None),
            P("section", "expert", None, None),
            P("section", "expert", None, None),
        ),
        check_vma=False,
    )
```

profile of v0, /device:TPU:12, one launch (start us, length us, event | category | flops | bytes accessed | tf_op | source)
XLA Modules:
  0.0 413.4 jit_solution(15379348896950277437)
XLA Ops:
  7.6 7.3 %all-to-all-start.3 = ((bf16[16,48,2048]{2,1,0:T(8,128)(2,1)}), bf16[16,48,2048]{2,1,0:T(8,128)(2,1)}, u32[]{:S(2)}, u32[]{:S(2)}) async-start(bf16[16,48,2048]{2,1,0:T(8,128)(2,1)} %bitcast.198), calls=%async_computation.3 | async-start | bytes 6291456 | tf_op jit(solution)/shard_map/all_to_all | solution.py:148
  18.7 66.8 %all-to-all-done.3 = bf16[16,48,2048]{2,1,0:T(8,128)(2,1)} async-done(((bf16[16,48,2048]{2,1,0:T(8,128)(2,1)}), bf16[16,48,2048]{2,1,0:T(8,128)(2,1)}, u32[]{:S(2)}, u32[]{:S(2)}) %all-to-all-start.3) | async-done | bytes 3145760 | tf_op jit(solution)/shard_map/all_to_all | solution.py:148
  87.5 5.6 %all-to-all-start = ((bf16[16,48,2048]{2,1,0:T(8,128)(2,1)}), bf16[16,48,2048]{2,1,0:T(8,128)(2,1)}, u32[]{:S(2)}, u32[]{:S(2)}) async-start(bf16[16,48,2048]{2,1,0:T(8,128)(2,1)} %bitcast.199), calls=%async_computation | async-start | bytes 6291456 | tf_op jit(solution)/shard_map/all_to_all | solution.py:147
  95.7 67.4 %all-to-all-done = bf16[16,48,2048]{2,1,0:T(8,128)(2,1)} async-done(((bf16[16,48,2048]{2,1,0:T(8,128)(2,1)}), bf16[16,48,2048]{2,1,0:T(8,128)(2,1)}, u32[]{:S(2)}, u32[]{:S(2)}) %all-to-all-start) | async-done | bytes 3145760 | tf_op jit(solution)/shard_map/all_to_all | solution.py:147
  165.2 5.0 %all-to-all-start.2 = ((bf16[16,48,2048]{2,1,0:T(8,128)(2,1)}), bf16[16,48,2048]{2,1,0:T(8,128)(2,1)}, u32[]{:S(2)}, u32[]{:S(2)}) async-start(bf16[16,48,2048]{2,1,0:T(8,128)(2,1)} %bitcast.200), calls=%async_computation.2 | async-start | bytes 6291456 | tf_op jit(solution)/shard_map/all_to_all | solution.py:149
  170.1 4.7 %fusion.18 = f32[768,384]{1,0:T(8,128)} fusion(bf16[768,2048]{1,0:T(8,128)(2,1)} %bitcast.6, bf16[1,1,2048,384]{3,2,1,0:T(8,128)(2,1)S(1)} %copy-done.2), kind=kOutput, calls=%fused_computation.45 | convolution fusion | flops 1207959552 | bytes 5898240 | tf_op jit(solution)/shard_map/dot_general | solution.py:42
  174.8 7.8 %convolution_convert_fusion = bf16[768,2048]{1,0:T(8,128)(2,1)} fusion(bf16[1,1,384,2048]{3,2,1,0:T(8,128)(2,1)} %param.21, bf16[768,2048]{1,0:T(8,128)(2,1)} %bitcast.6, bf16[1,1,2048,384]{3,2,1,0:T(8,128)(2,1)S(1)} %copy-done, f32[768,384]{1,0:T(8,128)} %fusion.18), kind=kOutput, calls=%fused_computation.8 | convolution fusion | flops 2419261440 | bytes 10616832 | tf_op jit(solution)/shard_map/dot_general | solution.py:45
  182.6 57.5 %all-to-all-done.2 = bf16[16,48,2048]{2,1,0:T(8,128)(2,1)} async-done(((bf16[16,48,2048]{2,1,0:T(8,128)(2,1)}), bf16[16,48,2048]{2,1,0:T(8,128)(2,1)}, u32[]{:S(2)}, u32[]{:S(2)}) %all-to-all-start.2) | async-done | bytes 3145760 | tf_op jit(solution)/shard_map/all_to_all | solution.py:149
  240.1 5.3 %all-to-all-start.1 = ((bf16[16,48,2048]{2,1,0:T(8,128)(2,1)}), bf16[16,48,2048]{2,1,0:T(8,128)(2,1)}, u32[]{:S(2)}, u32[]{:S(2)}) async-start(bf16[16,48,2048]{2,1,0:T(8,128)(2,1)} %bitcast.204), calls=%async_computation.1 | async-start | bytes 6291456 | tf_op jit(solution)/shard_map/all_to_all | solution.py:159
  245.5 3.8 fusion.16
  249.3 3.7 fusion.6
  253.1 4.9 %multiply_convert_fusion.1 = (bf16[768,384]{1,0:T(8,128)(2,1)}, bf16[768,384]{1,0:T(8,128)(2,1)S(1)}, bf16[768,384]{1,0:T(8,128)(2,1)S(1)}) fusion(f32[768,384]{1,0:T(8,128)S(1)} %fusion.16, f32[768,384]{1,0:T(8,128)S(1)} %fusion.6, bf16[768,2048]{1,0:T(8,128)(2,1)} %bitcast.26, bf16[1,1,2048,384]{3,2,1,0:T(8,128)(2,1)S(1)} %copy-done), kind=kOutput, calls=%fused_computation.49 | convolution fusion | flops 1212383232 | bytes 8847360 | tf_op jit(solution)/shard_map/dot_general | solution.py:67
  259.8 3.5 add_convert_fusion.1
  263.4 2.6 fusion.3
  266.0 49.1 %all-to-all-done.1 = bf16[16,48,2048]{2,1,0:T(8,128)(2,1)} async-done(((bf16[16,48,2048]{2,1,0:T(8,128)(2,1)}), bf16[16,48,2048]{2,1,0:T(8,128)(2,1)}, u32[]{:S(2)}, u32[]{:S(2)}) %all-to-all-start.1) | async-done | bytes 3145760 | tf_op jit(solution)/shard_map/all_to_all | solution.py:159
  315.0 5.3 %all-to-all-start.4 = ((bf16[16,48,2048]{2,1,0:T(8,128)(2,1)}), bf16[16,48,2048]{2,1,0:T(8,128)(2,1)}, u32[]{:S(2)}, u32[]{:S(2)}) async-start(bf16[16,48,2048]{2,1,0:T(8,128)(2,1)} %bitcast.27), calls=%async_computation.4 | async-start | bytes 6291456 | tf_op jit(solution)/shard_map/all_to_all | solution.py:160
  320.4 2.6 fusion.4
  323.1 2.6 fusion.5
  326.8 2.6 fusion
  329.3 2.6 fusion.2
  331.9 2.6 fusion.1
  336.3 2.1 slice_bitcast_fusion
  340.1 2.9 convert_reduce_fusion.1
  343.0 2.7 gather_fusion
  347.5 2.5 reshape.237
  350.1 40.0 %all-to-all-done.4 = bf16[16,48,2048]{2,1,0:T(8,128)(2,1)} async-done(((bf16[16,48,2048]{2,1,0:T(8,128)(2,1)}), bf16[16,48,2048]{2,1,0:T(8,128)(2,1)}, u32[]{:S(2)}, u32[]{:S(2)}) %all-to-all-start.4) | async-done | bytes 3145760 | tf_op jit(solution)/shard_map/all_to_all | solution.py:160
  390.1 2.9 convert_reduce_fusion
  393.0 2.7 gather_fusion.1
  395.7 3.1 broadcast_select_fusion
  398.8 3.6 reshape.247
  402.4 5.6 %multiply_reduce_fusion = bf16[128,2048]{1,0:T(8,128)(2,1)} fusion(f32[128,2,2048]{2,1,0:T(2,128)} %reshape.237, f32[128,2]{1,0:T(8,128)S(1)} %copy.49), kind=kLoop, calls=%fused_computation.25 | loop fusion | flops 786432 | bytes 2622464 | tf_op jit(solution)/shard_map/reduce_sum | solution.py:163
  408.0 5.0 %reduce_sum.95 = bf16[128,2048]{1,0:T(8,128)(2,1)} reduce(f32[128,2,2048]{2,1,0:T(2,128)} %reshape.247, f32[]{:T(128)} %constant.23.clone.1), dimensions={1}, to_apply=%region_12.14 | reduce | flops 262144 | bytes 2621444 | tf_op jit(solution)/shard_map/reduce_sum | solution.py:165
  (73 shorter events, 25.6 us)
Async XLA Ops:
  0.6 174.2 %copy-start = (bf16[1,1,2048,384]{3,2,1,0:T(8,128)(2,1)S(1)}, bf16[1,1,2048,384]{3,2,1,0:T(8,128)(2,1)}, u32[]{:S(2)}) copy-start(bf16[1,1,2048,384]{3,2,1,0:T(8,128)(2,1)} %param.20) | copy-start | bytes 4718596
  7.6 7.3 %copy-start.10 = (bf16[1,128,2048]{2,1,0:T(8,128)(2,1)S(1)}, bf16[1,128,2048]{2,1,0:T(8,128)(2,1)}, u32[]{:S(2)}) copy-start(bf16[1,128,2048]{2,1,0:T(8,128)(2,1)} %param.12) | copy-start | bytes 1572868
  7.6 7.4 %copy-start.7 = (s32[1,128,2]{1,2,0:T(2,128)S(1)}, s32[1,128,2]{1,2,0:T(2,128)}, u32[]{:S(2)}) copy-start(s32[1,128,2]{1,2,0:T(2,128)} %param.15) | copy-start | bytes 3076
  7.6 77.8 %all-to-all-start.3 = ((bf16[16,48,2048]{2,1,0:T(8,128)(2,1)}), bf16[16,48,2048]{2,1,0:T(8,128)(2,1)}, u32[]{:S(2)}, u32[]{:S(2)}) async-start(bf16[16,48,2048]{2,1,0:T(8,128)(2,1)} %bitcast.198), calls=%async_computation.3 | async-start | bytes 6291456 | tf_op jit(solution)/shard_map/all_to_all | solution.py:148
  14.9 2.1 collective-permute-start
  87.5 5.6 %copy-start.11 = (bf16[1,128,2048]{2,1,0:T(8,128)(2,1)S(1)}, bf16[1,128,2048]{2,1,0:T(8,128)(2,1)}, u32[]{:S(2)}) copy-start(bf16[1,128,2048]{2,1,0:T(8,128)(2,1)} %param.13) | copy-start | bytes 1572868
  87.5 75.6 %all-to-all-start = ((bf16[16,48,2048]{2,1,0:T(8,128)(2,1)}), bf16[16,48,2048]{2,1,0:T(8,128)(2,1)}, u32[]{:S(2)}, u32[]{:S(2)}) async-start(bf16[16,48,2048]{2,1,0:T(8,128)(2,1)} %bitcast.199), calls=%async_computation | async-start | bytes 6291456 | tf_op jit(solution)/shard_map/all_to_all | solution.py:147
  93.2 2.0 collective-permute-start.1
  165.2 5.0 %copy-start.2 = (bf16[1,1,2048,384]{3,2,1,0:T(8,128)(2,1)S(1)}, bf16[1,1,2048,384]{3,2,1,0:T(8,128)(2,1)}, u32[]{:S(2)}) copy-start(bf16[1,1,2048,384]{3,2,1,0:T(8,128)(2,1)} %param.19) | copy-start | bytes 4718596
  165.2 74.9 %all-to-all-start.2 = ((bf16[16,48,2048]{2,1,0:T(8,128)(2,1)}), bf16[16,48,2048]{2,1,0:T(8,128)(2,1)}, u32[]{:S(2)}, u32[]{:S(2)}) async-start(bf16[16,48,2048]{2,1,0:T(8,128)(2,1)} %bitcast.200), calls=%async_computation.2 | async-start | bytes 6291456 | tf_op jit(solution)/shard_map/all_to_all | solution.py:149
  240.1 5.3 %copy-start.8 = (f32[1,128,2]{1,2,0:T(2,128)S(1)}, f32[1,128,2]{1,2,0:T(2,128)}, u32[]{:S(2)}) copy-start(f32[1,128,2]{1,2,0:T(2,128)} %param.16) | copy-start | bytes 3076
  240.1 75.0 %all-to-all-start.1 = ((bf16[16,48,2048]{2,1,0:T(8,128)(2,1)}), bf16[16,48,2048]{2,1,0:T(8,128)(2,1)}, u32[]{:S(2)}, u32[]{:S(2)}) async-start(bf16[16,48,2048]{2,1,0:T(8,128)(2,1)} %bitcast.204), calls=%async_computation.1 | async-start | bytes 6291456 | tf_op jit(solution)/shard_map/all_to_all | solution.py:159
  245.5 3.8 copy-start.9
  258.0 1.8 copy-start.5
  258.0 5.4 %copy-start.3 = (bf16[768,384]{1,0:T(8,128)(2,1)}, bf16[768,384]{1,0:T(8,128)(2,1)S(1)}, u32[]{:S(2)}) copy-start(bf16[768,384]{1,0:T(8,128)(2,1)S(1)} %get-tuple-element.31) | copy-start | bytes 1769476
  315.0 5.4 %copy-start.6 = (bf16[768,384]{1,0:T(8,128)(2,1)S(1)}, bf16[768,384]{1,0:T(8,128)(2,1)}, u32[]{:S(2)}) copy-start(bf16[768,384]{1,0:T(8,128)(2,1)} %copy-done.5) | copy-start | bytes 1769476
  315.0 75.1 %all-to-all-start.4 = ((bf16[16,48,2048]{2,1,0:T(8,128)(2,1)}), bf16[16,48,2048]{2,1,0:T(8,128)(2,1)}, u32[]{:S(2)}, u32[]{:S(2)}) async-start(bf16[16,48,2048]{2,1,0:T(8,128)(2,1)} %bitcast.27), calls=%async_computation.4 | async-start | bytes 6291456 | tf_op jit(solution)/shard_map/all_to_all | solution.py:160
  320.4 2.7 copy-start.12
  325.7 1.1 copy-start.4
  398.8 14.1 %copy-start.1 = (bf16[1,1,2048,384]{3,2,1,0:T(8,128)(2,1)S(1)}, bf16[1,1,2048,384]{3,2,1,0:T(8,128)(2,1)}, u32[]{:S(2)}) copy-start(bf16[1,1,2048,384]{3,2,1,0:T(8,128)(2,1)} %param.20) | copy-start | bytes 4718596
where the time goes:
time: 420 us; the launch traced here: 413 us
  waiting for transfers between devices  283 us (67%)
  matrix products  49.7 us (12%)
  starting transfers between devices  28.7 us (7%)
  other arithmetic  26.2 us (6%)
  local copies, waits for them, and re-layouts  24.5 us (6%)
    all_to_all x1, waiting for transfers between devices, per_device(): lax.all_to_all(outbound(slots_forward), 'expert', split_axis=0, concat_ax...  67.4 us
    all_to_all x1, waiting for transfers between devices, per_device(): lax.all_to_all(outbound(slots_backward), 'expert', split_axis=0, concat_a...  66.8 us
    all_to_all x1, waiting for transfers between devices, per_device(): lax.all_to_all(outbound(slots_grad), 'expert', split_axis=0, concat_axis=...  57.5 us
    all_to_all x1, waiting for transfers between devices, per_device(): lax.all_to_all(forward_local, 'expert', split_axis=0, concat_axis=0, tile...  49.1 us
    all_to_all x1, waiting for transfers between devices, per_device(): lax.all_to_all(back_local, 'expert', split_axis=0, concat_axis=0, tiled=T...  40 us
  transfers between devices with their start and end apart: 7, of which 7 were waited for; matrix products, arithmetic and copies ran while one was open for 16% of the time, Pallas kernels for 0%

commit v1 on v0

v1 whole, which is shorter than its diff:
```python
import functools

import jax
import jax.numpy as jnp
from jax import lax
from jax.experimental import pallas as pl
from jax.experimental.pallas import tpu as pltpu
from jax.sharding import PartitionSpec as P

VMEM_LIMIT = 48 << 20


def whole(n):
    return [pl.BlockSpec(memory_space=pltpu.VMEM)] * n


def params():
    return pltpu.CompilerParams(vmem_limit_bytes=VMEM_LIMIT)


def placement(me, routes, experts, capacity):
    tokens = routes.shape[1]
    rel = lax.bitwise_xor(routes, me)
    expert_row = lax.broadcasted_iota(jnp.int32, (experts, tokens), 0)
    first = rel[0:1, :] == expert_row
    second = rel[1:2, :] == expert_row
    hits = (first | second).astype(jnp.bfloat16)
    before = lax.broadcasted_iota(jnp.int32, (tokens, tokens), 0) < lax.broadcasted_iota(
        jnp.int32, (tokens, tokens), 1
    )
    earlier = jnp.dot(hits, before.astype(jnp.bfloat16), preferred_element_type=jnp.float32)
    slot0 = jnp.sum(jnp.where(first, earlier, 0.0), axis=0, keepdims=True).astype(jnp.int32)
    slot1 = jnp.sum(jnp.where(second, earlier, 0.0), axis=0, keepdims=True).astype(jnp.int32)
    place = lax.broadcasted_iota(jnp.int32, (experts * capacity, tokens), 0)
    at0 = place == rel[0:1, :] * capacity + slot0
    at1 = place == rel[1:2, :] * capacity + slot1
    return at0, at1


def as_bf16(mask):
    return mask.astype(jnp.float32).astype(jnp.bfloat16)


def dispatch_kernel(experts, capacity, scaled, me_ref, routes_ref, *refs):
    if scaled:
        gates_ref, values_ref, *out_refs = refs
    else:
        values_ref, *out_refs = refs
    at0, at1 = placement(me_ref[0], routes_ref[...], experts, capacity)
    picked = jnp.dot(as_bf16(at0 | at1), values_ref[...], preferred_element_type=jnp.float32)
    if scaled:
        gate = jnp.where(at0, gates_ref[0:1, :], 0.0) + jnp.where(at1, gates_ref[1:2, :], 0.0)
        picked = picked * jnp.sum(gate, axis=1, keepdims=True)
    picked = picked.astype(jnp.bfloat16)
    for i, out in enumerate(out_refs):
        out[...] = picked[i * capacity : (i + 1) * capacity, :]


def dispatch(me, routes, values, experts, capacity, gates=None):
    width = values.shape[1]
    operands = (me, routes) + (() if gates is None else (gates,)) + (values,)
    return pl.pallas_call(
        functools.partial(dispatch_kernel, experts, capacity, gates is not None),
        out_shape=[jax.ShapeDtypeStruct((capacity, width), jnp.bfloat16)] * experts,
        in_specs=[pl.BlockSpec(memory_space=pltpu.SMEM)] + whole(len(operands) - 1),
        out_specs=whole(experts),
        compiler_params=params(),
        cost_estimate=pl.CostEstimate(
            flops=2 * experts * capacity * values.size,
            bytes_accessed=2 * (values.size + experts * capacity * width),
            transcendentals=0,
        ),
        name="dispatch",
    )(*operands)


def combine_kernel(experts, capacity, scaled, me_ref, routes_ref, *refs):
    if scaled:
        gates_ref, *refs = refs
    *in_refs, out_ref, rows = refs
    for i, ref in enumerate(in_refs):
        rows[i * capacity : (i + 1) * capacity, :] = ref[...]
    at0, at1 = placement(me_ref[0], routes_ref[...], experts, capacity)
    outer = (((0,), (0,)), ((), ()))

    def pick(table):
        return lax.dot_general(
            table, rows[...], outer, preferred_element_type=jnp.float32
        )

    if scaled:
        gate = jnp.where(at0, gates_ref[0:1, :], 0.0) + jnp.where(at1, gates_ref[1:2, :], 0.0)
        high = gate.astype(jnp.bfloat16)
        low = (gate - high.astype(jnp.float32)).astype(jnp.bfloat16)
        out_ref[...] = (pick(high) + pick(low)).astype(jnp.bfloat16)
    else:
        out_ref[...] = pick(as_bf16(at0 | at1)).astype(jnp.bfloat16)


def combine(me, routes, pieces, experts, capacity, gates=None):
    width = pieces[0].shape[1]
    tokens = routes.shape[1]
    operands = (me, routes) + (() if gates is None else (gates,)) + tuple(pieces)
    return pl.pallas_call(
        functools.partial(combine_kernel, experts, capacity, gates is not None),
        out_shape=jax.ShapeDtypeStruct((tokens, width), jnp.bfloat16),
        in_specs=[pl.BlockSpec(memory_space=pltpu.SMEM)] + whole(len(operands) - 1),
        out_specs=pl.BlockSpec(memory_space=pltpu.VMEM),
        scratch_shapes=[pltpu.VMEM((experts * capacity, width), jnp.bfloat16)],
        compiler_params=params(),
        cost_estimate=pl.CostEstimate(
            flops=2 * tokens * experts * capacity * width,
            bytes_accessed=2 * (tokens * width + experts * capacity * width),
            transcendentals=0,
        ),
        name="combine",
    )(*operands)


def forward_kernel(pieces, capacity, *refs):
    in_refs = refs[:pieces]
    gate_ref, up_ref, down_ref = refs[pieces : pieces + 3]
    out_refs = refs[pieces + 3 : 2 * pieces + 3]
    rows = refs[-1]
    for i, ref in enumerate(in_refs):
        rows[i * capacity : (i + 1) * capacity, :] = ref[...]
    gate_act = jnp.dot(rows[...], gate_ref[...], preferred_element_type=jnp.float32)
    up_act = jnp.dot(rows[...], up_ref[...], preferred_element_type=jnp.float32)
    hidden = (gate_act * jax.nn.sigmoid(gate_act) * up_act).astype(jnp.bfloat16)
    part = jnp.dot(hidden, down_ref[...], preferred_element_type=jnp.float32).astype(jnp.bfloat16)
    for i, out in enumerate(out_refs):
        out[...] = part[i * capacity : (i + 1) * capacity, :]


def forward_half(pieces, gate, up, down):
    n = len(pieces)
    capacity, width = pieces[0].shape
    hidden = gate.shape[1]
    return pl.pallas_call(
        functools.partial(forward_kernel, n, capacity),
        out_shape=[jax.ShapeDtypeStruct((capacity, width), jnp.bfloat16)] * n,
        in_specs=whole(n + 3),
        out_specs=whole(n),
        scratch_shapes=[pltpu.VMEM((n * capacity, width), jnp.bfloat16)],
        compiler_params=params(),
        cost_estimate=pl.CostEstimate(
            flops=6 * n * capacity * width * hidden,
            bytes_accessed=4 * n * capacity * width + 6 * width * hidden,
            transcendentals=n * capacity * hidden,
        ),
        name="forward_half",
    )(*pieces, gate, up, down)


def backward_kernel(pieces, capacity, *refs):
    in_refs = refs[:pieces]
    up_refs = refs[pieces : 2 * pieces]
    gate_ref, up_ref, down_ref = refs[2 * pieces : 2 * pieces + 3]
    out_refs = refs[2 * pieces + 3 : 3 * pieces + 3]
    hidden_ref, d_gate_ref, d_up_ref, rows, upstream = refs[3 * pieces + 3 :]
    for i in range(pieces):
        rows[i * capacity : (i + 1) * capacity, :] = in_refs[i][...]
        upstream[i * capacity : (i + 1) * capacity, :] = up_refs[i][...]
    inner = (((1,), (1,)), ((), ()))
    gate_act = jnp.dot(rows[...], gate_ref[...], preferred_element_type=jnp.float32)
    up_act = jnp.dot(rows[...], up_ref[...], preferred_element_type=jnp.float32)
    d_hidden = lax.dot_general(
        upstream[...], down_ref[...], inner, preferred_element_type=jnp.float32
    )
    sigma = jax.nn.sigmoid(gate_act)
    swish = gate_act * sigma
    hidden_ref[...] = (swish * up_act).astype(jnp.bfloat16)
    d_gate = (d_hidden * up_act * sigma * (1.0 + gate_act * (1.0 - sigma))).astype(jnp.bfloat16)
    d_up = (d_hidden * swish).astype(jnp.bfloat16)
    d_gate_ref[...] = d_gate
    d_up_ref[...] = d_up
    back = lax.dot_general(d_gate, gate_ref[...], inner, preferred_element_type=jnp.float32)
    back = back + lax.dot_general(d_up, up_ref[...], inner, preferred_element_type=jnp.float32)
    back = back.astype(jnp.bfloat16)
    for i, out in enumerate(out_refs):
        out[...] = back[i * capacity : (i + 1) * capacity, :]


def backward_half(pieces, upstream, gate, up, down):
    n = len(pieces)
    capacity, width = pieces[0].shape
    hidden = gate.shape[1]
    small = jax.ShapeDtypeStruct((n * capacity, hidden), jnp.bfloat16)
    out = pl.pallas_call(
        functools.partial(backward_kernel, n, capacity),
        out_shape=[jax.ShapeDtypeStruct((capacity, width), jnp.bfloat16)] * n + [small] * 3,
        in_specs=whole(2 * n + 3),
        out_specs=whole(n + 3),
        scratch_shapes=[pltpu.VMEM((n * capacity, width), jnp.bfloat16)] * 2,
        compiler_params=params(),
        cost_estimate=pl.CostEstimate(
            flops=10 * n * capacity * width * hidden,
            bytes_accessed=6 * n * capacity * width + 6 * width * hidden,
            transcendentals=n * capacity * hidden,
        ),
        name="backward_half",
    )(*pieces, *upstream, gate, up, down)
    return out[:n], out[n], out[n + 1], out[n + 2]


def add_pair(a, b):
    return (a.astype(jnp.float32) + b.astype(jnp.float32)).astype(jnp.bfloat16)


def per_device(
    sent_forward,
    grad_sent,
    saved_inputs,
    routes_forward,
    gates_forward,
    routes_backward,
    gates_backward,
    w_gate,
    w_up,
    w_down,
):
    devices = lax.axis_size("expert")
    experts = devices // 2
    sections = lax.axis_size("section")
    tokens = sent_forward.shape[1]
    chosen = routes_forward.shape[2]
    capacity = 3 * tokens * chosen // (2 * experts)
    me = (lax.axis_index("expert") // 2).astype(jnp.int32).reshape(1)

    def along(array, by):
        return lax.ppermute(array, "section", [(i, (i + by) % sections) for i in range(sections)])

    def to_xor(array, mask):
        return lax.ppermute(array, "expert", [(i, i ^ mask) for i in range(devices)])

    def spread(pieces):
        own = [pieces[0]] + [to_xor(pieces[d], 2 * d) for d in range(1, experts)]
        other = [to_xor(piece, 1) for piece in own]
        return own, other

    def gather_back(own, other):
        summed = [add_pair(own[d], to_xor(other[d], 1)) for d in range(experts)]
        return [summed[0]] + [to_xor(summed[d], 2 * d) for d in range(1, experts)]

    routes_f, gates_f = routes_forward[0].T, gates_forward[0].T
    routes_b, gates_b = routes_backward[0].T, gates_backward[0].T
    own_gate, own_up, own_down = w_gate[0, 0], w_up[0, 0], w_down[0, 0]

    slots_x = dispatch(me, routes_b, saved_inputs[0], experts, capacity)
    returned = along(grad_sent, -1)[0]
    slots_g = dispatch(me, routes_b, returned, experts, capacity, gates_b)
    arrived = along(sent_forward, 1)[0]
    slots_f = dispatch(me, routes_f, arrived, experts, capacity)

    x_own, x_other = spread(slots_x)
    g_own, g_other = spread(slots_g)
    f_own, f_other = spread(slots_f)

    back_own, hid_own, dg_own, du_own = backward_half(x_own, g_own, own_gate, own_up, own_down)
    back_other, hid_other, dg_other, du_other = backward_half(
        x_other, g_other, own_gate, own_up, own_down
    )
    back = gather_back(back_own, back_other)

    out_own = forward_half(f_own, own_gate, own_up, own_down)
    out_other = forward_half(f_other, own_gate, own_up, own_down)
    out = gather_back(out_own, out_other)

    inputs = jnp.concatenate(list(x_own) + list(x_other))
    upstream = jnp.concatenate(list(g_own) + list(g_other))
    hidden = jnp.concatenate([hid_own, hid_other])
    d_gate = jnp.concatenate([dg_own, dg_other])
    d_up = jnp.concatenate([du_own, du_other])
    outer = (((0,), (0,)), ((), ()))

    def weight_term(a, b):
        return lax.dot_general(a, b, outer, preferred_element_type=jnp.float32).astype(jnp.bfloat16)

    grad_gate = weight_term(inputs, d_gate)
    grad_up = weight_term(inputs, d_up)
    grad_down = weight_term(hidden, upstream)

    grad_in = combine(me, routes_b, back, experts, capacity)
    layer_out = combine(me, routes_f, out, experts, capacity, gates_f)
    return (
        layer_out[None],
        grad_in[None],
        grad_gate[None, None],
        grad_up[None, None],
        grad_down[None, None],
    )


def solution(mesh):
    rows = P("section", "expert", None)
    weights = P("section", "expert", None, None)
    return jax.shard_map(
        per_device,
        mesh=mesh,
        in_specs=(rows,) * 7 + (weights,) * 3,
        out_specs=(rows, rows, weights, weights, weights),
        check_vma=False,
    )
```

time: 420 us -> 324 us (0.77)
  the two profiles are of different devices: /device:TPU:12 before, /device:TPU:0 now
where the time goes in v1:
time: 324 us
  waiting for transfers between devices  154 us (48%)
  starting transfers between devices  127 us (39%)
  Pallas kernels  28.1 us (9%)
  matrix products  10.6 us (3%)
    ppermute x75, waiting for transfers between devices, to_xor(): lax.ppermute(array, 'expert', [(i, i ^ mask) for i in range(devices)])  154 us
    ppermute x75, starting transfers between devices, to_xor(): lax.ppermute(array, 'expert', [(i, i ^ mask) for i in range(devices)])  126 us
    pallas_call x2, Pallas kernels, backward_half(): pl.pallas_call(functools.partial(backward_kernel, n, capacity), out_shape...  13.8 us
    dot_general x3, matrix products, weight_term(): lax.dot_general(a, b, outer, preferred_element_type=jnp.float32)  10.6 us
    pallas_call x2, Pallas kernels, forward_half(): pl.pallas_call(functools.partial(forward_kernel, n, capacity), out_shape=...  9.07 us
  transfers between devices with their start and end apart: 77, of which 42 were waited for; matrix products, arithmetic and copies ran while one was open for 4% of the time, Pallas kernels for 8%

profile of v1, /device:TPU:0, one launch (start us, length us, event | category | flops | bytes accessed | tf_op | source)
XLA Modules:
  0.0 323.7 jit_solution(2038264161400739874)
XLA Ops:
  11.7 2.8 collective-permute-start.34
  16.5 4.1 %collective-permute-done.33.refs_3_ = bf16[48,2048]{1,0:T(8,128)(2,1)S(1)} collective-permute-done((bf16[48,2048]{1,0:T(8,128)(2,1)S(1)}, bf16[48,2048]{1,0:T(8,128)(2,1)S(1)}, u32[]{:S(2)}, u32[]{:S(2)}) %collective-permute-start.33) | collective-permute-done | bytes 196640 | tf_op jit(solution)/shard_map/ppermute | solution.py:234
  22.1 10.7 %collective-permute-done.34.refs_4_ = bf16[48,2048]{1,0:T(8,128)(2,1)S(1)} collective-permute-done((bf16[48,2048]{1,0:T(8,128)(2,1)S(1)}, bf16[48,2048]{1,0:T(8,128)(2,1)S(1)}, u32[]{:S(2)}, u32[]{:S(2)}) %collective-permute-start.34) | collective-permute-done | bytes 196640 | tf_op jit(solution)/shard_map/ppermute | solution.py:234
  32.8 4.5 %collective-permute-start.37 = (bf16[48,2048]{1,0:T(8,128)(2,1)S(1)}, bf16[48,2048]{1,0:T(8,128)(2,1)S(1)}, u32[]{:S(2)}, u32[]{:S(2)}) collective-permute-start(bf16[48,2048]{1,0:T(8,128)(2,1)S(1)} %get-tuple-element.98), channel_id=1, source_target_pairs={{0,14},{1,15},{2,12},{3,13},{4,10},{5,11},{6,8},{7,9},{8,6},{9,7},... | collective-permute-start | bytes 589832 | tf_op jit(solution)/shard_map/ppermute | solution.py:234
  37.4 5.3 %collective-permute-done.35.refs_5_ = bf16[48,2048]{1,0:T(8,128)(2,1)S(1)} collective-permute-done((bf16[48,2048]{1,0:T(8,128)(2,1)S(1)}, bf16[48,2048]{1,0:T(8,128)(2,1)S(1)}, u32[]{:S(2)}, u32[]{:S(2)}) %collective-permute-start.35) | collective-permute-done | bytes 196640 | tf_op jit(solution)/shard_map/ppermute | solution.py:234
  46.5 4.0 %collective-permute-done.47.refs_1_ = bf16[48,2048]{1,0:T(8,128)(2,1)S(1)} collective-permute-done((bf16[48,2048]{1,0:T(8,128)(2,1)S(1)}, bf16[48,2048]{1,0:T(8,128)(2,1)S(1)}, u32[]{:S(2)}, u32[]{:S(2)}) %collective-permute-start.47) | collective-permute-done | bytes 196640 | tf_op jit(solution)/shard_map/ppermute | solution.py:234
  52.0 2.7 collective-permute-done.48.refs_2_
  56.2 2.7 collective-permute-done.49.refs_3_
  60.4 2.7 collective-permute-done.50.refs_4_
  64.6 2.7 collective-permute-done.51.refs_5_
  67.4 4.2 %collective-permute-done.52.refs_6_ = bf16[48,2048]{1,0:T(8,128)(2,1)S(1)} collective-permute-done((bf16[48,2048]{1,0:T(8,128)(2,1)S(1)}, bf16[48,2048]{1,0:T(8,128)(2,1)S(1)}, u32[]{:S(2)}, u32[]{:S(2)}) %collective-permute-start.52) | collective-permute-done | bytes 196640 | tf_op jit(solution)/shard_map/ppermute | solution.py:234
  71.6 3.8 %collective-permute-done.53.refs_7_ = bf16[48,2048]{1,0:T(8,128)(2,1)S(1)} collective-permute-done((bf16[48,2048]{1,0:T(8,128)(2,1)S(1)}, bf16[48,2048]{1,0:T(8,128)(2,1)S(1)}, u32[]{:S(2)}, u32[]{:S(2)}) %collective-permute-start.53) | collective-permute-done | bytes 196640 | tf_op jit(solution)/shard_map/ppermute | solution.py:234
  76.2 3.6 %collective-permute-start.40 = (bf16[48,2048]{1,0:T(8,128)(2,1)S(1)}, bf16[48,2048]{1,0:T(8,128)(2,1)S(1)}, u32[]{:S(2)}, u32[]{:S(2)}) collective-permute-start(bf16[48,2048]{1,0:T(8,128)(2,1)S(1)} %get-tuple-element.101), channel_id=1, source_target_pairs={{0,4},{1,5},{2,6},{3,7},{4,0},{5,1},{6,2},{7,3},{8,12},{9,13},{10,... | collective-permute-start | bytes 589832 | tf_op jit(solution)/shard_map/ppermute | solution.py:234
  80.0 4.0 %collective-permute-start.42 = (bf16[48,2048]{1,0:T(8,128)(2,1)S(1)}, bf16[48,2048]{1,0:T(8,128)(2,1)S(1)}, u32[]{:S(2)}, u32[]{:S(2)}) collective-permute-start(bf16[48,2048]{1,0:T(8,128)(2,1)S(1)} %get-tuple-element.103), channel_id=1, source_target_pairs={{0,8},{1,9},{2,10},{3,11},{4,12},{5,13},{6,14},{7,15},{8,0},{9,1},... | collective-permute-start | bytes 589832 | tf_op jit(solution)/shard_map/ppermute | solution.py:234
  88.1 4.0 %collective-permute-done.40.refs_10_ = bf16[48,2048]{1,0:T(8,128)(2,1)S(1)} collective-permute-done((bf16[48,2048]{1,0:T(8,128)(2,1)S(1)}, bf16[48,2048]{1,0:T(8,128)(2,1)S(1)}, u32[]{:S(2)}, u32[]{:S(2)}) %collective-permute-start.40) | collective-permute-done | bytes 196640 | tf_op jit(solution)/shard_map/ppermute | solution.py:234
  97.9 12.9 %collective-permute-done.43.refs_13_ = bf16[48,2048]{1,0:T(8,128)(2,1)S(1)} collective-permute-done((bf16[48,2048]{1,0:T(8,128)(2,1)S(1)}, bf16[48,2048]{1,0:T(8,128)(2,1)S(1)}, u32[]{:S(2)}, u32[]{:S(2)}) %collective-permute-start.43) | collective-permute-done | bytes 196640 | tf_op jit(solution)/shard_map/ppermute | solution.py:234
  110.8 4.7 %collective-permute-start.3 = (bf16[48,2048]{1,0:T(8,128)(2,1)S(1)}, bf16[48,2048]{1,0:T(8,128)(2,1)S(1)}, u32[]{:S(2)}, u32[]{:S(2)}) collective-permute-start(bf16[48,2048]{1,0:T(8,128)(2,1)S(1)} %get-tuple-element.70), channel_id=1, source_target_pairs={{0,6},{1,7},{2,4},{3,5},{4,2},{5,3},{6,0},{7,1},{8,14},{9,15},{10,... | collective-permute-start | bytes 589832 | tf_op jit(solution)/shard_map/ppermute | solution.py:234
  115.6 5.2 %collective-permute-start.4 = (bf16[48,2048]{1,0:T(8,128)(2,1)S(1)}, bf16[48,2048]{1,0:T(8,128)(2,1)S(1)}, u32[]{:S(2)}, u32[]{:S(2)}) collective-permute-start(bf16[48,2048]{1,0:T(8,128)(2,1)S(1)} %get-tuple-element.71), channel_id=1, source_target_pairs={{0,8},{1,9},{2,10},{3,11},{4,12},{5,13},{6,14},{7,15},{8,0},{9,1},... | collective-permute-start | bytes 589832 | tf_op jit(solution)/shard_map/ppermute | solution.py:234
  120.8 6.8 %backward_half.2 = (bf16[48,2048]{1,0:T(8,128)(2,1)S(1)}, bf16[48,2048]{1,0:T(8,128)(2,1)S(1)}, bf16[48,2048]{1,0:T(8,128)(2,1)S(1)}, bf16[48,2048]{1,0:T(8,128)...) custom-call(bf16[48,2048]{1,0:T(8,128)(2,1)S(1)} %get-tuple-element., ...), custom_call_target="tpu_custom_call" | custom-call | flops 3019898880 | bytes 9437184 | tf_op jit(solution)/shard_map/backward_half/pallas_call | solution.py:189
  134.6 10.4 %collective-permute-done.5.refs_5_ = bf16[48,2048]{1,0:T(8,128)(2,1)S(1)} collective-permute-done((bf16[48,2048]{1,0:T(8,128)(2,1)S(1)}, bf16[48,2048]{1,0:T(8,128)(2,1)S(1)}, u32[]{:S(2)}, u32[]{:S(2)}) %collective-permute-start.5) | collective-permute-done | bytes 196640 | tf_op jit(solution)/shard_map/ppermute | solution.py:234
  150.6 4.5 %forward_half.2 = (bf16[48,2048]{1,0:T(8,128)(2,1)S(1)}, bf16[48,2048]{1,0:T(8,128)(2,1)S(1)}, bf16[48,2048]{1,0:T(8,128)(2,1)S(1)}, bf16[48,2048]{1,0:T(8,128)(...) custom-call(bf16[48,2048]{1,0:T(8,128)(2,1)S(1)} %get-tuple-element., ...), custom_call_target="tpu_custom_call" | custom-call | flops 1811939328 | bytes 7864320 | tf_op jit(solution)/shard_map/forward_half/pallas_call | solution.py:139
  171.2 6.9 %backward_half.3 = (bf16[48,2048]{1,0:T(8,128)(2,1)S(1)}, bf16[48,2048]{1,0:T(8,128)(2,1)S(1)}, bf16[48,2048]{1,0:T(8,128)(2,1)S(1)}, bf16[48,2048]{1,0:T(8,128)...) custom-call(bf16[48,2048]{1,0:T(8,128)(2,1)S(1)} %collective-permute, ...), custom_call_target="tpu_custom_call" | custom-call | flops 3019898880 | bytes 9437184 | tf_op jit(solution)/shard_map/backward_half/pallas_call | solution.py:189
  178.1 5.0 %fusion.1 = bf16[1,1,2048,384]{3,2,1,0:T(8,128)(2,1)} fusion(bf16[768,2048]{1,0:T(8,128)(2,1)} %copy-done.8, bf16[384,384]{1,0:T(8,128)(2,1)S(1)} %get-tuple-element.126, bf16[384,384]{1,0:T(8,128)(2,1)S(1)} %get-tuple-element.125), kind=kOutput, calls=%fused_computation.4 | convolution fusion | flops 1209925632 | bytes 5308416 | tf_op jit(solution)/shard_map/dot_general | solution.py:277
  183.1 3.0 fusion
  204.9 4.5 %forward_half.3 = (bf16[48,2048]{1,0:T(8,128)(2,1)S(1)}, bf16[48,2048]{1,0:T(8,128)(2,1)S(1)}, bf16[48,2048]{1,0:T(8,128)(2,1)S(1)}, bf16[48,2048]{1,0:T(8,128)(...) custom-call(bf16[48,2048]{1,0:T(8,128)(2,1)S(1)} %collective-permute, ...), custom_call_target="tpu_custom_call" | custom-call | flops 1811939328 | bytes 7864320 | tf_op jit(solution)/shard_map/forward_half/pallas_call | solution.py:139
  253.9 3.0 collective-permute-start.76
  263.7 2.9 collective-permute-done.17
  270.3 9.1 %collective-permute-start.66 = (bf16[48,2048]{1,0:T(8,128)(2,1)S(1)}, bf16[48,2048]{1,0:T(8,128)(2,1)S(1)}, u32[]{:S(2)}, u32[]{:S(2)}) collective-permute-start(bf16[48,2048]{1,0:T(8,128)(2,1)S(1)} %add_convert_fusion.5), channel_id=1, source_target_pairs={{0,4},{1,5},{2,6},{3,7},{4,0},{5,1},{6,2},{7,3},{8,12},{9,13},{10,... | collective-permute-start | bytes 589832 | tf_op jit(solution)/shard_map/ppermute | solution.py:234
  279.5 7.5 %collective-permute-done.72.refs_5_ = bf16[48,2048]{1,0:T(8,128)(2,1)S(1)} collective-permute-done((bf16[48,2048]{1,0:T(8,128)(2,1)S(1)}, bf16[48,2048]{1,0:T(8,128)(2,1)S(1)}, u32[]{:S(2)}, u32[]{:S(2)}) %collective-permute-start.72) | collective-permute-done | bytes 196640 | tf_op jit(solution)/shard_map/ppermute | solution.py:234
  289.2 10.9 %collective-permute-done.70.refs_4_ = bf16[48,2048]{1,0:T(8,128)(2,1)S(1)} collective-permute-done((bf16[48,2048]{1,0:T(8,128)(2,1)S(1)}, bf16[48,2048]{1,0:T(8,128)(2,1)S(1)}, u32[]{:S(2)}, u32[]{:S(2)}) %collective-permute-start.70) | collective-permute-done | bytes 196640 | tf_op jit(solution)/shard_map/ppermute | solution.py:234
  302.6 4.3 %collective-permute-start.24 = (bf16[48,2048]{1,0:T(8,128)(2,1)S(1)}, bf16[48,2048]{1,0:T(8,128)(2,1)S(1)}, u32[]{:S(2)}, u32[]{:S(2)}) collective-permute-start(bf16[48,2048]{1,0:T(8,128)(2,1)S(1)} %add_convert_fusion.11), channel_id=1, source_target_pairs={{0,8},{1,9},{2,10},{3,11},{4,12},{5,13},{6,14},{7,15},{8,0},{9,1},... | collective-permute-start | bytes 589832 | tf_op jit(solution)/shard_map/ppermute | solution.py:234
  313.2 7.6 %collective-permute-done.26.refs_6_ = bf16[48,2048]{1,0:T(8,128)(2,1)S(1)} collective-permute-done((bf16[48,2048]{1,0:T(8,128)(2,1)S(1)}, bf16[48,2048]{1,0:T(8,128)(2,1)S(1)}, u32[]{:S(2)}, u32[]{:S(2)}) %collective-permute-start.26) | collective-permute-done | bytes 196640 | tf_op jit(solution)/shard_map/ppermute | solution.py:234
  (202 shorter events, 151.2 us)
Async XLA Ops:
  0.6 74.8 %collective-permute-start.38 = (bf16[1,128,2048]{2,1,0:T(8,128)(2,1)}, bf16[1,128,2048]{2,1,0:T(8,128)(2,1)S(1)}, u32[]{:S(2)}, u32[]{:S(2)}) collective-permute-start(bf16[1,128,2048]{2,1,0:T(8,128)(2,1)} %param.11), channel_id=1, source_target_pairs={{0,16},{16,0},{1,17},{17,1},{2,18},{18,2},{3,19},{19,3},{4,20},{20... | collective-permute-start | bytes 1572872 | tf_op jit(solution)/shard_map/ppermute | solution.py:231
  7.8 37.2 %collective-permute-start.46 = (bf16[48,2048]{1,0:T(8,128)(2,1)S(1)}, bf16[48,2048]{1,0:T(8,128)(2,1)S(1)}, u32[]{:S(2)}, u32[]{:S(2)}) collective-permute-start(bf16[48,2048]{1,0:T(8,128)(2,1)S(1)} %get-tuple-element.91.refs_0_), channel_id=1, source_target_pairs={{0,1},{1,0},{2,3},{3,2},{4,5},{5,4},{6,7},{7,6},{8,9},{9,8},{10,11... | collective-permute-start | bytes 589832 | tf_op jit(solution)/shard_map/ppermute | solution.py:234
  11.7 21.1 %collective-permute-start.34 = (bf16[48,2048]{1,0:T(8,128)(2,1)S(1)}, bf16[48,2048]{1,0:T(8,128)(2,1)S(1)}, u32[]{:S(2)}, u32[]{:S(2)}) collective-permute-start(bf16[48,2048]{1,0:T(8,128)(2,1)S(1)} %get-tuple-element.95), channel_id=1, source_target_pairs={{0,8},{1,9},{2,10},{3,11},{4,12},{5,13},{6,14},{7,15},{8,0},{9,1},... | collective-permute-start | bytes 589832 | tf_op jit(solution)/shard_map/ppermute | solution.py:234
  14.6 28.1 %collective-permute-start.35 = (bf16[48,2048]{1,0:T(8,128)(2,1)S(1)}, bf16[48,2048]{1,0:T(8,128)(2,1)S(1)}, u32[]{:S(2)}, u32[]{:S(2)}) collective-permute-start(bf16[48,2048]{1,0:T(8,128)(2,1)S(1)} %get-tuple-element.96), channel_id=1, source_target_pairs={{0,10},{1,11},{2,8},{3,9},{4,14},{5,15},{6,12},{7,13},{8,2},{9,3},... | collective-permute-start | bytes 589832 | tf_op jit(solution)/shard_map/ppermute | solution.py:234
  20.5 22.2 %collective-permute-start.36 = (bf16[48,2048]{1,0:T(8,128)(2,1)S(1)}, bf16[48,2048]{1,0:T(8,128)(2,1)S(1)}, u32[]{:S(2)}, u32[]{:S(2)}) collective-permute-start(bf16[48,2048]{1,0:T(8,128)(2,1)S(1)} %get-tuple-element.97), channel_id=1, source_target_pairs={{0,12},{1,13},{2,14},{3,15},{4,8},{5,9},{6,10},{7,11},{8,4},{9,5},... | collective-permute-start | bytes 589832 | tf_op jit(solution)/shard_map/ppermute | solution.py:234
  42.7 41.4 %collective-permute-start = (bf16[1,128,2048]{2,1,0:T(8,128)(2,1)}, bf16[1,128,2048]{2,1,0:T(8,128)(2,1)S(1)}, u32[]{:S(2)}, u32[]{:S(2)}) collective-permute-start(bf16[1,128,2048]{2,1,0:T(8,128)(2,1)} %param.10), channel_id=1, source_target_pairs={{0,16},{16,0},{1,17},{17,1},{2,18},{18,2},{3,19},{19,3},{4,20},{20... | collective-permute-start | bytes 1572872 | tf_op jit(solution)/shard_map/ppermute | solution.py:231
  84.1 43.6 %collective-permute-start.54 = (bf16[48,2048]{1,0:T(8,128)(2,1)S(1)}, bf16[48,2048]{1,0:T(8,128)(2,1)S(1)}, u32[]{:S(2)}, u32[]{:S(2)}) collective-permute-start(bf16[48,2048]{1,0:T(8,128)(2,1)S(1)} %get-tuple-element.99.refs_8_), channel_id=1, source_target_pairs={{0,1},{1,0},{2,3},{3,2},{4,5},{5,4},{6,7},{7,6},{8,9},{9,8},{10,11... | collective-permute-start | bytes 589832 | tf_op jit(solution)/shard_map/ppermute | solution.py:234
  86.3 24.5 %collective-permute-start.43 = (bf16[48,2048]{1,0:T(8,128)(2,1)S(1)}, bf16[48,2048]{1,0:T(8,128)(2,1)S(1)}, u32[]{:S(2)}, u32[]{:S(2)}) collective-permute-start(bf16[48,2048]{1,0:T(8,128)(2,1)S(1)} %get-tuple-element.104), channel_id=1, source_target_pairs={{0,10},{1,11},{2,8},{3,9},{4,14},{5,15},{6,12},{7,13},{8,2},{9,3},... | collective-permute-start | bytes 589832 | tf_op jit(solution)/shard_map/ppermute | solution.py:234
  97.3 31.3 %collective-permute-start.1 = (bf16[48,2048]{1,0:T(8,128)(2,1)S(1)}, bf16[48,2048]{1,0:T(8,128)(2,1)S(1)}, u32[]{:S(2)}, u32[]{:S(2)}) collective-permute-start(bf16[48,2048]{1,0:T(8,128)(2,1)S(1)} %get-tuple-element.68), channel_id=1, source_target_pairs={{0,2},{1,3},{2,0},{3,1},{4,6},{5,7},{6,4},{7,5},{8,10},{9,11},{10,... | collective-permute-start | bytes 589832 | tf_op jit(solution)/shard_map/ppermute | solution.py:234
  110.8 21.7 %collective-permute-start.3 = (bf16[48,2048]{1,0:T(8,128)(2,1)S(1)}, bf16[48,2048]{1,0:T(8,128)(2,1)S(1)}, u32[]{:S(2)}, u32[]{:S(2)}) collective-permute-start(bf16[48,2048]{1,0:T(8,128)(2,1)S(1)} %get-tuple-element.70), channel_id=1, source_target_pairs={{0,6},{1,7},{2,4},{3,5},{4,2},{5,3},{6,0},{7,1},{8,14},{9,15},{10,... | collective-permute-start | bytes 589832 | tf_op jit(solution)/shard_map/ppermute | solution.py:234
  155.2 31.1 %collective-permute-start.8 = (bf16[48,2048]{1,0:T(8,128)(2,1)S(1)}, bf16[48,2048]{1,0:T(8,128)(2,1)S(1)}, u32[]{:S(2)}, u32[]{:S(2)}) collective-permute-start(bf16[48,2048]{1,0:T(8,128)(2,1)S(1)} %get-tuple-element.67.refs_0_), channel_id=1, source_target_pairs={{0,1},{1,0},{2,3},{3,2},{4,5},{5,4},{6,7},{7,6},{8,9},{9,8},{10,11... | collective-permute-start | bytes 589832 | tf_op jit(solution)/shard_map/ppermute | solution.py:234
  157.0 29.9 %collective-permute-start.10 = (bf16[48,2048]{1,0:T(8,128)(2,1)S(1)}, bf16[48,2048]{1,0:T(8,128)(2,1)S(1)}, u32[]{:S(2)}, u32[]{:S(2)}) collective-permute-start(bf16[48,2048]{1,0:T(8,128)(2,1)S(1)} %collective-permute-done.2.refs_2_), channel_id=1, source_target_pairs={{0,1},{1,0},{2,3},{3,2},{4,5},{5,4},{6,7},{7,6},{8,9},{9,8},{10,11... | collective-permute-start | bytes 589832 | tf_op jit(solution)/shard_map/ppermute | solution.py:234
  161.2 27.2 %collective-permute-start.11 = (bf16[48,2048]{1,0:T(8,128)(2,1)S(1)}, bf16[48,2048]{1,0:T(8,128)(2,1)S(1)}, u32[]{:S(2)}, u32[]{:S(2)}) collective-permute-start(bf16[48,2048]{1,0:T(8,128)(2,1)S(1)} %collective-permute-done.3.refs_3_), channel_id=1, source_target_pairs={{0,1},{1,0},{2,3},{3,2},{4,5},{5,4},{6,7},{7,6},{8,9},{9,8},{10,11... | collective-permute-start | bytes 589832 | tf_op jit(solution)/shard_map/ppermute | solution.py:234
  165.4 23.5 %collective-permute-start.12 = (bf16[48,2048]{1,0:T(8,128)(2,1)S(1)}, bf16[48,2048]{1,0:T(8,128)(2,1)S(1)}, u32[]{:S(2)}, u32[]{:S(2)}) collective-permute-start(bf16[48,2048]{1,0:T(8,128)(2,1)S(1)} %collective-permute-done.4.refs_4_), channel_id=1, source_target_pairs={{0,1},{1,0},{2,3},{3,2},{4,5},{5,4},{6,7},{7,6},{8,9},{9,8},{10,11... | collective-permute-start | bytes 589832 | tf_op jit(solution)/shard_map/ppermute | solution.py:234
  169.6 23.4 %collective-permute-start.13 = (bf16[48,2048]{1,0:T(8,128)(2,1)S(1)}, bf16[48,2048]{1,0:T(8,128)(2,1)S(1)}, u32[]{:S(2)}, u32[]{:S(2)}) collective-permute-start(bf16[48,2048]{1,0:T(8,128)(2,1)S(1)} %collective-permute-done.5.refs_5_), channel_id=1, source_target_pairs={{0,1},{1,0},{2,3},{3,2},{4,5},{5,4},{6,7},{7,6},{8,9},{9,8},{10,11... | collective-permute-start | bytes 589832 | tf_op jit(solution)/shard_map/ppermute | solution.py:234
  194.9 21.1 %collective-permute-start.71 = (bf16[48,2048]{1,0:T(8,128)(2,1)S(1)}, bf16[48,2048]{1,0:T(8,128)(2,1)S(1)}, u32[]{:S(2)}, u32[]{:S(2)}) collective-permute-start(bf16[48,2048]{1,0:T(8,128)(2,1)S(1)} %get-tuple-element.118), channel_id=1, source_target_pairs={{0,1},{1,0},{2,3},{3,2},{4,5},{5,4},{6,7},{7,6},{8,9},{9,8},{10,11... | collective-permute-start | bytes 589832 | tf_op jit(solution)/shard_map/ppermute | solution.py:234
  199.1 21.1 %collective-permute-start.69 = (bf16[48,2048]{1,0:T(8,128)(2,1)S(1)}, bf16[48,2048]{1,0:T(8,128)(2,1)S(1)}, u32[]{:S(2)}, u32[]{:S(2)}) collective-permute-start(bf16[48,2048]{1,0:T(8,128)(2,1)S(1)} %get-tuple-element.116), channel_id=1, source_target_pairs={{0,1},{1,0},{2,3},{3,2},{4,5},{5,4},{6,7},{7,6},{8,9},{9,8},{10,11... | collective-permute-start | bytes 589832 | tf_op jit(solution)/shard_map/ppermute | solution.py:234
  203.3 21.1 %collective-permute-start.67 = (bf16[48,2048]{1,0:T(8,128)(2,1)S(1)}, bf16[48,2048]{1,0:T(8,128)(2,1)S(1)}, u32[]{:S(2)}, u32[]{:S(2)}) collective-permute-start(bf16[48,2048]{1,0:T(8,128)(2,1)S(1)} %get-tuple-element.114), channel_id=1, source_target_pairs={{0,1},{1,0},{2,3},{3,2},{4,5},{5,4},{6,7},{7,6},{8,9},{9,8},{10,11... | collective-permute-start | bytes 589832 | tf_op jit(solution)/shard_map/ppermute | solution.py:234
  211.7 21.1 %collective-permute-start.63 = (bf16[48,2048]{1,0:T(8,128)(2,1)S(1)}, bf16[48,2048]{1,0:T(8,128)(2,1)S(1)}, u32[]{:S(2)}, u32[]{:S(2)}) collective-permute-start(bf16[48,2048]{1,0:T(8,128)(2,1)S(1)} %get-tuple-element.110), channel_id=1, source_target_pairs={{0,1},{1,0},{2,3},{3,2},{4,5},{5,4},{6,7},{7,6},{8,9},{9,8},{10,11... | collective-permute-start | bytes 589832 | tf_op jit(solution)/shard_map/ppermute | solution.py:234
  216.0 21.1 %collective-permute-start.62 = (bf16[48,2048]{1,0:T(8,128)(2,1)S(1)}, bf16[48,2048]{1,0:T(8,128)(2,1)S(1)}, u32[]{:S(2)}, u32[]{:S(2)}) collective-permute-start(bf16[48,2048]{1,0:T(8,128)(2,1)S(1)} %get-tuple-element.108), channel_id=1, source_target_pairs={{0,1},{1,0},{2,3},{3,2},{4,5},{5,4},{6,7},{7,6},{8,9},{9,8},{10,11... | collective-permute-start | bytes 589832 | tf_op jit(solution)/shard_map/ppermute | solution.py:234
  220.2 21.1 %collective-permute-start.29 = (bf16[48,2048]{1,0:T(8,128)(2,1)S(1)}, bf16[48,2048]{1,0:T(8,128)(2,1)S(1)}, u32[]{:S(2)}, u32[]{:S(2)}) collective-permute-start(bf16[48,2048]{1,0:T(8,128)(2,1)S(1)} %get-tuple-element.90), channel_id=1, source_target_pairs={{0,1},{1,0},{2,3},{3,2},{4,5},{5,4},{6,7},{7,6},{8,9},{9,8},{10,11... | collective-permute-start | bytes 589832 | tf_op jit(solution)/shard_map/ppermute | solution.py:234
  224.4 21.1 %collective-permute-start.27 = (bf16[48,2048]{1,0:T(8,128)(2,1)S(1)}, bf16[48,2048]{1,0:T(8,128)(2,1)S(1)}, u32[]{:S(2)}, u32[]{:S(2)}) collective-permute-start(bf16[48,2048]{1,0:T(8,128)(2,1)S(1)} %get-tuple-element.88), channel_id=1, source_target_pairs={{0,1},{1,0},{2,3},{3,2},{4,5},{5,4},{6,7},{7,6},{8,9},{9,8},{10,11... | collective-permute-start | bytes 589832 | tf_op jit(solution)/shard_map/ppermute | solution.py:234
  232.8 21.1 %collective-permute-start.23 = (bf16[48,2048]{1,0:T(8,128)(2,1)S(1)}, bf16[48,2048]{1,0:T(8,128)(2,1)S(1)}, u32[]{:S(2)}, u32[]{:S(2)}) collective-permute-start(bf16[48,2048]{1,0:T(8,128)(2,1)S(1)} %get-tuple-element.84), channel_id=1, source_target_pairs={{0,1},{1,0},{2,3},{3,2},{4,5},{5,4},{6,7},{7,6},{8,9},{9,8},{10,11... | collective-permute-start | bytes 589832 | tf_op jit(solution)/shard_map/ppermute | solution.py:234
  237.0 21.1 %collective-permute-start.21 = (bf16[48,2048]{1,0:T(8,128)(2,1)S(1)}, bf16[48,2048]{1,0:T(8,128)(2,1)S(1)}, u32[]{:S(2)}, u32[]{:S(2)}) collective-permute-start(bf16[48,2048]{1,0:T(8,128)(2,1)S(1)} %get-tuple-element.82), channel_id=1, source_target_pairs={{0,1},{1,0},{2,3},{3,2},{4,5},{5,4},{6,7},{7,6},{8,9},{9,8},{10,11... | collective-permute-start | bytes 589832 | tf_op jit(solution)/shard_map/ppermute | solution.py:234
  241.2 21.1 %collective-permute-start.19 = (bf16[48,2048]{1,0:T(8,128)(2,1)S(1)}, bf16[48,2048]{1,0:T(8,128)(2,1)S(1)}, u32[]{:S(2)}, u32[]{:S(2)}) collective-permute-start(bf16[48,2048]{1,0:T(8,128)(2,1)S(1)} %get-tuple-element.80), channel_id=1, source_target_pairs={{0,1},{1,0},{2,3},{3,2},{4,5},{5,4},{6,7},{7,6},{8,9},{9,8},{10,11... | collective-permute-start | bytes 589832 | tf_op jit(solution)/shard_map/ppermute | solution.py:234
  245.5 21.1 %collective-permute-start.17 = (bf16[48,2048]{1,0:T(8,128)(2,1)S(1)}, bf16[48,2048]{1,0:T(8,128)(2,1)S(1)}, u32[]{:S(2)}, u32[]{:S(2)}) collective-permute-start(bf16[48,2048]{1,0:T(8,128)(2,1)S(1)} %get-tuple-element.78), channel_id=1, source_target_pairs={{0,1},{1,0},{2,3},{3,2},{4,5},{5,4},{6,7},{7,6},{8,9},{9,8},{10,11... | collective-permute-start | bytes 589832 | tf_op jit(solution)/shard_map/ppermute | solution.py:234
  258.1 21.4 %collective-permute-start.74 = (bf16[48,2048]{1,0:T(8,128)(2,1)S(1)}, bf16[48,2048]{1,0:T(8,128)(2,1)S(1)}, u32[]{:S(2)}, u32[]{:S(2)}) collective-permute-start(bf16[48,2048]{1,0:T(8,128)(2,1)S(1)} %add_convert_fusion.1), channel_id=1, source_target_pairs={{0,12},{1,13},{2,14},{3,15},{4,8},{5,9},{6,10},{7,11},{8,4},{9,5},... | collective-permute-start | bytes 589832 | tf_op jit(solution)/shard_map/ppermute | solution.py:234
  262.3 24.6 %collective-permute-start.72 = (bf16[48,2048]{1,0:T(8,128)(2,1)S(1)}, bf16[48,2048]{1,0:T(8,128)(2,1)S(1)}, u32[]{:S(2)}, u32[]{:S(2)}) collective-permute-start(bf16[48,2048]{1,0:T(8,128)(2,1)S(1)} %add_convert_fusion.2), channel_id=1, source_target_pairs={{0,10},{1,11},{2,8},{3,9},{4,14},{5,15},{6,12},{7,13},{8,2},{9,3},... | collective-permute-start | bytes 589832 | tf_op jit(solution)/shard_map/ppermute | solution.py:234
  266.5 33.7 %collective-permute-start.70 = (bf16[48,2048]{1,0:T(8,128)(2,1)S(1)}, bf16[48,2048]{1,0:T(8,128)(2,1)S(1)}, u32[]{:S(2)}, u32[]{:S(2)}) collective-permute-start(bf16[48,2048]{1,0:T(8,128)(2,1)S(1)} %add_convert_fusion.3), channel_id=1, source_target_pairs={{0,8},{1,9},{2,10},{3,11},{4,12},{5,13},{6,14},{7,15},{8,0},{9,1},... | collective-permute-start | bytes 589832 | tf_op jit(solution)/shard_map/ppermute | solution.py:234
  269.7 30.6 %collective-permute-start.68 = (bf16[48,2048]{1,0:T(8,128)(2,1)S(1)}, bf16[48,2048]{1,0:T(8,128)(2,1)S(1)}, u32[]{:S(2)}, u32[]{:S(2)}) collective-permute-start(bf16[48,2048]{1,0:T(8,128)(2,1)S(1)} %add_convert_fusion.4), channel_id=1, source_target_pairs={{0,6},{1,7},{2,4},{3,5},{4,2},{5,3},{6,0},{7,1},{8,14},{9,15},{10,... | collective-permute-start | bytes 589832 | tf_op jit(solution)/shard_map/ppermute | solution.py:234
  270.3 32.3 %collective-permute-start.66 = (bf16[48,2048]{1,0:T(8,128)(2,1)S(1)}, bf16[48,2048]{1,0:T(8,128)(2,1)S(1)}, u32[]{:S(2)}, u32[]{:S(2)}) collective-permute-start(bf16[48,2048]{1,0:T(8,128)(2,1)S(1)} %add_convert_fusion.5), channel_id=1, source_target_pairs={{0,4},{1,5},{2,6},{3,7},{4,0},{5,1},{6,2},{7,3},{8,12},{9,13},{10,... | collective-permute-start | bytes 589832 | tf_op jit(solution)/shard_map/ppermute | solution.py:234
  279.4 27.5 %collective-permute-start.64 = (bf16[48,2048]{1,0:T(8,128)(2,1)S(1)}, bf16[48,2048]{1,0:T(8,128)(2,1)S(1)}, u32[]{:S(2)}, u32[]{:S(2)}) collective-permute-start(bf16[48,2048]{1,0:T(8,128)(2,1)S(1)} %add_convert_fusion.6), channel_id=1, source_target_pairs={{0,2},{1,3},{2,0},{3,1},{4,6},{5,7},{6,4},{7,5},{8,10},{9,11},{10,... | collective-permute-start | bytes 589832 | tf_op jit(solution)/shard_map/ppermute | solution.py:234
  (55 other events, 1041.8 us)

commit v2 on v1

v2 whole, which is shorter than its diff:
```python
import functools

import jax
import jax.numpy as jnp
from jax import lax
from jax.experimental import pallas as pl
from jax.experimental.pallas import tpu as pltpu
from jax.sharding import PartitionSpec as P

VMEM_LIMIT = 48 << 20


def whole(n):
    return [pl.BlockSpec(memory_space=pltpu.VMEM)] * n


def params():
    return pltpu.CompilerParams(vmem_limit_bytes=VMEM_LIMIT)


def placement(me, routes, experts, capacity):
    tokens = routes.shape[1]
    rel = lax.bitwise_xor(routes, me)
    expert_row = lax.broadcasted_iota(jnp.int32, (experts, tokens), 0)
    first = rel[0:1, :] == expert_row
    second = rel[1:2, :] == expert_row
    hits = (first | second).astype(jnp.bfloat16)
    before = lax.broadcasted_iota(jnp.int32, (tokens, tokens), 0) < lax.broadcasted_iota(
        jnp.int32, (tokens, tokens), 1
    )
    earlier = jnp.dot(hits, before.astype(jnp.bfloat16), preferred_element_type=jnp.float32)
    slot0 = jnp.sum(jnp.where(first, earlier, 0.0), axis=0, keepdims=True).astype(jnp.int32)
    slot1 = jnp.sum(jnp.where(second, earlier, 0.0), axis=0, keepdims=True).astype(jnp.int32)
    place = lax.broadcasted_iota(jnp.int32, (experts * capacity, tokens), 0)
    at0 = place == rel[0:1, :] * capacity + slot0
    at1 = place == rel[1:2, :] * capacity + slot1
    return at0, at1


def as_bf16(mask):
    return mask.astype(jnp.float32).astype(jnp.bfloat16)


def dispatch_kernel(experts, capacity, me_ref, routes_ref, *refs):
    out_refs = refs[-experts:]
    at0, at1 = placement(me_ref[0], routes_ref[...], experts, capacity)
    table = as_bf16(at0 | at1)
    picked = jnp.dot(table, refs[0][...], preferred_element_type=jnp.float32).astype(jnp.bfloat16)
    for i, out in enumerate(out_refs):
        out[0:capacity, :] = picked[i * capacity : (i + 1) * capacity, :]
    if len(refs) == experts + 3:
        gates_ref, upstream_ref = refs[1:3]
        gate = jnp.where(at0, gates_ref[0:1, :], 0.0) + jnp.where(at1, gates_ref[1:2, :], 0.0)
        scaled = jnp.dot(table, upstream_ref[...], preferred_element_type=jnp.float32)
        scaled = (scaled * jnp.sum(gate, axis=1, keepdims=True)).astype(jnp.bfloat16)
        for i, out in enumerate(out_refs):
            out[capacity:, :] = scaled[i * capacity : (i + 1) * capacity, :]


def dispatch(me, routes, values, experts, capacity, gates=None, upstream=None):
    width = values.shape[1]
    many = 1 if gates is None else 2
    operands = (me, routes, values) + (() if gates is None else (gates, upstream))
    return pl.pallas_call(
        functools.partial(dispatch_kernel, experts, capacity),
        out_shape=[jax.ShapeDtypeStruct((many * capacity, width), jnp.bfloat16)] * experts,
        in_specs=[pl.BlockSpec(memory_space=pltpu.SMEM)] + whole(len(operands) - 1),
        out_specs=whole(experts),
        compiler_params=params(),
        cost_estimate=pl.CostEstimate(
            flops=2 * many * experts * capacity * values.size,
            bytes_accessed=2 * many * (values.size + experts * capacity * width),
            transcendentals=0,
        ),
        name="dispatch",
    )(*operands)


def combine_kernel(experts, capacity, scaled, me_ref, routes_ref, *refs):
    if scaled:
        gates_ref, *refs = refs
    *in_refs, out_ref, rows = refs
    for i, ref in enumerate(in_refs):
        rows[i * capacity : (i + 1) * capacity, :] = ref[...]
    at0, at1 = placement(me_ref[0], routes_ref[...], experts, capacity)
    outer = (((0,), (0,)), ((), ()))

    def pick(table):
        return lax.dot_general(
            table, rows[...], outer, preferred_element_type=jnp.float32
        )

    if scaled:
        gate = jnp.where(at0, gates_ref[0:1, :], 0.0) + jnp.where(at1, gates_ref[1:2, :], 0.0)
        high = gate.astype(jnp.bfloat16)
        low = (gate - high.astype(jnp.float32)).astype(jnp.bfloat16)
        out_ref[...] = (pick(high) + pick(low)).astype(jnp.bfloat16)
    else:
        out_ref[...] = pick(as_bf16(at0 | at1)).astype(jnp.bfloat16)


def combine(me, routes, pieces, experts, capacity, gates=None):
    width = pieces[0].shape[1]
    tokens = routes.shape[1]
    operands = (me, routes) + (() if gates is None else (gates,)) + tuple(pieces)
    return pl.pallas_call(
        functools.partial(combine_kernel, experts, capacity, gates is not None),
        out_shape=jax.ShapeDtypeStruct((tokens, width), jnp.bfloat16),
        in_specs=[pl.BlockSpec(memory_space=pltpu.SMEM)] + whole(len(operands) - 1),
        out_specs=pl.BlockSpec(memory_space=pltpu.VMEM),
        scratch_shapes=[pltpu.VMEM((experts * capacity, width), jnp.bfloat16)],
        compiler_params=params(),
        cost_estimate=pl.CostEstimate(
            flops=2 * tokens * experts * capacity * width,
            bytes_accessed=2 * (tokens * width + experts * capacity * width),
            transcendentals=0,
        ),
        name="combine",
    )(*operands)


def put(out_refs, values, order):
    step, at, places = values.shape[0] // len(order), 0, {}
    for out in out_refs:
        for row in range(0, out.shape[0], step):
            places[at] = (out, row)
            at += 1
    for n, i in enumerate(order):
        out, row = places[i]
        out[row : row + step, :] = values[n * step : (n + 1) * step, :]


def forward_kernel(pieces, outs, order, *refs):
    in_refs = refs[:pieces]
    gate_ref, up_ref, down_ref = refs[pieces : pieces + 3]
    out_refs = refs[pieces + 3 : pieces + 3 + outs]
    rows = refs[-1]
    at = 0
    for ref in in_refs:
        rows[at : at + ref.shape[0], :] = ref[...]
        at += ref.shape[0]
    gate_act = jnp.dot(rows[...], gate_ref[...], preferred_element_type=jnp.float32)
    up_act = jnp.dot(rows[...], up_ref[...], preferred_element_type=jnp.float32)
    hidden = (gate_act * jax.nn.sigmoid(gate_act) * up_act).astype(jnp.bfloat16)
    part = jnp.dot(hidden, down_ref[...], preferred_element_type=jnp.float32).astype(jnp.bfloat16)
    put(out_refs, part, order)


def forward_half(pieces, gate, up, down, outs, order=None):
    n = len(pieces)
    total = sum(piece.shape[0] for piece in pieces)
    width, hidden = gate.shape
    return pl.pallas_call(
        functools.partial(forward_kernel, n, len(outs), order or range(8)),
        out_shape=[jax.ShapeDtypeStruct((rows, width), jnp.bfloat16) for rows in outs],
        in_specs=whole(n + 3),
        out_specs=whole(len(outs)),
        scratch_shapes=[pltpu.VMEM((total, width), jnp.bfloat16)],
        compiler_params=params(),
        cost_estimate=pl.CostEstimate(
            flops=6 * total * width * hidden,
            bytes_accessed=4 * total * width + 6 * width * hidden,
            transcendentals=total * hidden,
        ),
        name="forward_half",
    )(*pieces, gate, up, down)


def backward_kernel(pieces, outs, *refs):
    in_refs = refs[:pieces]
    gate_ref, up_ref, down_ref = refs[pieces : pieces + 3]
    out_refs = refs[pieces + 3 : pieces + 3 + outs]
    hidden_ref, d_gate_ref, d_up_ref, rows, upstream = refs[pieces + 3 + outs :]
    half = in_refs[0].shape[0] // 2
    for i, ref in enumerate(in_refs):
        rows[i * half : (i + 1) * half, :] = ref[0:half, :]
        upstream[i * half : (i + 1) * half, :] = ref[half:, :]
    inner = (((1,), (1,)), ((), ()))
    gate_act = jnp.dot(rows[...], gate_ref[...], preferred_element_type=jnp.float32)
    up_act = jnp.dot(rows[...], up_ref[...], preferred_element_type=jnp.float32)
    d_hidden = lax.dot_general(
        upstream[...], down_ref[...], inner, preferred_element_type=jnp.float32
    )
    sigma = jax.nn.sigmoid(gate_act)
    swish = gate_act * sigma
    hidden_ref[...] = (swish * up_act).astype(jnp.bfloat16)
    d_gate = (d_hidden * up_act * sigma * (1.0 + gate_act * (1.0 - sigma))).astype(jnp.bfloat16)
    d_up = (d_hidden * swish).astype(jnp.bfloat16)
    d_gate_ref[...] = d_gate
    d_up_ref[...] = d_up
    back = lax.dot_general(d_gate, gate_ref[...], inner, preferred_element_type=jnp.float32)
    back = back + lax.dot_general(d_up, up_ref[...], inner, preferred_element_type=jnp.float32)
    back = back.astype(jnp.bfloat16)
    put(out_refs, back, range(8))


def backward_half(pieces, gate, up, down, outs):
    n = len(pieces)
    total = sum(piece.shape[0] for piece in pieces) // 2
    width, hidden = gate.shape
    small = jax.ShapeDtypeStruct((total, hidden), jnp.bfloat16)
    large = jax.ShapeDtypeStruct((total, width), jnp.bfloat16)
    out = pl.pallas_call(
        functools.partial(backward_kernel, n, len(outs)),
        out_shape=[jax.ShapeDtypeStruct((rows, width), jnp.bfloat16) for rows in outs]
        + [small] * 3
        + [large] * 2,
        in_specs=whole(n + 3),
        out_specs=whole(len(outs) + 5),
        compiler_params=params(),
        cost_estimate=pl.CostEstimate(
            flops=10 * total * width * hidden,
            bytes_accessed=10 * total * width + 6 * width * hidden,
            transcendentals=total * hidden,
        ),
        name="backward_half",
    )(*pieces, gate, up, down)
    return out[: len(outs)], out[len(outs) :]


def add_pair(a, b):
    return (a.astype(jnp.float32) + b.astype(jnp.float32)).astype(jnp.bfloat16)


def per_device(
    sent_forward,
    grad_sent,
    saved_inputs,
    routes_forward,
    gates_forward,
    routes_backward,
    gates_backward,
    w_gate,
    w_up,
    w_down,
):
    devices = lax.axis_size("expert")
    experts = devices // 2
    sections = lax.axis_size("section")
    tokens = sent_forward.shape[1]
    chosen = routes_forward.shape[2]
    capacity = 3 * tokens * chosen // (2 * experts)
    me = (lax.axis_index("expert") // 2).astype(jnp.int32).reshape(1)

    def along(array, by):
        return lax.ppermute(array, "section", [(i, (i + by) % sections) for i in range(sections)])

    def to_xor(array, mask):
        return lax.ppermute(array, "expert", [(i, i ^ mask) for i in range(devices)])

    routes_f, gates_f = routes_forward[0].T, gates_forward[0].T
    routes_b, gates_b = routes_backward[0].T, gates_backward[0].T
    weights = w_gate[0, 0], w_up[0, 0], w_down[0, 0]
    span = experts // 8
    group = [list(range(i * span, (i + 1) * span)) for i in range(8)]
    lump = span * capacity
    split = [lump, lump, 2 * lump, 2 * lump, 2 * lump]

    held, met, rounds = {}, [], []

    def after_met(array):
        return lax.optimization_barrier((array, *met))[0] if met else array

    def start(name, arrays, masks):
        held[name] = [
            to_xor(after_met(a), m) if m else a for a, m in zip(arrays, masks, strict=True)
        ]

    def meet(*names):
        met[:] = [a for name in names for a in held[name]]
        rounds.append(list(met))

    def z_start(kind, slots, i):
        start((kind, i), [slots[d] for d in group[i]], [2 * d for d in group[i]])

    def x_start(i):
        start(("x", i), held["b", i], [1] * span)

    def x_join(q, members):
        rows = [a for i in members for a in held["f", i]]
        start(("fx", q), [jnp.concatenate(rows) if len(rows) > 1 else rows[0]], [1])

    def part_start(kind, parts, q):
        start((kind, q), [parts[q + 1]], [1])

    def both_start(i):
        start(("bx", i), [jnp.concatenate([back_other[i], out_other[i]])], [1])

    def give_back(kind, own, i):
        q, first = i // 2, (i % 2) * span
        both = []
        for n in range(span):
            rows = slice((first + n) * capacity, (first + n + 1) * capacity)
            both.append(add_pair(own[q + 1][rows], held[kind + "x", q][0][rows]))
        start((kind, i), both, [2 * d for d in group[i]])

    def give_both(i):
        both = []
        for n in range(span):
            own_rows = slice(n * capacity, (n + 1) * capacity)
            met_rows = slice(lump + n * capacity, lump + (n + 1) * capacity)
            pair = [
                add_pair(back_own[i][own_rows], held["bx", i][0][own_rows]),
                add_pair(out_own[i][own_rows], held["bx", i][0][met_rows]),
            ]
            both.append(jnp.concatenate(pair))
        start(("both", i), both, [2 * d for d in group[i]])
        held["r", i] = [a[:capacity] for a in held["both", i]]
        held["o", i] = [a[capacity:] for a in held["both", i]]

    returned = along(grad_sent, -1)[0]
    arrived = along(sent_forward, 1)[0]
    slots_b = dispatch(me, routes_b, saved_inputs[0], experts, capacity, gates_b, returned)
    slots_b = lax.optimization_barrier((slots_b, arrived))[0]
    slots_f = dispatch(me, routes_f, arrived, experts, capacity)

    z_start("b", slots_b, 0)
    z_start("f", slots_f, 0)
    z_start("b", slots_b, 4)
    x_start(0)
    z_start("b", slots_b, 1)
    x_join(0, [0])
    meet(("b", 4), ("b", 1), ("x", 0), ("fx", 0))
    x_start(1)
    z_start("b", slots_b, 5)
    x_start(4)
    z_start("b", slots_b, 2)
    meet(("b", 5), ("b", 2), ("x", 1), ("x", 4))
    x_start(2)
    z_start("b", slots_b, 6)
    x_start(5)
    z_start("b", slots_b, 3)
    meet(("b", 6), ("b", 3), ("x", 2), ("x", 5))
    x_start(3)
    z_start("b", slots_b, 7)
    x_start(6)
    z_start("f", slots_f, 1)
    meet(("b", 7), ("f", 1), ("x", 3), ("x", 6))
    x_start(7)
    z_start("f", slots_f, 4)
    z_start("f", slots_f, 2)
    back_own, kept_own = backward_half(
        [a for i in range(8) for a in held["b", i]], *weights, split
    )
    meet(("x", 7), ("f", 4), ("f", 2))
    met.append(kept_own[1])
    x_join(1, [1, 2, 4])
    z_start("f", slots_f, 5)
    z_start("f", slots_f, 3)
    back_other, kept_other = backward_half(
        [a for i in range(8) for a in held["x", i]], *weights, split
    )
    meet(("f", 5), ("f", 3), ("fx", 1))
    met.append(kept_other[1])
    part_start("rx", back_other, 2)
    z_start("f", slots_f, 6)
    part_start("rx", back_other, 3)
    z_start("f", slots_f, 7)
    meet(("rx", 2), ("f", 6), ("f", 7), ("rx", 3))
    x_join(2, [3, 5, 6, 7])
    give_back("r", back_own, 4)
    give_back("r", back_own, 5)
    out_own = forward_half([a for i in range(8) for a in held["f", i]], *weights, split)
    meet(("r", 4), ("r", 5), ("fx", 2))
    part_start("rx", back_other, 1)
    give_back("r", back_own, 6)
    give_back("r", back_own, 7)
    other_rows = held["fx", 0] + held["fx", 1] + held["fx", 2]
    out_other = forward_half(other_rows, *weights, split, [0, 1, 2, 4, 3, 5, 6, 7])
    part_start("ox", out_other, 2)
    meet(("rx", 1), ("r", 6), ("r", 7), ("ox", 2))
    part_start("ox", out_other, 3)
    give_back("o", out_own, 4)
    part_start("ox", out_other, 1)
    give_back("o", out_own, 5)
    give_back("r", back_own, 2)
    give_back("r", back_own, 3)
    meet(("o", 4), ("o", 5), ("ox", 3), ("ox", 1), ("r", 2), ("r", 3))
    give_back("o", out_own, 6)
    give_back("o", out_own, 7)
    both_start(1)
    give_back("o", out_own, 2)
    meet(("bx", 1), ("o", 2))
    both_start(0)
    give_both(1)
    give_back("o", out_own, 3)
    give_both(0)

    outer = (((0,), (0,)), ((), ()))

    def weight_term(a, b, others):
        terms = []
        for kept in (kept_own, kept_other):
            left = lax.optimization_barrier((kept[a], *others))[0]
            terms.append(lax.dot_general(left, kept[b], outer, preferred_element_type=jnp.float32))
        return (terms[0] + terms[1]).astype(jnp.bfloat16)

    grad_gate = weight_term(3, 1, rounds[6])
    grad_up = weight_term(3, 2, rounds[7])
    grad_down = weight_term(0, 4, rounds[8])

    back = [a for i in range(8) for a in held["r", i]]
    out = [a for i in range(8) for a in held["o", i]]
    grad_in = combine(me, routes_b, back, experts, capacity)
    layer_out = combine(me, routes_f, out, experts, capacity, gates_f)
    return (
        layer_out[None],
        grad_in[None],
        grad_gate[None, None],
        grad_up[None, None],
        grad_down[None, None],
    )


def solution(mesh):
    rows = P("section", "expert", None)
    weights = P("section", "expert", None, None)
    return jax.shard_map(
        per_device,
        mesh=mesh,
        in_specs=(rows,) * 7 + (weights,) * 3,
        out_specs=(rows, rows, weights, weights, weights),
        check_vma=False,
    )
```

time: 324 us -> 231 us (0.71)
  starting transfers between devices: 127 us -> 71.9 us
  waiting for transfers between devices: 154 us -> 116 us
    ppermute x75 -> x46, starting transfers between devices: 126 us -> 71.4 us  [to_xor(): lax.ppermute(array, 'expert', [(i, i ^ mask) for i in range(devices)])]
    ppermute x75 -> x46, waiting for transfers between devices: 154 us -> 114 us  [to_xor(): lax.ppermute(array, 'expert', [(i, i ^ mask) for i in range(devices)])]
    dot_general x3 -> x6, matrix products: 10.6 us -> 10.3 us  [weight_term(): lax.dot_general(left, kept[b], outer, preferred_element_type=jnp.float32)]
    pallas_call x7 -> x6, Pallas kernels: 25 us -> 24.6 us  [the longest x2 13.7 us: backward_half(): pl.pallas_call(functools.partial(backward_kernel, n, len(outs)), out_shap...]
  transfers between devices with their start and end apart: 77 -> 48, of which waited for: 42 -> 26; matrix products, arithmetic and copies ran while one was open for 4% -> 5% of each run, Pallas kernels for 8% -> 11%
where the time goes in v2:
time: 231 us
  waiting for transfers between devices  116 us (50%)
  starting transfers between devices  71.9 us (31%)
  Pallas kernels  27.8 us (12%)
  matrix products  10.3 us (4%)
  local copies, waits for them, and re-layouts  3.45 us (1%)
    ppermute x46, waiting for transfers between devices, to_xor(): lax.ppermute(array, 'expert', [(i, i ^ mask) for i in range(devices)])  114 us
    ppermute x46, starting transfers between devices, to_xor(): lax.ppermute(array, 'expert', [(i, i ^ mask) for i in range(devices)])  71.4 us
    pallas_call x2, Pallas kernels, backward_half(): pl.pallas_call(functools.partial(backward_kernel, n, len(outs)), out_shap...  13.7 us
    dot_general x6, matrix products, weight_term(): lax.dot_general(left, kept[b], outer, preferred_element_type=jnp.float32)  10.3 us
    pallas_call x2, Pallas kernels, forward_half(): pl.pallas_call(functools.partial(forward_kernel, n, len(outs), order or r...  9.06 us
  transfers between devices with their start and end apart: 48, of which 26 were waited for; matrix products, arithmetic and copies ran while one was open for 5% of the time, Pallas kernels for 11%

profile of v2, /device:TPU:0, one launch (start us, length us, event | category | flops | bytes accessed | tf_op | source)
XLA Modules:
  0.0 230.9 jit_solution(13379215527612306876)
XLA Ops:
  6.5 3.0 %collective-permute-start.3 = (bf16[96,2048]{1,0:T(8,128)(2,1)S(1)}, bf16[96,2048]{1,0:T(8,128)(2,1)S(1)}, u32[]{:S(2)}, u32[]{:S(2)}) collective-permute-start(bf16[96,2048]{1,0:T(8,128)(2,1)S(1)} %get-tuple-element.120), channel_id=1, source_target_pairs={{0,2},{1,3},{2,0},{3,1},{4,6},{5,7},{6,4},{7,5},{8,10},{9,11},{10,... | collective-permute-start | bytes 1179656 | tf_op jit(solution)/shard_map/ppermute | solution.py:249
  9.4 2.6 %collective-permute-start.2 = (bf16[96,2048]{1,0:T(8,128)(2,1)S(1)}, bf16[96,2048]{1,0:T(8,128)(2,1)S(1)}, u32[]{:S(2)}, u32[]{:S(2)}) collective-permute-start(bf16[96,2048]{1,0:T(8,128)(2,1)S(1)} %get-tuple-element.119), channel_id=1, source_target_pairs={{0,8},{1,9},{2,10},{3,11},{4,12},{5,13},{6,14},{7,15},{8,0},{9,1},... | collective-permute-start | bytes 1179656 | tf_op jit(solution)/shard_map/ppermute | solution.py:249
  15.5 11.3 %collective-permute-done.5.refs_0_ = bf16[48,2048]{1,0:T(8,128)(2,1)S(1)} collective-permute-done((bf16[48,2048]{1,0:T(8,128)(2,1)S(1)}, bf16[48,2048]{1,0:T(8,128)(2,1)S(1)}, u32[]{:S(2)}, u32[]{:S(2)}) %collective-permute-start.5) | collective-permute-done | bytes 196640 | tf_op jit(solution)/shard_map/ppermute | solution.py:249
  26.8 2.8 %collective-permute-done.2.refs_4_ = bf16[96,2048]{1,0:T(8,128)(2,1)S(1)} collective-permute-done((bf16[96,2048]{1,0:T(8,128)(2,1)S(1)}, bf16[96,2048]{1,0:T(8,128)(2,1)S(1)}, u32[]{:S(2)}, u32[]{:S(2)}) %collective-permute-start.2) | collective-permute-done | bytes 393248 | tf_op jit(solution)/shard_map/ppermute | solution.py:249
  30.3 3.3 %collective-permute-start.6 = (bf16[96,2048]{1,0:T(8,128)(2,1)S(1)}, bf16[96,2048]{1,0:T(8,128)(2,1)S(1)}, u32[]{:S(2)}, u32[]{:S(2)}) collective-permute-start(bf16[96,2048]{1,0:T(8,128)(2,1)S(1)} %get-tuple-element.122), channel_id=1, source_target_pairs={{0,10},{1,11},{2,8},{3,9},{4,14},{5,15},{6,12},{7,13},{8,2},{9,3},... | collective-permute-start | bytes 1179656 | tf_op jit(solution)/shard_map/ppermute | solution.py:249
  35.6 12.2 %collective-permute-done.7.refs_2_ = bf16[96,2048]{1,0:T(8,128)(2,1)S(1)} collective-permute-done((bf16[96,2048]{1,0:T(8,128)(2,1)S(1)}, bf16[96,2048]{1,0:T(8,128)(2,1)S(1)}, u32[]{:S(2)}, u32[]{:S(2)}) %collective-permute-start.7) | collective-permute-done | bytes 393248 | tf_op jit(solution)/shard_map/ppermute | solution.py:249
  47.8 3.5 %collective-permute-done.6.refs_5_ = bf16[96,2048]{1,0:T(8,128)(2,1)S(1)} collective-permute-done((bf16[96,2048]{1,0:T(8,128)(2,1)S(1)}, bf16[96,2048]{1,0:T(8,128)(2,1)S(1)}, u32[]{:S(2)}, u32[]{:S(2)}) %collective-permute-start.6) | collective-permute-done | bytes 393248 | tf_op jit(solution)/shard_map/ppermute | solution.py:249
  56.5 8.5 %collective-permute-done.11.refs_3_ = bf16[96,2048]{1,0:T(8,128)(2,1)S(1)} collective-permute-done((bf16[96,2048]{1,0:T(8,128)(2,1)S(1)}, bf16[96,2048]{1,0:T(8,128)(2,1)S(1)}, u32[]{:S(2)}, u32[]{:S(2)}) %collective-permute-start.11) | collective-permute-done | bytes 393248 | tf_op jit(solution)/shard_map/ppermute | solution.py:249
  65.1 6.3 %collective-permute-done.10.refs_6_ = bf16[96,2048]{1,0:T(8,128)(2,1)S(1)} collective-permute-done((bf16[96,2048]{1,0:T(8,128)(2,1)S(1)}, bf16[96,2048]{1,0:T(8,128)(2,1)S(1)}, u32[]{:S(2)}, u32[]{:S(2)}) %collective-permute-start.10) | collective-permute-done | bytes 393248 | tf_op jit(solution)/shard_map/ppermute | solution.py:249
  72.8 2.4 %collective-permute-start.15 = (bf16[96,2048]{1,0:T(8,128)(2,1)S(1)}, bf16[96,2048]{1,0:T(8,128)(2,1)S(1)}, u32[]{:S(2)}, u32[]{:S(2)}) collective-permute-start(bf16[96,2048]{1,0:T(8,128)(2,1)S(1)} %get-tuple-element.135), channel_id=1, source_target_pairs={{0,14},{1,15},{2,12},{3,13},{4,10},{5,11},{6,8},{7,9},{8,6},{9,7},... | collective-permute-start | bytes 1179656 | tf_op jit(solution)/shard_map/ppermute | solution.py:249
  78.8 10.0 %collective-permute-done.14.refs_1_ = bf16[48,2048]{1,0:T(8,128)(2,1)S(1)} collective-permute-done((bf16[48,2048]{1,0:T(8,128)(2,1)S(1)}, bf16[48,2048]{1,0:T(8,128)(2,1)S(1)}, u32[]{:S(2)}, u32[]{:S(2)}) %collective-permute-start.14) | collective-permute-done | bytes 196640 | tf_op jit(solution)/shard_map/ppermute | solution.py:249
  88.8 3.0 %collective-permute-done.17.refs_6_ = bf16[96,2048]{1,0:T(8,128)(2,1)S(1)} collective-permute-done((bf16[96,2048]{1,0:T(8,128)(2,1)S(1)}, bf16[96,2048]{1,0:T(8,128)(2,1)S(1)}, u32[]{:S(2)}, u32[]{:S(2)}) %collective-permute-start.17) | collective-permute-done | bytes 393248 | tf_op jit(solution)/shard_map/ppermute | solution.py:249
  95.4 6.8 %backward_half.2 = (bf16[48,2048]{1,0:T(8,128)(2,1)S(1)}, bf16[48,2048]{1,0:T(8,128)(2,1)S(1)}, bf16[96,2048]{1,0:T(8,128)(2,1)S(1)}, bf16[96,2048]{1,0:T(8,128)...) custom-call(bf16[96,2048]{1,0:T(8,128)(2,1)S(1)} %get-tuple-element., ...), custom_call_target="tpu_custom_call" | custom-call | flops 3019898880 | bytes 12582912 | tf_op jit(solution)/shard_map/backward_half/pallas_call | solution.py:203
  103.3 3.6 %collective-permute-start.22 = (bf16[48,2048]{1,0:T(8,128)(2,1)S(1)}, bf16[48,2048]{1,0:T(8,128)(2,1)S(1)}, u32[]{:S(2)}, u32[]{:S(2)}) collective-permute-start(bf16[48,2048]{1,0:T(8,128)(2,1)S(1)} %get-tuple-element.146), channel_id=1, source_target_pairs={{0,10},{1,11},{2,8},{3,9},{4,14},{5,15},{6,12},{7,13},{8,2},{9,3},... | collective-permute-start | bytes 589832 | tf_op jit(solution)/shard_map/ppermute | solution.py:249
  106.9 6.9 %backward_half.3 = (bf16[48,2048]{1,0:T(8,128)(2,1)S(1)}, bf16[48,2048]{1,0:T(8,128)(2,1)S(1)}, bf16[96,2048]{1,0:T(8,128)(2,1)S(1)}, bf16[96,2048]{1,0:T(8,128)...) custom-call(bf16[96,2048]{1,0:T(8,128)(2,1)S(1)} %collective-permute, ...), custom_call_target="tpu_custom_call" | custom-call | flops 3019898880 | bytes 12582912 | tf_op jit(solution)/shard_map/backward_half/pallas_call | solution.py:203
  115.1 4.3 %collective-permute-start.25 = (bf16[48,2048]{1,0:T(8,128)(2,1)S(1)}, bf16[48,2048]{1,0:T(8,128)(2,1)S(1)}, u32[]{:S(2)}, u32[]{:S(2)}) collective-permute-start(bf16[48,2048]{1,0:T(8,128)(2,1)S(1)} %get-tuple-element.152), channel_id=1, source_target_pairs={{0,14},{1,15},{2,12},{3,13},{4,10},{5,11},{6,8},{7,9},{8,6},{9,7},... | collective-permute-start | bytes 589832 | tf_op jit(solution)/shard_map/ppermute | solution.py:249
  121.5 3.3 %collective-permute-done.25.refs_7_ = bf16[48,2048]{1,0:T(8,128)(2,1)S(1)} collective-permute-done((bf16[48,2048]{1,0:T(8,128)(2,1)S(1)}, bf16[48,2048]{1,0:T(8,128)(2,1)S(1)}, u32[]{:S(2)}, u32[]{:S(2)}) %collective-permute-start.25) | collective-permute-done | bytes 196640 | tf_op jit(solution)/shard_map/ppermute | solution.py:249
  124.8 2.7 %collective-permute-done.24.refs_6_ = bf16[48,2048]{1,0:T(8,128)(2,1)S(1)} collective-permute-done((bf16[48,2048]{1,0:T(8,128)(2,1)S(1)}, bf16[48,2048]{1,0:T(8,128)(2,1)S(1)}, u32[]{:S(2)}, u32[]{:S(2)}) %collective-permute-start.24) | collective-permute-done | bytes 196640 | tf_op jit(solution)/shard_map/ppermute | solution.py:249
  127.5 4.5 %forward_half.2 = (bf16[48,2048]{1,0:T(8,128)(2,1)S(1)}, bf16[48,2048]{1,0:T(8,128)(2,1)S(1)}, bf16[96,2048]{1,0:T(8,128)(2,1)S(1)}, bf16[96,2048]{1,0:T(8,128)(2,1)S(1)}, bf16[96,2048]{1,0:T(8,128)(2,1)S(1)}) custom-call(bf16[48,2048]{1,0:T(8,128)(2,1)S(1)} %get-tuple-element.107.refs_0_, bf16[48,2048]{1,0:T(8,128)(2,1)S(1)} %collective-permute-done.14.refs_1_, ...), custom_call_target="tpu_custom_call" | custom-call | flops 1811939328 | bytes 7864320 | tf_op jit(solution)/shard_map/forward_half/pallas_call | solution.py:153
  132.1 5.1 %collective-permute-done.27 = bf16[96,2048]{1,0:T(8,128)(2,1)S(1)} collective-permute-done((bf16[96,2048]{1,0:T(8,128)(2,1)S(1)}, bf16[96,2048]{1,0:T(8,128)(2,1)S(1)}, u32[]{:S(2)}, u32[]{:S(2)}) %collective-permute-start.27) | collective-permute-done | bytes 393248 | tf_op jit(solution)/shard_map/ppermute | solution.py:249
  143.3 2.3 %fusion = bf16[1,1,2048,384]{3,2,1,0:T(8,128)(2,1)} fusion(f32[2048,384]{1,0:T(8,128)S(1)} %fusion.4, bf16[384,2048]{1,0:T(8,128)(2,1)S(1)} %copy-done.9, bf16[384,384]{1,0:T(8,128)(2,1)S(1)} %get-tuple-element.143), kind=kOutput, calls=%fused_computation.3 | convolution fusion | flops 605552640 | bytes 6586368 | tf_op jit(solution)/shard_map/dot_general | solution.py:395
  145.7 7.9 %collective-permute-done.28.refs_2_ = bf16[192,2048]{1,0:T(8,128)(2,1)S(1)} collective-permute-done((bf16[192,2048]{1,0:T(8,128)(2,1)S(1)}, bf16[192,2048]{1,0:T(8,128)(2,1)S(1)}, u32[]{:S(2)}, u32[]{:S(2)}) %collective-permute-start.28) | collective-permute-done | bytes 786464 | tf_op jit(solution)/shard_map/ppermute | solution.py:249
  153.5 4.5 %forward_half.3 = (bf16[48,2048]{1,0:T(8,128)(2,1)S(1)}, bf16[48,2048]{1,0:T(8,128)(2,1)S(1)}, bf16[96,2048]{1,0:T(8,128)(2,1)S(1)}, bf16[96,2048]{1,0:T(8,128)(2,1)S(1)}, bf16[96,2048]{1,0:T(8,128)(2,1)S(1)}) custom-call(bf16[48,2048]{1,0:T(8,128)(2,1)S(1)} %collective-permute-done.5.refs_0_, bf16[144,2048]{1,0:T(8,128)(2,1)S(1)} %collective-permute-done.23.refs_1_, ...), custom_call_target="tpu_custom_call" | custom-call | flops 1811939328 | bytes 7864320 | tf_op jit(solution)/shard_map/forward_half/pallas_call | solution.py:153
  160.2 3.5 %collective-permute-start.33 = (bf16[48,2048]{1,0:T(8,128)(2,1)S(1)}, bf16[48,2048]{1,0:T(8,128)(2,1)S(1)}, u32[]{:S(2)}, u32[]{:S(2)}) collective-permute-start(bf16[48,2048]{1,0:T(8,128)(2,1)S(1)} %get-tuple-element.172), channel_id=1, source_target_pairs={{0,12},{1,13},{2,14},{3,15},{4,8},{5,9},{6,10},{7,11},{8,4},{9,5},... | collective-permute-start | bytes 589832 | tf_op jit(solution)/shard_map/ppermute | solution.py:249
  165.5 2.4 %fusion.1 = bf16[1,1,2048,384]{3,2,1,0:T(8,128)(2,1)} fusion(f32[2048,384]{1,0:T(8,128)S(1)} %fusion.5, bf16[384,2048]{1,0:T(8,128)(2,1)S(1)} %copy-done.10, bf16[384,384]{1,0:T(8,128)(2,1)S(1)} %get-tuple-element.200), kind=kOutput, calls=%fused_computation.4 | convolution fusion | flops 605552640 | bytes 6586368 | tf_op jit(solution)/shard_map/dot_general | solution.py:395
  169.5 2.7 %collective-permute-done.34.refs_7_ = bf16[48,2048]{1,0:T(8,128)(2,1)S(1)} collective-permute-done((bf16[48,2048]{1,0:T(8,128)(2,1)S(1)}, bf16[48,2048]{1,0:T(8,128)(2,1)S(1)}, u32[]{:S(2)}, u32[]{:S(2)}) %collective-permute-start.34) | collective-permute-done | bytes 196640 | tf_op jit(solution)/shard_map/ppermute | solution.py:249
  173.6 5.3 %collective-permute-start.35 = (bf16[48,2048]{1,0:T(8,128)(2,1)S(1)}, bf16[48,2048]{1,0:T(8,128)(2,1)S(1)}, u32[]{:S(2)}, u32[]{:S(2)}) collective-permute-start(bf16[48,2048]{1,0:T(8,128)(2,1)S(1)} %get-tuple-element.174), channel_id=1, source_target_pairs={{0,8},{1,9},{2,10},{3,11},{4,12},{5,13},{6,14},{7,15},{8,0},{9,1},... | collective-permute-start | bytes 589832 | tf_op jit(solution)/shard_map/ppermute | solution.py:249
  184.4 7.9 %collective-permute-done.35.refs_5_ = bf16[48,2048]{1,0:T(8,128)(2,1)S(1)} collective-permute-done((bf16[48,2048]{1,0:T(8,128)(2,1)S(1)}, bf16[48,2048]{1,0:T(8,128)(2,1)S(1)}, u32[]{:S(2)}, u32[]{:S(2)}) %collective-permute-start.35) | collective-permute-done | bytes 196640 | tf_op jit(solution)/shard_map/ppermute | solution.py:249
  195.7 4.4 %collective-permute-done.40.refs_3_ = bf16[48,2048]{1,0:T(8,128)(2,1)S(1)} collective-permute-done((bf16[48,2048]{1,0:T(8,128)(2,1)S(1)}, bf16[48,2048]{1,0:T(8,128)(2,1)S(1)}, u32[]{:S(2)}, u32[]{:S(2)}) %collective-permute-start.40) | collective-permute-done | bytes 196640 | tf_op jit(solution)/shard_map/ppermute | solution.py:249
  202.7 3.4 %collective-permute-start.47 = (bf16[48,2048]{1,0:T(8,128)(2,1)S(1)}, bf16[48,2048]{1,0:T(8,128)(2,1)S(1)}, u32[]{:S(2)}, u32[]{:S(2)}) collective-permute-start(bf16[48,2048]{1,0:T(8,128)(2,1)S(1)} %get-tuple-element.193), channel_id=1, source_target_pairs={{0,14},{1,15},{2,12},{3,13},{4,10},{5,11},{6,8},{7,9},{8,6},{9,7},... | collective-permute-start | bytes 589832 | tf_op jit(solution)/shard_map/ppermute | solution.py:249
  210.6 5.6 %collective-permute-start.44 = (bf16[96,2048]{1,0:T(8,128)(2,1)S(1)}, bf16[96,2048]{1,0:T(8,128)(2,1)S(1)}, u32[]{:S(2)}, u32[]{:S(2)}) collective-permute-start(bf16[96,2048]{1,0:T(8,128)(2,1)S(1)} %pad_maximum_fusion.4), channel_id=1, source_target_pairs={{0,2},{1,3},{2,0},{3,1},{4,6},{5,7},{6,4},{7,5},{8,10},{9,11},{10,... | collective-permute-start | bytes 1179656 | tf_op jit(solution)/shard_map/ppermute | solution.py:249
  217.7 10.0 %collective-permute-done.44 = bf16[96,2048]{1,0:T(8,128)(2,1)S(1)} collective-permute-done((bf16[96,2048]{1,0:T(8,128)(2,1)S(1)}, bf16[96,2048]{1,0:T(8,128)(2,1)S(1)}, u32[]{:S(2)}, u32[]{:S(2)}) %collective-permute-start.44) | collective-permute-done | bytes 393248 | tf_op jit(solution)/shard_map/ppermute | solution.py:249
  (118 shorter events, 64.0 us)
Async XLA Ops:
  6.5 20.4 %collective-permute-start.3 = (bf16[96,2048]{1,0:T(8,128)(2,1)S(1)}, bf16[96,2048]{1,0:T(8,128)(2,1)S(1)}, u32[]{:S(2)}, u32[]{:S(2)}) collective-permute-start(bf16[96,2048]{1,0:T(8,128)(2,1)S(1)} %get-tuple-element.120), channel_id=1, source_target_pairs={{0,2},{1,3},{2,0},{3,1},{4,6},{5,7},{6,4},{7,5},{8,10},{9,11},{10,... | collective-permute-start | bytes 1179656 | tf_op jit(solution)/shard_map/ppermute | solution.py:249
  9.4 20.2 %collective-permute-start.2 = (bf16[96,2048]{1,0:T(8,128)(2,1)S(1)}, bf16[96,2048]{1,0:T(8,128)(2,1)S(1)}, u32[]{:S(2)}, u32[]{:S(2)}) collective-permute-start(bf16[96,2048]{1,0:T(8,128)(2,1)S(1)} %get-tuple-element.119), channel_id=1, source_target_pairs={{0,8},{1,9},{2,10},{3,11},{4,12},{5,13},{6,14},{7,15},{8,0},{9,1},... | collective-permute-start | bytes 1179656 | tf_op jit(solution)/shard_map/ppermute | solution.py:249
  12.0 17.6 %collective-permute-start.4 = (bf16[96,2048]{1,0:T(8,128)(2,1)S(1)}, bf16[96,2048]{1,0:T(8,128)(2,1)S(1)}, u32[]{:S(2)}, u32[]{:S(2)}) collective-permute-start(bf16[96,2048]{1,0:T(8,128)(2,1)S(1)} %get-tuple-element.121.refs_0_), channel_id=1, source_target_pairs={{0,1},{1,0},{2,3},{3,2},{4,5},{5,4},{6,7},{7,6},{8,9},{9,8},{10,11... | collective-permute-start | bytes 1179656 | tf_op jit(solution)/shard_map/ppermute | solution.py:249
  14.9 11.9 %collective-permute-start.5 = (bf16[48,2048]{1,0:T(8,128)(2,1)S(1)}, bf16[48,2048]{1,0:T(8,128)(2,1)S(1)}, u32[]{:S(2)}, u32[]{:S(2)}) collective-permute-start(bf16[48,2048]{1,0:T(8,128)(2,1)S(1)} %get-tuple-element.107.refs_0_), channel_id=1, source_target_pairs={{0,1},{1,0},{2,3},{3,2},{4,5},{5,4},{6,7},{7,6},{8,9},{9,8},{10,11... | collective-permute-start | bytes 589832 | tf_op jit(solution)/shard_map/ppermute | solution.py:249
  29.6 18.2 %collective-permute-start.7 = (bf16[96,2048]{1,0:T(8,128)(2,1)S(1)}, bf16[96,2048]{1,0:T(8,128)(2,1)S(1)}, u32[]{:S(2)}, u32[]{:S(2)}) collective-permute-start(bf16[96,2048]{1,0:T(8,128)(2,1)S(1)} %get-tuple-element.124), channel_id=1, source_target_pairs={{0,4},{1,5},{2,6},{3,7},{4,0},{5,1},{6,2},{7,3},{8,12},{9,13},{10,... | collective-permute-start | bytes 1179656 | tf_op jit(solution)/shard_map/ppermute | solution.py:249
  30.3 21.0 %collective-permute-start.6 = (bf16[96,2048]{1,0:T(8,128)(2,1)S(1)}, bf16[96,2048]{1,0:T(8,128)(2,1)S(1)}, u32[]{:S(2)}, u32[]{:S(2)}) collective-permute-start(bf16[96,2048]{1,0:T(8,128)(2,1)S(1)} %get-tuple-element.122), channel_id=1, source_target_pairs={{0,10},{1,11},{2,8},{3,9},{4,14},{5,15},{6,12},{7,13},{8,2},{9,3},... | collective-permute-start | bytes 1179656 | tf_op jit(solution)/shard_map/ppermute | solution.py:249
  33.6 17.7 %collective-permute-start.8 = (bf16[96,2048]{1,0:T(8,128)(2,1)S(1)}, bf16[96,2048]{1,0:T(8,128)(2,1)S(1)}, u32[]{:S(2)}, u32[]{:S(2)}) collective-permute-start(bf16[96,2048]{1,0:T(8,128)(2,1)S(1)} %collective-permute-done.3.refs_1_), channel_id=1, source_target_pairs={{0,1},{1,0},{2,3},{3,2},{4,5},{5,4},{6,7},{7,6},{8,9},{9,8},{10,11... | collective-permute-start | bytes 1179656 | tf_op jit(solution)/shard_map/ppermute | solution.py:249
  35.1 17.4 %collective-permute-start.9 = (bf16[96,2048]{1,0:T(8,128)(2,1)S(1)}, bf16[96,2048]{1,0:T(8,128)(2,1)S(1)}, u32[]{:S(2)}, u32[]{:S(2)}) collective-permute-start(bf16[96,2048]{1,0:T(8,128)(2,1)S(1)} %collective-permute-done.2.refs_4_), channel_id=1, source_target_pairs={{0,1},{1,0},{2,3},{3,2},{4,5},{5,4},{6,7},{7,6},{8,9},{9,8},{10,11... | collective-permute-start | bytes 1179656 | tf_op jit(solution)/shard_map/ppermute | solution.py:249
  52.5 12.5 %collective-permute-start.11 = (bf16[96,2048]{1,0:T(8,128)(2,1)S(1)}, bf16[96,2048]{1,0:T(8,128)(2,1)S(1)}, u32[]{:S(2)}, u32[]{:S(2)}) collective-permute-start(bf16[96,2048]{1,0:T(8,128)(2,1)S(1)} %get-tuple-element.129), channel_id=1, source_target_pairs={{0,6},{1,7},{2,4},{3,5},{4,2},{5,3},{6,0},{7,1},{8,14},{9,15},{10,... | collective-permute-start | bytes 1179656 | tf_op jit(solution)/shard_map/ppermute | solution.py:249
  53.8 17.7 %collective-permute-start.10 = (bf16[96,2048]{1,0:T(8,128)(2,1)S(1)}, bf16[96,2048]{1,0:T(8,128)(2,1)S(1)}, u32[]{:S(2)}, u32[]{:S(2)}) collective-permute-start(bf16[96,2048]{1,0:T(8,128)(2,1)S(1)} %get-tuple-element.127), channel_id=1, source_target_pairs={{0,12},{1,13},{2,14},{3,15},{4,8},{5,9},{6,10},{7,11},{8,4},{9,5},... | collective-permute-start | bytes 1179656 | tf_op jit(solution)/shard_map/ppermute | solution.py:249
  54.5 16.9 %collective-permute-start.12 = (bf16[96,2048]{1,0:T(8,128)(2,1)S(1)}, bf16[96,2048]{1,0:T(8,128)(2,1)S(1)}, u32[]{:S(2)}, u32[]{:S(2)}) collective-permute-start(bf16[96,2048]{1,0:T(8,128)(2,1)S(1)} %collective-permute-done.7.refs_2_), channel_id=1, source_target_pairs={{0,1},{1,0},{2,3},{3,2},{4,5},{5,4},{6,7},{7,6},{8,9},{9,8},{10,11... | collective-permute-start | bytes 1179656 | tf_op jit(solution)/shard_map/ppermute | solution.py:249
  56.0 16.8 %collective-permute-start.13 = (bf16[96,2048]{1,0:T(8,128)(2,1)S(1)}, bf16[96,2048]{1,0:T(8,128)(2,1)S(1)}, u32[]{:S(2)}, u32[]{:S(2)}) collective-permute-start(bf16[96,2048]{1,0:T(8,128)(2,1)S(1)} %collective-permute-done.6.refs_5_), channel_id=1, source_target_pairs={{0,1},{1,0},{2,3},{3,2},{4,5},{5,4},{6,7},{7,6},{8,9},{9,8},{10,11... | collective-permute-start | bytes 1179656 | tf_op jit(solution)/shard_map/ppermute | solution.py:249
  72.8 16.0 %collective-permute-start.15 = (bf16[96,2048]{1,0:T(8,128)(2,1)S(1)}, bf16[96,2048]{1,0:T(8,128)(2,1)S(1)}, u32[]{:S(2)}, u32[]{:S(2)}) collective-permute-start(bf16[96,2048]{1,0:T(8,128)(2,1)S(1)} %get-tuple-element.135), channel_id=1, source_target_pairs={{0,14},{1,15},{2,12},{3,13},{4,10},{5,11},{6,8},{7,9},{8,6},{9,7},... | collective-permute-start | bytes 1179656 | tf_op jit(solution)/shard_map/ppermute | solution.py:249
  75.3 13.6 %collective-permute-start.16 = (bf16[96,2048]{1,0:T(8,128)(2,1)S(1)}, bf16[96,2048]{1,0:T(8,128)(2,1)S(1)}, u32[]{:S(2)}, u32[]{:S(2)}) collective-permute-start(bf16[96,2048]{1,0:T(8,128)(2,1)S(1)} %collective-permute-done.11.refs_3_), channel_id=1, source_target_pairs={{0,1},{1,0},{2,3},{3,2},{4,5},{5,4},{6,7},{7,6},{8,9},{9,8},{10,11... | collective-permute-start | bytes 1179656 | tf_op jit(solution)/shard_map/ppermute | solution.py:249
  76.7 15.0 %collective-permute-start.17 = (bf16[96,2048]{1,0:T(8,128)(2,1)S(1)}, bf16[96,2048]{1,0:T(8,128)(2,1)S(1)}, u32[]{:S(2)}, u32[]{:S(2)}) collective-permute-start(bf16[96,2048]{1,0:T(8,128)(2,1)S(1)} %collective-permute-done.10.refs_6_), channel_id=1, source_target_pairs={{0,1},{1,0},{2,3},{3,2},{4,5},{5,4},{6,7},{7,6},{8,9},{9,8},{10,11... | collective-permute-start | bytes 1179656 | tf_op jit(solution)/shard_map/ppermute | solution.py:249
  77.3 11.5 %collective-permute-start.14 = (bf16[48,2048]{1,0:T(8,128)(2,1)S(1)}, bf16[48,2048]{1,0:T(8,128)(2,1)S(1)}, u32[]{:S(2)}, u32[]{:S(2)}) collective-permute-start(bf16[48,2048]{1,0:T(8,128)(2,1)S(1)} %get-tuple-element.132), channel_id=1, source_target_pairs={{0,2},{1,3},{2,0},{3,1},{4,6},{5,7},{6,4},{7,5},{8,10},{9,11},{10,... | collective-permute-start | bytes 589832 | tf_op jit(solution)/shard_map/ppermute | solution.py:249
  102.3 12.8 %collective-permute-start.23 = (bf16[144,2048]{1,0:T(8,128)(2,1)S(1)}, bf16[144,2048]{1,0:T(8,128)(2,1)S(1)}, u32[]{:S(2)}, u32[]{:S(2)}) collective-permute-start(bf16[144,2048]{1,0:T(8,128)(2,1)S(1)} %pad_maximum_fusion.1), channel_id=1, source_target_pairs={{0,1},{1,0},{2,3},{3,2},{4,5},{5,4},{6,7},{7,6},{8,9},{9,8},{10,11... | collective-permute-start | bytes 1769480 | tf_op jit(solution)/shard_map/ppermute | solution.py:249
  119.5 12.6 %collective-permute-start.26 = (bf16[96,2048]{1,0:T(8,128)(2,1)S(1)}, bf16[96,2048]{1,0:T(8,128)(2,1)S(1)}, u32[]{:S(2)}, u32[]{:S(2)}) collective-permute-start(bf16[96,2048]{1,0:T(8,128)(2,1)S(1)} %get-tuple-element.156), channel_id=1, source_target_pairs={{0,1},{1,0},{2,3},{3,2},{4,5},{5,4},{6,7},{7,6},{8,9},{9,8},{10,11... | collective-permute-start | bytes 1179656 | tf_op jit(solution)/shard_map/ppermute | solution.py:249
  121.0 16.2 %collective-permute-start.27 = (bf16[96,2048]{1,0:T(8,128)(2,1)S(1)}, bf16[96,2048]{1,0:T(8,128)(2,1)S(1)}, u32[]{:S(2)}, u32[]{:S(2)}) collective-permute-start(bf16[96,2048]{1,0:T(8,128)(2,1)S(1)} %get-tuple-element.158), channel_id=1, source_target_pairs={{0,1},{1,0},{2,3},{3,2},{4,5},{5,4},{6,7},{7,6},{8,9},{9,8},{10,11... | collective-permute-start | bytes 1179656 | tf_op jit(solution)/shard_map/ppermute | solution.py:249
  137.2 16.3 %collective-permute-start.28 = (bf16[192,2048]{1,0:T(8,128)(2,1)S(1)}, bf16[192,2048]{1,0:T(8,128)(2,1)S(1)}, u32[]{:S(2)}, u32[]{:S(2)}) collective-permute-start(bf16[192,2048]{1,0:T(8,128)(2,1)S(1)} %pad_maximum_fusion), channel_id=1, source_target_pairs={{0,1},{1,0},{2,3},{3,2},{4,5},{5,4},{6,7},{7,6},{8,9},{9,8},{10,11... | collective-permute-start | bytes 2359304 | tf_op jit(solution)/shard_map/ppermute | solution.py:249
  138.8 19.3 %collective-permute-start.29 = (bf16[48,2048]{1,0:T(8,128)(2,1)S(1)}, bf16[48,2048]{1,0:T(8,128)(2,1)S(1)}, u32[]{:S(2)}, u32[]{:S(2)}) collective-permute-start(bf16[48,2048]{1,0:T(8,128)(2,1)S(1)} %get-tuple-element.166), channel_id=1, source_target_pairs={{0,8},{1,9},{2,10},{3,11},{4,12},{5,13},{6,14},{7,15},{8,0},{9,1},... | collective-permute-start | bytes 589832 | tf_op jit(solution)/shard_map/ppermute | solution.py:249
  141.1 17.0 %collective-permute-start.30 = (bf16[48,2048]{1,0:T(8,128)(2,1)S(1)}, bf16[48,2048]{1,0:T(8,128)(2,1)S(1)}, u32[]{:S(2)}, u32[]{:S(2)}) collective-permute-start(bf16[48,2048]{1,0:T(8,128)(2,1)S(1)} %get-tuple-element.167), channel_id=1, source_target_pairs={{0,10},{1,11},{2,8},{3,9},{4,14},{5,15},{6,12},{7,13},{8,2},{9,3},... | collective-permute-start | bytes 589832 | tf_op jit(solution)/shard_map/ppermute | solution.py:249
  159.5 14.1 %collective-permute-start.32 = (bf16[96,2048]{1,0:T(8,128)(2,1)S(1)}, bf16[96,2048]{1,0:T(8,128)(2,1)S(1)}, u32[]{:S(2)}, u32[]{:S(2)}) collective-permute-start(bf16[96,2048]{1,0:T(8,128)(2,1)S(1)} %get-tuple-element.170), channel_id=1, source_target_pairs={{0,1},{1,0},{2,3},{3,2},{4,5},{5,4},{6,7},{7,6},{8,9},{9,8},{10,11... | collective-permute-start | bytes 1179656 | tf_op jit(solution)/shard_map/ppermute | solution.py:249
  173.6 18.7 %collective-permute-start.35 = (bf16[48,2048]{1,0:T(8,128)(2,1)S(1)}, bf16[48,2048]{1,0:T(8,128)(2,1)S(1)}, u32[]{:S(2)}, u32[]{:S(2)}) collective-permute-start(bf16[48,2048]{1,0:T(8,128)(2,1)S(1)} %get-tuple-element.174), channel_id=1, source_target_pairs={{0,8},{1,9},{2,10},{3,11},{4,12},{5,13},{6,14},{7,15},{8,0},{9,1},... | collective-permute-start | bytes 589832 | tf_op jit(solution)/shard_map/ppermute | solution.py:249
  178.8 16.9 %collective-permute-start.36 = (bf16[48,2048]{1,0:T(8,128)(2,1)S(1)}, bf16[48,2048]{1,0:T(8,128)(2,1)S(1)}, u32[]{:S(2)}, u32[]{:S(2)}) collective-permute-start(bf16[48,2048]{1,0:T(8,128)(2,1)S(1)} %get-tuple-element.175), channel_id=1, source_target_pairs={{0,10},{1,11},{2,8},{3,9},{4,14},{5,15},{6,12},{7,13},{8,2},{9,3},... | collective-permute-start | bytes 589832 | tf_op jit(solution)/shard_map/ppermute | solution.py:249
  179.1 21.0 %collective-permute-start.37 = (bf16[96,2048]{1,0:T(8,128)(2,1)S(1)}, bf16[96,2048]{1,0:T(8,128)(2,1)S(1)}, u32[]{:S(2)}, u32[]{:S(2)}) collective-permute-start(bf16[96,2048]{1,0:T(8,128)(2,1)S(1)} %get-tuple-element.177), channel_id=1, source_target_pairs={{0,1},{1,0},{2,3},{3,2},{4,5},{5,4},{6,7},{7,6},{8,9},{9,8},{10,11... | collective-permute-start | bytes 1179656 | tf_op jit(solution)/shard_map/ppermute | solution.py:249
  179.9 20.2 %collective-permute-start.38 = (bf16[96,2048]{1,0:T(8,128)(2,1)S(1)}, bf16[96,2048]{1,0:T(8,128)(2,1)S(1)}, u32[]{:S(2)}, u32[]{:S(2)}) collective-permute-start(bf16[96,2048]{1,0:T(8,128)(2,1)S(1)} %get-tuple-element.179), channel_id=1, source_target_pairs={{0,1},{1,0},{2,3},{3,2},{4,5},{5,4},{6,7},{7,6},{8,9},{9,8},{10,11... | collective-permute-start | bytes 1179656 | tf_op jit(solution)/shard_map/ppermute | solution.py:249
  181.2 14.5 %collective-permute-start.39 = (bf16[48,2048]{1,0:T(8,128)(2,1)S(1)}, bf16[48,2048]{1,0:T(8,128)(2,1)S(1)}, u32[]{:S(2)}, u32[]{:S(2)}) collective-permute-start(bf16[48,2048]{1,0:T(8,128)(2,1)S(1)} %get-tuple-element.181), channel_id=1, source_target_pairs={{0,4},{1,5},{2,6},{3,7},{4,0},{5,1},{6,2},{7,3},{8,12},{9,13},{10,... | collective-permute-start | bytes 589832 | tf_op jit(solution)/shard_map/ppermute | solution.py:249
  201.0 28.2 %collective-permute-start.46 = (bf16[48,2048]{1,0:T(8,128)(2,1)S(1)}, bf16[48,2048]{1,0:T(8,128)(2,1)S(1)}, u32[]{:S(2)}, u32[]{:S(2)}) collective-permute-start(bf16[48,2048]{1,0:T(8,128)(2,1)S(1)} %get-tuple-element.192), channel_id=1, source_target_pairs={{0,12},{1,13},{2,14},{3,15},{4,8},{5,9},{6,10},{7,11},{8,4},{9,5},... | collective-permute-start | bytes 589832 | tf_op jit(solution)/shard_map/ppermute | solution.py:249
  202.7 26.5 %collective-permute-start.47 = (bf16[48,2048]{1,0:T(8,128)(2,1)S(1)}, bf16[48,2048]{1,0:T(8,128)(2,1)S(1)}, u32[]{:S(2)}, u32[]{:S(2)}) collective-permute-start(bf16[48,2048]{1,0:T(8,128)(2,1)S(1)} %get-tuple-element.193), channel_id=1, source_target_pairs={{0,14},{1,15},{2,12},{3,13},{4,10},{5,11},{6,8},{7,9},{8,6},{9,7},... | collective-permute-start | bytes 589832 | tf_op jit(solution)/shard_map/ppermute | solution.py:249
  210.6 17.1 %collective-permute-start.44 = (bf16[96,2048]{1,0:T(8,128)(2,1)S(1)}, bf16[96,2048]{1,0:T(8,128)(2,1)S(1)}, u32[]{:S(2)}, u32[]{:S(2)}) collective-permute-start(bf16[96,2048]{1,0:T(8,128)(2,1)S(1)} %pad_maximum_fusion.4), channel_id=1, source_target_pairs={{0,2},{1,3},{2,0},{3,1},{4,6},{5,7},{6,4},{7,5},{8,10},{9,11},{10,... | collective-permute-start | bytes 1179656 | tf_op jit(solution)/shard_map/ppermute | solution.py:249
  216.2 12.9 %collective-permute-start.45 = (bf16[48,2048]{1,0:T(8,128)(2,1)S(1)}, bf16[48,2048]{1,0:T(8,128)(2,1)S(1)}, u32[]{:S(2)}, u32[]{:S(2)}) collective-permute-start(bf16[48,2048]{1,0:T(8,128)(2,1)S(1)} %get-tuple-element.190), channel_id=1, source_target_pairs={{0,6},{1,7},{2,4},{3,5},{4,2},{5,3},{6,0},{7,1},{8,14},{9,15},{10,... | collective-permute-start | bytes 589832 | tf_op jit(solution)/shard_map/ppermute | solution.py:249
  (29 other events, 233.9 us)

commit v3 on v2

--- a/solution.py
+++ b/solution.py
@@ -320,19 +320,22 @@
     x_start(0)
     z_start("b", slots_b, 1)
     x_join(0, [0])
+    meet(("b", 4),)
+    z_start("b", slots_b, 5)
     meet(("b", 4), ("b", 1), ("x", 0), ("fx", 0))
     x_start(1)
-    z_start("b", slots_b, 5)
     x_start(4)
     z_start("b", slots_b, 2)
+    meet(("b", 5),)
+    z_start("b", slots_b, 6)
     meet(("b", 5), ("b", 2), ("x", 1), ("x", 4))
     x_start(2)
-    z_start("b", slots_b, 6)
     x_start(5)
     z_start("b", slots_b, 3)
+    meet(("b", 6),)
+    z_start("b", slots_b, 7)
     meet(("b", 6), ("b", 3), ("x", 2), ("x", 5))
     x_start(3)
-    z_start("b", slots_b, 7)
     x_start(6)
     z_start("f", slots_f, 1)
     meet(("b", 7), ("f", 1), ("x", 3), ("x", 6))
@@ -371,18 +374,20 @@
     meet(("rx", 1), ("r", 6), ("r", 7), ("ox", 2))
     part_start("ox", out_other, 3)
     give_back("o", out_own, 4)
+    both_start(1)
+    give_back("o", out_own, 5)
+    give_back("r", back_own, 3)
+    meet(("o", 4), ("o", 5))
+    give_back("o", out_own, 6)
+    meet(("o", 4), ("o", 5), ("ox", 3), ("bx", 1), ("r", 3))
     part_start("ox", out_other, 1)
-    give_back("o", out_own, 5)
+    give_both(1)
     give_back("r", back_own, 2)
-    give_back("r", back_own, 3)
-    meet(("o", 4), ("o", 5), ("ox", 3), ("ox", 1), ("r", 2), ("r", 3))
-    give_back("o", out_own, 6)
+    meet(("o", 6),)
     give_back("o", out_own, 7)
-    both_start(1)
+    meet(("o", 6), ("ox", 1), ("both", 1), ("r", 2))
+    both_start(0)
     give_back("o", out_own, 2)
-    meet(("bx", 1), ("o", 2))
-    both_start(0)
-    give_both(1)
     give_back("o", out_own, 3)
     give_both(0)
 
@@ -395,9 +400,9 @@
             terms.append(lax.dot_general(left, kept[b], outer, preferred_element_type=jnp.float32))
         return (terms[0] + terms[1]).astype(jnp.bfloat16)
 
-    grad_gate = weight_term(3, 1, rounds[6])
-    grad_up = weight_term(3, 2, rounds[7])
-    grad_down = weight_term(0, 4, rounds[8])
+    grad_gate = weight_term(3, 1, rounds[9])
+    grad_up = weight_term(3, 2, rounds[10])
+    grad_down = weight_term(0, 4, rounds[11])
 
     back = [a for i in range(8) for a in held["r", i]]
     out = [a for i in range(8) for a in held["o", i]]

time: 231 us -> 222 us (0.961)
  waiting for transfers between devices: 116 us -> 111 us
  starting transfers between devices: 71.9 us -> 67 us
    ppermute x46, starting transfers between devices: 71.4 us -> 66.4 us  [to_xor(): lax.ppermute(array, 'expert', [(i, i ^ mask) for i in range(devices)])]
    ppermute x46, waiting for transfers between devices: 114 us -> 110 us  [to_xor(): lax.ppermute(array, 'expert', [(i, i ^ mask) for i in range(devices)])]
  transfers between devices with their start and end apart: 48 -> 48, of which waited for: 26 -> 23; matrix products, arithmetic and copies ran while one was open for 5% -> 5% of each run, Pallas kernels for 11% -> 12%
where the time goes in v3:
time: 222 us
  waiting for transfers between devices  111 us (50%)
  starting transfers between devices  67 us (30%)
  Pallas kernels  27.7 us (12%)
  matrix products  10.3 us (5%)
  local copies, waits for them, and re-layouts  3.48 us (2%)
    ppermute x46, waiting for transfers between devices, to_xor(): lax.ppermute(array, 'expert', [(i, i ^ mask) for i in range(devices)])  110 us
    ppermute x46, starting transfers between devices, to_xor(): lax.ppermute(array, 'expert', [(i, i ^ mask) for i in range(devices)])  66.4 us
    pallas_call x2, Pallas kernels, backward_half(): pl.pallas_call(functools.partial(backward_kernel, n, len(outs)), out_shap...  13.7 us
    dot_general x6, matrix products, weight_term(): lax.dot_general(left, kept[b], outer, preferred_element_type=jnp.float32)  10.3 us
    pallas_call x2, Pallas kernels, forward_half(): pl.pallas_call(functools.partial(forward_kernel, n, len(outs), order or r...  9.05 us
  transfers between devices with their start and end apart: 48, of which 23 were waited for; matrix products, arithmetic and copies ran while one was open for 5% of the time, Pallas kernels for 12%

profile of v3, /device:TPU:0, one launch (start us, length us, event | category | flops | bytes accessed | tf_op | source)
XLA Modules:
  0.0 221.7 jit_solution(1884101037371824873)
XLA Ops:
  6.5 3.0 %collective-permute-start.5 = (bf16[96,2048]{1,0:T(8,128)(2,1)S(1)}, bf16[96,2048]{1,0:T(8,128)(2,1)S(1)}, u32[]{:S(2)}, u32[]{:S(2)}) collective-permute-start(bf16[96,2048]{1,0:T(8,128)(2,1)S(1)} %get-tuple-element.124), channel_id=1, source_target_pairs={{0,2},{1,3},{2,0},{3,1},{4,6},{5,7},{6,4},{7,5},{8,10},{9,11},{10,... | collective-permute-start | bytes 1179656 | tf_op jit(solution)/shard_map/ppermute | solution.py:249
  9.4 2.6 %collective-permute-start.2 = (bf16[96,2048]{1,0:T(8,128)(2,1)S(1)}, bf16[96,2048]{1,0:T(8,128)(2,1)S(1)}, u32[]{:S(2)}, u32[]{:S(2)}) collective-permute-start(bf16[96,2048]{1,0:T(8,128)(2,1)S(1)} %get-tuple-element.119), channel_id=1, source_target_pairs={{0,8},{1,9},{2,10},{3,11},{4,12},{5,13},{6,14},{7,15},{8,0},{9,1},... | collective-permute-start | bytes 1179656 | tf_op jit(solution)/shard_map/ppermute | solution.py:249
  15.5 11.3 %collective-permute-done.7.refs_0_ = bf16[48,2048]{1,0:T(8,128)(2,1)S(1)} collective-permute-done((bf16[48,2048]{1,0:T(8,128)(2,1)S(1)}, bf16[48,2048]{1,0:T(8,128)(2,1)S(1)}, u32[]{:S(2)}, u32[]{:S(2)}) %collective-permute-start.7) | collective-permute-done | bytes 196640 | tf_op jit(solution)/shard_map/ppermute | solution.py:249
  26.8 2.8 %collective-permute-done.2.refs_4_ = bf16[96,2048]{1,0:T(8,128)(2,1)S(1)} collective-permute-done((bf16[96,2048]{1,0:T(8,128)(2,1)S(1)}, bf16[96,2048]{1,0:T(8,128)(2,1)S(1)}, u32[]{:S(2)}, u32[]{:S(2)}) %collective-permute-start.2) | collective-permute-done | bytes 393248 | tf_op jit(solution)/shard_map/ppermute | solution.py:249
  30.3 3.3 %collective-permute-start.3 = (bf16[96,2048]{1,0:T(8,128)(2,1)S(1)}, bf16[96,2048]{1,0:T(8,128)(2,1)S(1)}, u32[]{:S(2)}, u32[]{:S(2)}) collective-permute-start(bf16[96,2048]{1,0:T(8,128)(2,1)S(1)} %get-tuple-element.120), channel_id=1, source_target_pairs={{0,10},{1,11},{2,8},{3,9},{4,14},{5,15},{6,12},{7,13},{8,2},{9,3},... | collective-permute-start | bytes 1179656 | tf_op jit(solution)/shard_map/ppermute | solution.py:249
  35.6 12.2 %collective-permute-done.8.refs_2_ = bf16[96,2048]{1,0:T(8,128)(2,1)S(1)} collective-permute-done((bf16[96,2048]{1,0:T(8,128)(2,1)S(1)}, bf16[96,2048]{1,0:T(8,128)(2,1)S(1)}, u32[]{:S(2)}, u32[]{:S(2)}) %collective-permute-start.8) | collective-permute-done | bytes 393248 | tf_op jit(solution)/shard_map/ppermute | solution.py:249
  47.8 3.5 %collective-permute-done.3.refs_5_ = bf16[96,2048]{1,0:T(8,128)(2,1)S(1)} collective-permute-done((bf16[96,2048]{1,0:T(8,128)(2,1)S(1)}, bf16[96,2048]{1,0:T(8,128)(2,1)S(1)}, u32[]{:S(2)}, u32[]{:S(2)}) %collective-permute-start.3) | collective-permute-done | bytes 393248 | tf_op jit(solution)/shard_map/ppermute | solution.py:249
  56.5 14.9 %collective-permute-done.4.refs_6_ = bf16[96,2048]{1,0:T(8,128)(2,1)S(1)} collective-permute-done((bf16[96,2048]{1,0:T(8,128)(2,1)S(1)}, bf16[96,2048]{1,0:T(8,128)(2,1)S(1)}, u32[]{:S(2)}, u32[]{:S(2)}) %collective-permute-start.4) | collective-permute-done | bytes 393248 | tf_op jit(solution)/shard_map/ppermute | solution.py:249
  71.4 2.5 %collective-permute-start.15 = (bf16[96,2048]{1,0:T(8,128)(2,1)S(1)}, bf16[96,2048]{1,0:T(8,128)(2,1)S(1)}, u32[]{:S(2)}, u32[]{:S(2)}) collective-permute-start(bf16[96,2048]{1,0:T(8,128)(2,1)S(1)} %get-tuple-element.135), channel_id=1, source_target_pairs={{0,14},{1,15},{2,12},{3,13},{4,10},{5,11},{6,8},{7,9},{8,6},{9,7},... | collective-permute-start | bytes 1179656 | tf_op jit(solution)/shard_map/ppermute | solution.py:249
  77.5 10.3 %collective-permute-done.14.refs_1_ = bf16[48,2048]{1,0:T(8,128)(2,1)S(1)} collective-permute-done((bf16[48,2048]{1,0:T(8,128)(2,1)S(1)}, bf16[48,2048]{1,0:T(8,128)(2,1)S(1)}, u32[]{:S(2)}, u32[]{:S(2)}) %collective-permute-start.14) | collective-permute-done | bytes 196640 | tf_op jit(solution)/shard_map/ppermute | solution.py:249
  87.9 3.2 %collective-permute-done.17.refs_6_ = bf16[96,2048]{1,0:T(8,128)(2,1)S(1)} collective-permute-done((bf16[96,2048]{1,0:T(8,128)(2,1)S(1)}, bf16[96,2048]{1,0:T(8,128)(2,1)S(1)}, u32[]{:S(2)}, u32[]{:S(2)}) %collective-permute-start.17) | collective-permute-done | bytes 393248 | tf_op jit(solution)/shard_map/ppermute | solution.py:249
  94.6 6.8 %backward_half.2 = (bf16[48,2048]{1,0:T(8,128)(2,1)S(1)}, bf16[48,2048]{1,0:T(8,128)(2,1)S(1)}, bf16[96,2048]{1,0:T(8,128)(2,1)S(1)}, bf16[96,2048]{1,0:T(8,128)...) custom-call(bf16[96,2048]{1,0:T(8,128)(2,1)S(1)} %get-tuple-element., ...), custom_call_target="tpu_custom_call" | custom-call | flops 3019898880 | bytes 12582912 | tf_op jit(solution)/shard_map/backward_half/pallas_call | solution.py:203
  106.1 6.8 %backward_half.3 = (bf16[48,2048]{1,0:T(8,128)(2,1)S(1)}, bf16[48,2048]{1,0:T(8,128)(2,1)S(1)}, bf16[96,2048]{1,0:T(8,128)(2,1)S(1)}, bf16[96,2048]{1,0:T(8,128)...) custom-call(bf16[96,2048]{1,0:T(8,128)(2,1)S(1)} %collective-permute, ...), custom_call_target="tpu_custom_call" | custom-call | flops 3019898880 | bytes 12582912 | tf_op jit(solution)/shard_map/backward_half/pallas_call | solution.py:203
  114.3 2.8 %collective-permute-start.25 = (bf16[48,2048]{1,0:T(8,128)(2,1)S(1)}, bf16[48,2048]{1,0:T(8,128)(2,1)S(1)}, u32[]{:S(2)}, u32[]{:S(2)}) collective-permute-start(bf16[48,2048]{1,0:T(8,128)(2,1)S(1)} %get-tuple-element.152), channel_id=1, source_target_pairs={{0,14},{1,15},{2,12},{3,13},{4,10},{5,11},{6,8},{7,9},{8,6},{9,7},... | collective-permute-start | bytes 589832 | tf_op jit(solution)/shard_map/ppermute | solution.py:249
  117.1 2.5 %collective-permute-start.24 = (bf16[48,2048]{1,0:T(8,128)(2,1)S(1)}, bf16[48,2048]{1,0:T(8,128)(2,1)S(1)}, u32[]{:S(2)}, u32[]{:S(2)}) collective-permute-start(bf16[48,2048]{1,0:T(8,128)(2,1)S(1)} %get-tuple-element.150), channel_id=1, source_target_pairs={{0,12},{1,13},{2,14},{3,15},{4,8},{5,9},{6,10},{7,11},{8,4},{9,5},... | collective-permute-start | bytes 589832 | tf_op jit(solution)/shard_map/ppermute | solution.py:249
  122.7 2.7 %collective-permute-done.24.refs_6_ = bf16[48,2048]{1,0:T(8,128)(2,1)S(1)} collective-permute-done((bf16[48,2048]{1,0:T(8,128)(2,1)S(1)}, bf16[48,2048]{1,0:T(8,128)(2,1)S(1)}, u32[]{:S(2)}, u32[]{:S(2)}) %collective-permute-start.24) | collective-permute-done | bytes 196640 | tf_op jit(solution)/shard_map/ppermute | solution.py:249
  125.5 4.5 %forward_half.2 = (bf16[48,2048]{1,0:T(8,128)(2,1)S(1)}, bf16[48,2048]{1,0:T(8,128)(2,1)S(1)}, bf16[96,2048]{1,0:T(8,128)(2,1)S(1)}, bf16[96,2048]{1,0:T(8,128)(2,1)S(1)}, bf16[96,2048]{1,0:T(8,128)(2,1)S(1)}) custom-call(bf16[48,2048]{1,0:T(8,128)(2,1)S(1)} %get-tuple-element.107.refs_0_, bf16[48,2048]{1,0:T(8,128)(2,1)S(1)} %collective-permute-done.14.refs_1_, ...), custom_call_target="tpu_custom_call" | custom-call | flops 1811939328 | bytes 7864320 | tf_op jit(solution)/shard_map/forward_half/pallas_call | solution.py:153
  130.1 7.2 %collective-permute-done.27 = bf16[96,2048]{1,0:T(8,128)(2,1)S(1)} collective-permute-done((bf16[96,2048]{1,0:T(8,128)(2,1)S(1)}, bf16[96,2048]{1,0:T(8,128)(2,1)S(1)}, u32[]{:S(2)}, u32[]{:S(2)}) %collective-permute-start.27) | collective-permute-done | bytes 393248 | tf_op jit(solution)/shard_map/ppermute | solution.py:249
  138.0 2.7 %collective-permute-start.30 = (bf16[48,2048]{1,0:T(8,128)(2,1)S(1)}, bf16[48,2048]{1,0:T(8,128)(2,1)S(1)}, u32[]{:S(2)}, u32[]{:S(2)}) collective-permute-start(bf16[48,2048]{1,0:T(8,128)(2,1)S(1)} %get-tuple-element.166), channel_id=1, source_target_pairs={{0,10},{1,11},{2,8},{3,9},{4,14},{5,15},{6,12},{7,13},{8,2},{9,3},... | collective-permute-start | bytes 589832 | tf_op jit(solution)/shard_map/ppermute | solution.py:249
  144.4 5.7 %collective-permute-done.29.refs_4_ = bf16[48,2048]{1,0:T(8,128)(2,1)S(1)} collective-permute-done((bf16[48,2048]{1,0:T(8,128)(2,1)S(1)}, bf16[48,2048]{1,0:T(8,128)(2,1)S(1)}, u32[]{:S(2)}, u32[]{:S(2)}) %collective-permute-start.29) | collective-permute-done | bytes 196640 | tf_op jit(solution)/shard_map/ppermute | solution.py:249
  153.9 2.4 %collective-permute-start.32 = (bf16[48,2048]{1,0:T(8,128)(2,1)S(1)}, bf16[48,2048]{1,0:T(8,128)(2,1)S(1)}, u32[]{:S(2)}, u32[]{:S(2)}) collective-permute-start(bf16[48,2048]{1,0:T(8,128)(2,1)S(1)} %get-tuple-element.169), channel_id=1, source_target_pairs={{0,12},{1,13},{2,14},{3,15},{4,8},{5,9},{6,10},{7,11},{8,4},{9,5},... | collective-permute-start | bytes 589832 | tf_op jit(solution)/shard_map/ppermute | solution.py:249
  156.3 2.7 %collective-permute-start.33 = (bf16[48,2048]{1,0:T(8,128)(2,1)S(1)}, bf16[48,2048]{1,0:T(8,128)(2,1)S(1)}, u32[]{:S(2)}, u32[]{:S(2)}) collective-permute-start(bf16[48,2048]{1,0:T(8,128)(2,1)S(1)} %get-tuple-element.170), channel_id=1, source_target_pairs={{0,14},{1,15},{2,12},{3,13},{4,10},{5,11},{6,8},{7,9},{8,6},{9,7},... | collective-permute-start | bytes 589832 | tf_op jit(solution)/shard_map/ppermute | solution.py:249
  159.0 4.5 %forward_half.3 = (bf16[48,2048]{1,0:T(8,128)(2,1)S(1)}, bf16[48,2048]{1,0:T(8,128)(2,1)S(1)}, bf16[96,2048]{1,0:T(8,128)(2,1)S(1)}, bf16[96,2048]{1,0:T(8,128)(2,1)S(1)}, bf16[96,2048]{1,0:T(8,128)(2,1)S(1)}) custom-call(bf16[48,2048]{1,0:T(8,128)(2,1)S(1)} %collective-permute-done.7.refs_0_, bf16[144,2048]{1,0:T(8,128)(2,1)S(1)} %collective-permute-done.23.refs_1_, ...), custom_call_target="tpu_custom_call" | custom-call | flops 1811939328 | bytes 7864320 | tf_op jit(solution)/shard_map/forward_half/pallas_call | solution.py:153
  167.8 5.1 %collective-permute-done.34 = bf16[96,2048]{1,0:T(8,128)(2,1)S(1)} collective-permute-done((bf16[96,2048]{1,0:T(8,128)(2,1)S(1)}, bf16[96,2048]{1,0:T(8,128)(2,1)S(1)}, u32[]{:S(2)}, u32[]{:S(2)}) %collective-permute-start.34) | collective-permute-done | bytes 393248 | tf_op jit(solution)/shard_map/ppermute | solution.py:249
  173.4 3.5 %collective-permute-start.37 = (bf16[48,2048]{1,0:T(8,128)(2,1)S(1)}, bf16[48,2048]{1,0:T(8,128)(2,1)S(1)}, u32[]{:S(2)}, u32[]{:S(2)}) collective-permute-start(bf16[48,2048]{1,0:T(8,128)(2,1)S(1)} %get-tuple-element.176), channel_id=1, source_target_pairs={{0,10},{1,11},{2,8},{3,9},{4,14},{5,15},{6,12},{7,13},{8,2},{9,3},... | collective-permute-start | bytes 589832 | tf_op jit(solution)/shard_map/ppermute | solution.py:249
  179.1 7.5 %collective-permute-done.36.refs_5_ = bf16[48,2048]{1,0:T(8,128)(2,1)S(1)} collective-permute-done((bf16[48,2048]{1,0:T(8,128)(2,1)S(1)}, bf16[48,2048]{1,0:T(8,128)(2,1)S(1)}, u32[]{:S(2)}, u32[]{:S(2)}) %collective-permute-start.36) | collective-permute-done | bytes 196640 | tf_op jit(solution)/shard_map/ppermute | solution.py:249
  186.6 4.1 %collective-permute-done.37.refs_6_ = bf16[48,2048]{1,0:T(8,128)(2,1)S(1)} collective-permute-done((bf16[48,2048]{1,0:T(8,128)(2,1)S(1)}, bf16[48,2048]{1,0:T(8,128)(2,1)S(1)}, u32[]{:S(2)}, u32[]{:S(2)}) %collective-permute-start.37) | collective-permute-done | bytes 196640 | tf_op jit(solution)/shard_map/ppermute | solution.py:249
  197.3 5.4 %collective-permute-done.38.refs_7_ = bf16[48,2048]{1,0:T(8,128)(2,1)S(1)} collective-permute-done((bf16[48,2048]{1,0:T(8,128)(2,1)S(1)}, bf16[48,2048]{1,0:T(8,128)(2,1)S(1)}, u32[]{:S(2)}, u32[]{:S(2)}) %collective-permute-start.38) | collective-permute-done | bytes 196640 | tf_op jit(solution)/shard_map/ppermute | solution.py:249
  202.7 2.4 %collective-permute-start.47 = (bf16[48,2048]{1,0:T(8,128)(2,1)S(1)}, bf16[48,2048]{1,0:T(8,128)(2,1)S(1)}, u32[]{:S(2)}, u32[]{:S(2)}) collective-permute-start(bf16[48,2048]{1,0:T(8,128)(2,1)S(1)} %get-tuple-element.193), channel_id=1, source_target_pairs={{0,14},{1,15},{2,12},{3,13},{4,10},{5,11},{6,8},{7,9},{8,6},{9,7},... | collective-permute-start | bytes 589832 | tf_op jit(solution)/shard_map/ppermute | solution.py:249
  207.1 3.5 %collective-permute-start.46 = (bf16[48,2048]{1,0:T(8,128)(2,1)S(1)}, bf16[48,2048]{1,0:T(8,128)(2,1)S(1)}, u32[]{:S(2)}, u32[]{:S(2)}) collective-permute-start(bf16[48,2048]{1,0:T(8,128)(2,1)S(1)} %get-tuple-element.192), channel_id=1, source_target_pairs={{0,6},{1,7},{2,4},{3,5},{4,2},{5,3},{6,0},{7,1},{8,14},{9,15},{10,... | collective-permute-start | bytes 589832 | tf_op jit(solution)/shard_map/ppermute | solution.py:249
  210.6 4.2 %collective-permute-done.44 = bf16[96,2048]{1,0:T(8,128)(2,1)S(1)} collective-permute-done((bf16[96,2048]{1,0:T(8,128)(2,1)S(1)}, bf16[96,2048]{1,0:T(8,128)(2,1)S(1)}, u32[]{:S(2)}, u32[]{:S(2)}) %collective-permute-start.44) | collective-permute-done | bytes 393248 | tf_op jit(solution)/shard_map/ppermute | solution.py:249
  216.3 3.7 %collective-permute-done.46.refs_4_ = bf16[48,2048]{1,0:T(8,128)(2,1)S(1)} collective-permute-done((bf16[48,2048]{1,0:T(8,128)(2,1)S(1)}, bf16[48,2048]{1,0:T(8,128)(2,1)S(1)}, u32[]{:S(2)}, u32[]{:S(2)}) %collective-permute-start.46) | collective-permute-done | bytes 196640 | tf_op jit(solution)/shard_map/ppermute | solution.py:249
  (118 shorter events, 60.4 us)
Async XLA Ops:
  6.5 20.4 %collective-permute-start.5 = (bf16[96,2048]{1,0:T(8,128)(2,1)S(1)}, bf16[96,2048]{1,0:T(8,128)(2,1)S(1)}, u32[]{:S(2)}, u32[]{:S(2)}) collective-permute-start(bf16[96,2048]{1,0:T(8,128)(2,1)S(1)} %get-tuple-element.124), channel_id=1, source_target_pairs={{0,2},{1,3},{2,0},{3,1},{4,6},{5,7},{6,4},{7,5},{8,10},{9,11},{10,... | collective-permute-start | bytes 1179656 | tf_op jit(solution)/shard_map/ppermute | solution.py:249
  9.4 20.2 %collective-permute-start.2 = (bf16[96,2048]{1,0:T(8,128)(2,1)S(1)}, bf16[96,2048]{1,0:T(8,128)(2,1)S(1)}, u32[]{:S(2)}, u32[]{:S(2)}) collective-permute-start(bf16[96,2048]{1,0:T(8,128)(2,1)S(1)} %get-tuple-element.119), channel_id=1, source_target_pairs={{0,8},{1,9},{2,10},{3,11},{4,12},{5,13},{6,14},{7,15},{8,0},{9,1},... | collective-permute-start | bytes 1179656 | tf_op jit(solution)/shard_map/ppermute | solution.py:249
  12.0 17.6 %collective-permute-start.6 = (bf16[96,2048]{1,0:T(8,128)(2,1)S(1)}, bf16[96,2048]{1,0:T(8,128)(2,1)S(1)}, u32[]{:S(2)}, u32[]{:S(2)}) collective-permute-start(bf16[96,2048]{1,0:T(8,128)(2,1)S(1)} %get-tuple-element.125.refs_0_), channel_id=1, source_target_pairs={{0,1},{1,0},{2,3},{3,2},{4,5},{5,4},{6,7},{7,6},{8,9},{9,8},{10,11... | collective-permute-start | bytes 1179656 | tf_op jit(solution)/shard_map/ppermute | solution.py:249
  14.9 11.9 %collective-permute-start.7 = (bf16[48,2048]{1,0:T(8,128)(2,1)S(1)}, bf16[48,2048]{1,0:T(8,128)(2,1)S(1)}, u32[]{:S(2)}, u32[]{:S(2)}) collective-permute-start(bf16[48,2048]{1,0:T(8,128)(2,1)S(1)} %get-tuple-element.107.refs_0_), channel_id=1, source_target_pairs={{0,1},{1,0},{2,3},{3,2},{4,5},{5,4},{6,7},{7,6},{8,9},{9,8},{10,11... | collective-permute-start | bytes 589832 | tf_op jit(solution)/shard_map/ppermute | solution.py:249
  29.6 18.2 %collective-permute-start.8 = (bf16[96,2048]{1,0:T(8,128)(2,1)S(1)}, bf16[96,2048]{1,0:T(8,128)(2,1)S(1)}, u32[]{:S(2)}, u32[]{:S(2)}) collective-permute-start(bf16[96,2048]{1,0:T(8,128)(2,1)S(1)} %get-tuple-element.126), channel_id=1, source_target_pairs={{0,4},{1,5},{2,6},{3,7},{4,0},{5,1},{6,2},{7,3},{8,12},{9,13},{10,... | collective-permute-start | bytes 1179656 | tf_op jit(solution)/shard_map/ppermute | solution.py:249
  30.3 21.0 %collective-permute-start.3 = (bf16[96,2048]{1,0:T(8,128)(2,1)S(1)}, bf16[96,2048]{1,0:T(8,128)(2,1)S(1)}, u32[]{:S(2)}, u32[]{:S(2)}) collective-permute-start(bf16[96,2048]{1,0:T(8,128)(2,1)S(1)} %get-tuple-element.120), channel_id=1, source_target_pairs={{0,10},{1,11},{2,8},{3,9},{4,14},{5,15},{6,12},{7,13},{8,2},{9,3},... | collective-permute-start | bytes 1179656 | tf_op jit(solution)/shard_map/ppermute | solution.py:249
  33.6 17.7 %collective-permute-start.9 = (bf16[96,2048]{1,0:T(8,128)(2,1)S(1)}, bf16[96,2048]{1,0:T(8,128)(2,1)S(1)}, u32[]{:S(2)}, u32[]{:S(2)}) collective-permute-start(bf16[96,2048]{1,0:T(8,128)(2,1)S(1)} %collective-permute-done.5.refs_1_), channel_id=1, source_target_pairs={{0,1},{1,0},{2,3},{3,2},{4,5},{5,4},{6,7},{7,6},{8,9},{9,8},{10,11... | collective-permute-start | bytes 1179656 | tf_op jit(solution)/shard_map/ppermute | solution.py:249
  35.1 17.4 %collective-permute-start.10 = (bf16[96,2048]{1,0:T(8,128)(2,1)S(1)}, bf16[96,2048]{1,0:T(8,128)(2,1)S(1)}, u32[]{:S(2)}, u32[]{:S(2)}) collective-permute-start(bf16[96,2048]{1,0:T(8,128)(2,1)S(1)} %collective-permute-done.2.refs_4_), channel_id=1, source_target_pairs={{0,1},{1,0},{2,3},{3,2},{4,5},{5,4},{6,7},{7,6},{8,9},{9,8},{10,11... | collective-permute-start | bytes 1179656 | tf_op jit(solution)/shard_map/ppermute | solution.py:249
  52.5 21.4 %collective-permute-start.11 = (bf16[96,2048]{1,0:T(8,128)(2,1)S(1)}, bf16[96,2048]{1,0:T(8,128)(2,1)S(1)}, u32[]{:S(2)}, u32[]{:S(2)}) collective-permute-start(bf16[96,2048]{1,0:T(8,128)(2,1)S(1)} %get-tuple-element.129), channel_id=1, source_target_pairs={{0,6},{1,7},{2,4},{3,5},{4,2},{5,3},{6,0},{7,1},{8,14},{9,15},{10,... | collective-permute-start | bytes 1179656 | tf_op jit(solution)/shard_map/ppermute | solution.py:249
  53.8 17.6 %collective-permute-start.4 = (bf16[96,2048]{1,0:T(8,128)(2,1)S(1)}, bf16[96,2048]{1,0:T(8,128)(2,1)S(1)}, u32[]{:S(2)}, u32[]{:S(2)}) collective-permute-start(bf16[96,2048]{1,0:T(8,128)(2,1)S(1)} %get-tuple-element.121), channel_id=1, source_target_pairs={{0,12},{1,13},{2,14},{3,15},{4,8},{5,9},{6,10},{7,11},{8,4},{9,5},... | collective-permute-start | bytes 1179656 | tf_op jit(solution)/shard_map/ppermute | solution.py:249
  54.5 19.4 %collective-permute-start.12 = (bf16[96,2048]{1,0:T(8,128)(2,1)S(1)}, bf16[96,2048]{1,0:T(8,128)(2,1)S(1)}, u32[]{:S(2)}, u32[]{:S(2)}) collective-permute-start(bf16[96,2048]{1,0:T(8,128)(2,1)S(1)} %collective-permute-done.8.refs_2_), channel_id=1, source_target_pairs={{0,1},{1,0},{2,3},{3,2},{4,5},{5,4},{6,7},{7,6},{8,9},{9,8},{10,11... | collective-permute-start | bytes 1179656 | tf_op jit(solution)/shard_map/ppermute | solution.py:249
  56.0 17.9 %collective-permute-start.13 = (bf16[96,2048]{1,0:T(8,128)(2,1)S(1)}, bf16[96,2048]{1,0:T(8,128)(2,1)S(1)}, u32[]{:S(2)}, u32[]{:S(2)}) collective-permute-start(bf16[96,2048]{1,0:T(8,128)(2,1)S(1)} %collective-permute-done.3.refs_5_), channel_id=1, source_target_pairs={{0,1},{1,0},{2,3},{3,2},{4,5},{5,4},{6,7},{7,6},{8,9},{9,8},{10,11... | collective-permute-start | bytes 1179656 | tf_op jit(solution)/shard_map/ppermute | solution.py:249
  71.4 16.4 %collective-permute-start.15 = (bf16[96,2048]{1,0:T(8,128)(2,1)S(1)}, bf16[96,2048]{1,0:T(8,128)(2,1)S(1)}, u32[]{:S(2)}, u32[]{:S(2)}) collective-permute-start(bf16[96,2048]{1,0:T(8,128)(2,1)S(1)} %get-tuple-element.135), channel_id=1, source_target_pairs={{0,14},{1,15},{2,12},{3,13},{4,10},{5,11},{6,8},{7,9},{8,6},{9,7},... | collective-permute-start | bytes 1179656 | tf_op jit(solution)/shard_map/ppermute | solution.py:249
  73.9 13.9 %collective-permute-start.16 = (bf16[96,2048]{1,0:T(8,128)(2,1)S(1)}, bf16[96,2048]{1,0:T(8,128)(2,1)S(1)}, u32[]{:S(2)}, u32[]{:S(2)}) collective-permute-start(bf16[96,2048]{1,0:T(8,128)(2,1)S(1)} %collective-permute-done.11.refs_3_), channel_id=1, source_target_pairs={{0,1},{1,0},{2,3},{3,2},{4,5},{5,4},{6,7},{7,6},{8,9},{9,8},{10,11... | collective-permute-start | bytes 1179656 | tf_op jit(solution)/shard_map/ppermute | solution.py:249
  75.5 15.5 %collective-permute-start.17 = (bf16[96,2048]{1,0:T(8,128)(2,1)S(1)}, bf16[96,2048]{1,0:T(8,128)(2,1)S(1)}, u32[]{:S(2)}, u32[]{:S(2)}) collective-permute-start(bf16[96,2048]{1,0:T(8,128)(2,1)S(1)} %collective-permute-done.4.refs_6_), channel_id=1, source_target_pairs={{0,1},{1,0},{2,3},{3,2},{4,5},{5,4},{6,7},{7,6},{8,9},{9,8},{10,11... | collective-permute-start | bytes 1179656 | tf_op jit(solution)/shard_map/ppermute | solution.py:249
  76.0 11.9 %collective-permute-start.14 = (bf16[48,2048]{1,0:T(8,128)(2,1)S(1)}, bf16[48,2048]{1,0:T(8,128)(2,1)S(1)}, u32[]{:S(2)}, u32[]{:S(2)}) collective-permute-start(bf16[48,2048]{1,0:T(8,128)(2,1)S(1)} %get-tuple-element.132), channel_id=1, source_target_pairs={{0,2},{1,3},{2,0},{3,1},{4,6},{5,7},{6,4},{7,5},{8,10},{9,11},{10,... | collective-permute-start | bytes 589832 | tf_op jit(solution)/shard_map/ppermute | solution.py:249
  101.5 12.8 %collective-permute-start.23 = (bf16[144,2048]{1,0:T(8,128)(2,1)S(1)}, bf16[144,2048]{1,0:T(8,128)(2,1)S(1)}, u32[]{:S(2)}, u32[]{:S(2)}) collective-permute-start(bf16[144,2048]{1,0:T(8,128)(2,1)S(1)} %pad_maximum_fusion.1), channel_id=1, source_target_pairs={{0,1},{1,0},{2,3},{3,2},{4,5},{5,4},{6,7},{7,6},{8,9},{9,8},{10,11... | collective-permute-start | bytes 1769480 | tf_op jit(solution)/shard_map/ppermute | solution.py:249
  120.1 17.2 %collective-permute-start.27 = (bf16[96,2048]{1,0:T(8,128)(2,1)S(1)}, bf16[96,2048]{1,0:T(8,128)(2,1)S(1)}, u32[]{:S(2)}, u32[]{:S(2)}) collective-permute-start(bf16[96,2048]{1,0:T(8,128)(2,1)S(1)} %get-tuple-element.158), channel_id=1, source_target_pairs={{0,1},{1,0},{2,3},{3,2},{4,5},{5,4},{6,7},{7,6},{8,9},{9,8},{10,11... | collective-permute-start | bytes 1179656 | tf_op jit(solution)/shard_map/ppermute | solution.py:249
  137.3 14.8 %collective-permute-start.28 = (bf16[192,2048]{1,0:T(8,128)(2,1)S(1)}, bf16[192,2048]{1,0:T(8,128)(2,1)S(1)}, u32[]{:S(2)}, u32[]{:S(2)}) collective-permute-start(bf16[192,2048]{1,0:T(8,128)(2,1)S(1)} %pad_maximum_fusion), channel_id=1, source_target_pairs={{0,1},{1,0},{2,3},{3,2},{4,5},{5,4},{6,7},{7,6},{8,9},{9,8},{10,11... | collective-permute-start | bytes 2359304 | tf_op jit(solution)/shard_map/ppermute | solution.py:249
  137.9 12.2 %collective-permute-start.29 = (bf16[48,2048]{1,0:T(8,128)(2,1)S(1)}, bf16[48,2048]{1,0:T(8,128)(2,1)S(1)}, u32[]{:S(2)}, u32[]{:S(2)}) collective-permute-start(bf16[48,2048]{1,0:T(8,128)(2,1)S(1)} %get-tuple-element.165), channel_id=1, source_target_pairs={{0,8},{1,9},{2,10},{3,11},{4,12},{5,13},{6,14},{7,15},{8,0},{9,1},... | collective-permute-start | bytes 589832 | tf_op jit(solution)/shard_map/ppermute | solution.py:249
  138.0 14.2 %collective-permute-start.30 = (bf16[48,2048]{1,0:T(8,128)(2,1)S(1)}, bf16[48,2048]{1,0:T(8,128)(2,1)S(1)}, u32[]{:S(2)}, u32[]{:S(2)}) collective-permute-start(bf16[48,2048]{1,0:T(8,128)(2,1)S(1)} %get-tuple-element.166), channel_id=1, source_target_pairs={{0,10},{1,11},{2,8},{3,9},{4,14},{5,15},{6,12},{7,13},{8,2},{9,3},... | collective-permute-start | bytes 589832 | tf_op jit(solution)/shard_map/ppermute | solution.py:249
  152.2 15.7 %collective-permute-start.31 = (bf16[96,2048]{1,0:T(8,128)(2,1)S(1)}, bf16[96,2048]{1,0:T(8,128)(2,1)S(1)}, u32[]{:S(2)}, u32[]{:S(2)}) collective-permute-start(bf16[96,2048]{1,0:T(8,128)(2,1)S(1)} %get-tuple-element.167), channel_id=1, source_target_pairs={{0,1},{1,0},{2,3},{3,2},{4,5},{5,4},{6,7},{7,6},{8,9},{9,8},{10,11... | collective-permute-start | bytes 1179656 | tf_op jit(solution)/shard_map/ppermute | solution.py:249
  153.9 13.9 %collective-permute-start.32 = (bf16[48,2048]{1,0:T(8,128)(2,1)S(1)}, bf16[48,2048]{1,0:T(8,128)(2,1)S(1)}, u32[]{:S(2)}, u32[]{:S(2)}) collective-permute-start(bf16[48,2048]{1,0:T(8,128)(2,1)S(1)} %get-tuple-element.169), channel_id=1, source_target_pairs={{0,12},{1,13},{2,14},{3,15},{4,8},{5,9},{6,10},{7,11},{8,4},{9,5},... | collective-permute-start | bytes 589832 | tf_op jit(solution)/shard_map/ppermute | solution.py:249
  172.9 18.0 %collective-permute-start.35 = (bf16[96,2048]{1,0:T(8,128)(2,1)S(1)}, bf16[96,2048]{1,0:T(8,128)(2,1)S(1)}, u32[]{:S(2)}, u32[]{:S(2)}) collective-permute-start(bf16[96,2048]{1,0:T(8,128)(2,1)S(1)} %get-tuple-element.173), channel_id=1, source_target_pairs={{0,1},{1,0},{2,3},{3,2},{4,5},{5,4},{6,7},{7,6},{8,9},{9,8},{10,11... | collective-permute-start | bytes 1179656 | tf_op jit(solution)/shard_map/ppermute | solution.py:249
  173.3 13.3 %collective-permute-start.36 = (bf16[48,2048]{1,0:T(8,128)(2,1)S(1)}, bf16[48,2048]{1,0:T(8,128)(2,1)S(1)}, u32[]{:S(2)}, u32[]{:S(2)}) collective-permute-start(bf16[48,2048]{1,0:T(8,128)(2,1)S(1)} %get-tuple-element.175), channel_id=1, source_target_pairs={{0,8},{1,9},{2,10},{3,11},{4,12},{5,13},{6,14},{7,15},{8,0},{9,1},... | collective-permute-start | bytes 589832 | tf_op jit(solution)/shard_map/ppermute | solution.py:249
  173.4 17.4 %collective-permute-start.37 = (bf16[48,2048]{1,0:T(8,128)(2,1)S(1)}, bf16[48,2048]{1,0:T(8,128)(2,1)S(1)}, u32[]{:S(2)}, u32[]{:S(2)}) collective-permute-start(bf16[48,2048]{1,0:T(8,128)(2,1)S(1)} %get-tuple-element.176), channel_id=1, source_target_pairs={{0,10},{1,11},{2,8},{3,9},{4,14},{5,15},{6,12},{7,13},{8,2},{9,3},... | collective-permute-start | bytes 589832 | tf_op jit(solution)/shard_map/ppermute | solution.py:249
  176.9 14.1 %collective-permute-start.39 = (bf16[96,2048]{1,0:T(8,128)(2,1)S(1)}, bf16[96,2048]{1,0:T(8,128)(2,1)S(1)}, u32[]{:S(2)}, u32[]{:S(2)}) collective-permute-start(bf16[96,2048]{1,0:T(8,128)(2,1)S(1)} %pad_maximum_fusion.3), channel_id=1, source_target_pairs={{0,1},{1,0},{2,3},{3,2},{4,5},{5,4},{6,7},{7,6},{8,9},{9,8},{10,11... | collective-permute-start | bytes 1179656 | tf_op jit(solution)/shard_map/ppermute | solution.py:249
  177.2 13.7 %collective-permute-start.40 = (bf16[48,2048]{1,0:T(8,128)(2,1)S(1)}, bf16[48,2048]{1,0:T(8,128)(2,1)S(1)}, u32[]{:S(2)}, u32[]{:S(2)}) collective-permute-start(bf16[48,2048]{1,0:T(8,128)(2,1)S(1)} %get-tuple-element.183), channel_id=1, source_target_pairs={{0,6},{1,7},{2,4},{3,5},{4,2},{5,3},{6,0},{7,1},{8,14},{9,15},{10,... | collective-permute-start | bytes 589832 | tf_op jit(solution)/shard_map/ppermute | solution.py:249
  190.9 14.2 %collective-permute-start.41 = (bf16[96,2048]{1,0:T(8,128)(2,1)S(1)}, bf16[96,2048]{1,0:T(8,128)(2,1)S(1)}, u32[]{:S(2)}, u32[]{:S(2)}) collective-permute-start(bf16[96,2048]{1,0:T(8,128)(2,1)S(1)} %get-tuple-element.184), channel_id=1, source_target_pairs={{0,1},{1,0},{2,3},{3,2},{4,5},{5,4},{6,7},{7,6},{8,9},{9,8},{10,11... | collective-permute-start | bytes 1179656 | tf_op jit(solution)/shard_map/ppermute | solution.py:249
  192.5 12.6 %collective-permute-start.42 = (bf16[96,2048]{1,0:T(8,128)(2,1)S(1)}, bf16[96,2048]{1,0:T(8,128)(2,1)S(1)}, u32[]{:S(2)}, u32[]{:S(2)}) collective-permute-start(bf16[96,2048]{1,0:T(8,128)(2,1)S(1)} %pad_maximum_fusion.4), channel_id=1, source_target_pairs={{0,2},{1,3},{2,0},{3,1},{4,6},{5,7},{6,4},{7,5},{8,10},{9,11},{10,... | collective-permute-start | bytes 1179656 | tf_op jit(solution)/shard_map/ppermute | solution.py:249
  202.7 13.6 %collective-permute-start.47 = (bf16[48,2048]{1,0:T(8,128)(2,1)S(1)}, bf16[48,2048]{1,0:T(8,128)(2,1)S(1)}, u32[]{:S(2)}, u32[]{:S(2)}) collective-permute-start(bf16[48,2048]{1,0:T(8,128)(2,1)S(1)} %get-tuple-element.193), channel_id=1, source_target_pairs={{0,14},{1,15},{2,12},{3,13},{4,10},{5,11},{6,8},{7,9},{8,6},{9,7},... | collective-permute-start | bytes 589832 | tf_op jit(solution)/shard_map/ppermute | solution.py:249
  207.1 12.9 %collective-permute-start.46 = (bf16[48,2048]{1,0:T(8,128)(2,1)S(1)}, bf16[48,2048]{1,0:T(8,128)(2,1)S(1)}, u32[]{:S(2)}, u32[]{:S(2)}) collective-permute-start(bf16[48,2048]{1,0:T(8,128)(2,1)S(1)} %get-tuple-element.192), channel_id=1, source_target_pairs={{0,6},{1,7},{2,4},{3,5},{4,2},{5,3},{6,0},{7,1},{8,14},{9,15},{10,... | collective-permute-start | bytes 589832 | tf_op jit(solution)/shard_map/ppermute | solution.py:249
  (29 other events, 209.5 us)

commit v4 on v3

--- a/solution.py
+++ b/solution.py
@@ -338,9 +338,10 @@
     x_start(3)
     x_start(6)
     z_start("f", slots_f, 1)
+    meet(("b", 7),)
+    z_start("f", slots_f, 4)
     meet(("b", 7), ("f", 1), ("x", 3), ("x", 6))
     x_start(7)
-    z_start("f", slots_f, 4)
     z_start("f", slots_f, 2)
     back_own, kept_own = backward_half(
         [a for i in range(8) for a in held["b", i]], *weights, split
@@ -400,9 +401,9 @@
             terms.append(lax.dot_general(left, kept[b], outer, preferred_element_type=jnp.float32))
         return (terms[0] + terms[1]).astype(jnp.bfloat16)
 
-    grad_gate = weight_term(3, 1, rounds[9])
-    grad_up = weight_term(3, 2, rounds[10])
-    grad_down = weight_term(0, 4, rounds[11])
+    grad_gate = weight_term(3, 1, rounds[10])
+    grad_up = weight_term(3, 2, rounds[11])
+    grad_down = weight_term(0, 4, rounds[12])
 
     back = [a for i in range(8) for a in held["r", i]]
     out = [a for i in range(8) for a in held["o", i]]

time: 222 us -> 218 us (0.982)
  waiting for transfers between devices: 111 us -> 104 us
  starting transfers between devices: 67 us -> 70.3 us
    ppermute x46, waiting for transfers between devices: 110 us -> 103 us  [to_xor(): lax.ppermute(array, 'expert', [(i, i ^ mask) for i in range(devices)])]
    ppermute x46, starting transfers between devices: 66.4 us -> 69.7 us  [to_xor(): lax.ppermute(array, 'expert', [(i, i ^ mask) for i in range(devices)])]
  transfers between devices with their start and end apart: 48 -> 48, of which waited for: 23 -> 24; matrix products, arithmetic and copies ran while one was open for 5% -> 5% of each run, Pallas kernels for 12% -> 12%
where the time goes in v4:
time: 218 us
  waiting for transfers between devices  104 us (48%)
  starting transfers between devices  70.3 us (32%)
  Pallas kernels  27.8 us (13%)
  matrix products  10.3 us (5%)
  local copies, waits for them, and re-layouts  3.49 us (2%)
    ppermute x46, waiting for transfers between devices, to_xor(): lax.ppermute(array, 'expert', [(i, i ^ mask) for i in range(devices)])  103 us
    ppermute x46, starting transfers between devices, to_xor(): lax.ppermute(array, 'expert', [(i, i ^ mask) for i in range(devices)])  69.7 us
    pallas_call x2, Pallas kernels, backward_half(): pl.pallas_call(functools.partial(backward_kernel, n, len(outs)), out_shap...  13.8 us
    dot_general x6, matrix products, weight_term(): lax.dot_general(left, kept[b], outer, preferred_element_type=jnp.float32)  10.3 us
    pallas_call x2, Pallas kernels, forward_half(): pl.pallas_call(functools.partial(forward_kernel, n, len(outs), order or r...  9.06 us
  transfers between devices with their start and end apart: 48, of which 24 were waited for; matrix products, arithmetic and copies ran while one was open for 5% of the time, Pallas kernels for 12%

profile of v4, /device:TPU:0, one launch (start us, length us, event | category | flops | bytes accessed | tf_op | source)
XLA Modules:
  0.0 218.0 jit_solution(15957763559397963426)
XLA Ops:
  6.5 3.0 %collective-permute-start.5 = (bf16[96,2048]{1,0:T(8,128)(2,1)S(1)}, bf16[96,2048]{1,0:T(8,128)(2,1)S(1)}, u32[]{:S(2)}, u32[]{:S(2)}) collective-permute-start(bf16[96,2048]{1,0:T(8,128)(2,1)S(1)} %get-tuple-element.124), channel_id=1, source_target_pairs={{0,2},{1,3},{2,0},{3,1},{4,6},{5,7},{6,4},{7,5},{8,10},{9,11},{10,... | collective-permute-start | bytes 1179656 | tf_op jit(solution)/shard_map/ppermute | solution.py:249
  9.4 2.6 %collective-permute-start.2 = (bf16[96,2048]{1,0:T(8,128)(2,1)S(1)}, bf16[96,2048]{1,0:T(8,128)(2,1)S(1)}, u32[]{:S(2)}, u32[]{:S(2)}) collective-permute-start(bf16[96,2048]{1,0:T(8,128)(2,1)S(1)} %get-tuple-element.119), channel_id=1, source_target_pairs={{0,8},{1,9},{2,10},{3,11},{4,12},{5,13},{6,14},{7,15},{8,0},{9,1},... | collective-permute-start | bytes 1179656 | tf_op jit(solution)/shard_map/ppermute | solution.py:249
  15.5 11.3 %collective-permute-done.7.refs_0_ = bf16[48,2048]{1,0:T(8,128)(2,1)S(1)} collective-permute-done((bf16[48,2048]{1,0:T(8,128)(2,1)S(1)}, bf16[48,2048]{1,0:T(8,128)(2,1)S(1)}, u32[]{:S(2)}, u32[]{:S(2)}) %collective-permute-start.7) | collective-permute-done | bytes 196640 | tf_op jit(solution)/shard_map/ppermute | solution.py:249
  26.8 2.8 %collective-permute-done.2.refs_4_ = bf16[96,2048]{1,0:T(8,128)(2,1)S(1)} collective-permute-done((bf16[96,2048]{1,0:T(8,128)(2,1)S(1)}, bf16[96,2048]{1,0:T(8,128)(2,1)S(1)}, u32[]{:S(2)}, u32[]{:S(2)}) %collective-permute-start.2) | collective-permute-done | bytes 393248 | tf_op jit(solution)/shard_map/ppermute | solution.py:249
  30.3 3.3 %collective-permute-start.3 = (bf16[96,2048]{1,0:T(8,128)(2,1)S(1)}, bf16[96,2048]{1,0:T(8,128)(2,1)S(1)}, u32[]{:S(2)}, u32[]{:S(2)}) collective-permute-start(bf16[96,2048]{1,0:T(8,128)(2,1)S(1)} %get-tuple-element.120), channel_id=1, source_target_pairs={{0,10},{1,11},{2,8},{3,9},{4,14},{5,15},{6,12},{7,13},{8,2},{9,3},... | collective-permute-start | bytes 1179656 | tf_op jit(solution)/shard_map/ppermute | solution.py:249
  35.6 12.2 %collective-permute-done.8.refs_2_ = bf16[96,2048]{1,0:T(8,128)(2,1)S(1)} collective-permute-done((bf16[96,2048]{1,0:T(8,128)(2,1)S(1)}, bf16[96,2048]{1,0:T(8,128)(2,1)S(1)}, u32[]{:S(2)}, u32[]{:S(2)}) %collective-permute-start.8) | collective-permute-done | bytes 393248 | tf_op jit(solution)/shard_map/ppermute | solution.py:249
  47.8 3.5 %collective-permute-done.3.refs_5_ = bf16[96,2048]{1,0:T(8,128)(2,1)S(1)} collective-permute-done((bf16[96,2048]{1,0:T(8,128)(2,1)S(1)}, bf16[96,2048]{1,0:T(8,128)(2,1)S(1)}, u32[]{:S(2)}, u32[]{:S(2)}) %collective-permute-start.3) | collective-permute-done | bytes 393248 | tf_op jit(solution)/shard_map/ppermute | solution.py:249
  56.5 14.9 %collective-permute-done.4.refs_6_ = bf16[96,2048]{1,0:T(8,128)(2,1)S(1)} collective-permute-done((bf16[96,2048]{1,0:T(8,128)(2,1)S(1)}, bf16[96,2048]{1,0:T(8,128)(2,1)S(1)}, u32[]{:S(2)}, u32[]{:S(2)}) %collective-permute-start.4) | collective-permute-done | bytes 393248 | tf_op jit(solution)/shard_map/ppermute | solution.py:249
  71.4 2.5 %collective-permute-start.15 = (bf16[96,2048]{1,0:T(8,128)(2,1)S(1)}, bf16[96,2048]{1,0:T(8,128)(2,1)S(1)}, u32[]{:S(2)}, u32[]{:S(2)}) collective-permute-start(bf16[96,2048]{1,0:T(8,128)(2,1)S(1)} %get-tuple-element.135), channel_id=1, source_target_pairs={{0,14},{1,15},{2,12},{3,13},{4,10},{5,11},{6,8},{7,9},{8,6},{9,7},... | collective-permute-start | bytes 1179656 | tf_op jit(solution)/shard_map/ppermute | solution.py:249
  77.5 6.2 %collective-permute-done.15.refs_7_ = bf16[96,2048]{1,0:T(8,128)(2,1)S(1)} collective-permute-done((bf16[96,2048]{1,0:T(8,128)(2,1)S(1)}, bf16[96,2048]{1,0:T(8,128)(2,1)S(1)}, u32[]{:S(2)}, u32[]{:S(2)}) %collective-permute-start.15) | collective-permute-done | bytes 393248 | tf_op jit(solution)/shard_map/ppermute | solution.py:249
  83.7 7.3 %collective-permute-start.20 = (bf16[48,2048]{1,0:T(8,128)(2,1)S(1)}, bf16[48,2048]{1,0:T(8,128)(2,1)S(1)}, u32[]{:S(2)}, u32[]{:S(2)}) collective-permute-start(bf16[48,2048]{1,0:T(8,128)(2,1)S(1)} %get-tuple-element.142), channel_id=1, source_target_pairs={{0,8},{1,9},{2,10},{3,11},{4,12},{5,13},{6,14},{7,15},{8,0},{9,1},... | collective-permute-start | bytes 589832 | tf_op jit(solution)/shard_map/ppermute | solution.py:249
  92.7 6.8 %backward_half.2 = (bf16[48,2048]{1,0:T(8,128)(2,1)S(1)}, bf16[48,2048]{1,0:T(8,128)(2,1)S(1)}, bf16[96,2048]{1,0:T(8,128)(2,1)S(1)}, bf16[96,2048]{1,0:T(8,128)...) custom-call(bf16[96,2048]{1,0:T(8,128)(2,1)S(1)} %get-tuple-element., ...), custom_call_target="tpu_custom_call" | custom-call | flops 3019898880 | bytes 12582912 | tf_op jit(solution)/shard_map/backward_half/pallas_call | solution.py:203
  101.4 3.7 %collective-permute-start.22 = (bf16[48,2048]{1,0:T(8,128)(2,1)S(1)}, bf16[48,2048]{1,0:T(8,128)(2,1)S(1)}, u32[]{:S(2)}, u32[]{:S(2)}) collective-permute-start(bf16[48,2048]{1,0:T(8,128)(2,1)S(1)} %get-tuple-element.146), channel_id=1, source_target_pairs={{0,10},{1,11},{2,8},{3,9},{4,14},{5,15},{6,12},{7,13},{8,2},{9,3},... | collective-permute-start | bytes 589832 | tf_op jit(solution)/shard_map/ppermute | solution.py:249
  105.1 6.9 %backward_half.3 = (bf16[48,2048]{1,0:T(8,128)(2,1)S(1)}, bf16[48,2048]{1,0:T(8,128)(2,1)S(1)}, bf16[96,2048]{1,0:T(8,128)(2,1)S(1)}, bf16[96,2048]{1,0:T(8,128)...) custom-call(bf16[96,2048]{1,0:T(8,128)(2,1)S(1)} %collective-permute, ...), custom_call_target="tpu_custom_call" | custom-call | flops 3019898880 | bytes 12582912 | tf_op jit(solution)/shard_map/backward_half/pallas_call | solution.py:203
  113.2 3.1 %collective-permute-start.25 = (bf16[48,2048]{1,0:T(8,128)(2,1)S(1)}, bf16[48,2048]{1,0:T(8,128)(2,1)S(1)}, u32[]{:S(2)}, u32[]{:S(2)}) collective-permute-start(bf16[48,2048]{1,0:T(8,128)(2,1)S(1)} %get-tuple-element.152), channel_id=1, source_target_pairs={{0,14},{1,15},{2,12},{3,13},{4,10},{5,11},{6,8},{7,9},{8,6},{9,7},... | collective-permute-start | bytes 589832 | tf_op jit(solution)/shard_map/ppermute | solution.py:249
  119.0 3.2 %collective-permute-done.25.refs_7_ = bf16[48,2048]{1,0:T(8,128)(2,1)S(1)} collective-permute-done((bf16[48,2048]{1,0:T(8,128)(2,1)S(1)}, bf16[48,2048]{1,0:T(8,128)(2,1)S(1)}, u32[]{:S(2)}, u32[]{:S(2)}) %collective-permute-start.25) | collective-permute-done | bytes 196640 | tf_op jit(solution)/shard_map/ppermute | solution.py:249
  124.3 4.5 %forward_half.2 = (bf16[48,2048]{1,0:T(8,128)(2,1)S(1)}, bf16[48,2048]{1,0:T(8,128)(2,1)S(1)}, bf16[96,2048]{1,0:T(8,128)(2,1)S(1)}, bf16[96,2048]{1,0:T(8,128)(2,1)S(1)}, bf16[96,2048]{1,0:T(8,128)(2,1)S(1)}) custom-call(bf16[48,2048]{1,0:T(8,128)(2,1)S(1)} %get-tuple-element.107.refs_0_, bf16[48,2048]{1,0:T(8,128)(2,1)S(1)} %collective-permute-done.14.refs_1_, ...), custom_call_target="tpu_custom_call" | custom-call | flops 1811939328 | bytes 7864320 | tf_op jit(solution)/shard_map/forward_half/pallas_call | solution.py:153
  129.0 5.7 %collective-permute-done.27 = bf16[96,2048]{1,0:T(8,128)(2,1)S(1)} collective-permute-done((bf16[96,2048]{1,0:T(8,128)(2,1)S(1)}, bf16[96,2048]{1,0:T(8,128)(2,1)S(1)}, u32[]{:S(2)}, u32[]{:S(2)}) %collective-permute-start.27) | collective-permute-done | bytes 393248 | tf_op jit(solution)/shard_map/ppermute | solution.py:249
  137.6 2.6 %collective-permute-start.30 = (bf16[48,2048]{1,0:T(8,128)(2,1)S(1)}, bf16[48,2048]{1,0:T(8,128)(2,1)S(1)}, u32[]{:S(2)}, u32[]{:S(2)}) collective-permute-start(bf16[48,2048]{1,0:T(8,128)(2,1)S(1)} %get-tuple-element.166), channel_id=1, source_target_pairs={{0,10},{1,11},{2,8},{3,9},{4,14},{5,15},{6,12},{7,13},{8,2},{9,3},... | collective-permute-start | bytes 589832 | tf_op jit(solution)/shard_map/ppermute | solution.py:249
  141.6 2.3 %fusion = bf16[1,1,2048,384]{3,2,1,0:T(8,128)(2,1)} fusion(f32[2048,384]{1,0:T(8,128)S(1)} %fusion.4, bf16[384,2048]{1,0:T(8,128)(2,1)S(1)} %copy-done.9, bf16[384,384]{1,0:T(8,128)(2,1)S(1)} %get-tuple-element.143), kind=kOutput, calls=%fused_computation.3 | convolution fusion | flops 605552640 | bytes 6586368 | tf_op jit(solution)/shard_map/dot_general | solution.py:401
  143.9 5.4 %collective-permute-done.29.refs_4_ = bf16[48,2048]{1,0:T(8,128)(2,1)S(1)} collective-permute-done((bf16[48,2048]{1,0:T(8,128)(2,1)S(1)}, bf16[48,2048]{1,0:T(8,128)(2,1)S(1)}, u32[]{:S(2)}, u32[]{:S(2)}) %collective-permute-start.29) | collective-permute-done | bytes 196640 | tf_op jit(solution)/shard_map/ppermute | solution.py:249
  152.5 2.8 %collective-permute-start.32 = (bf16[48,2048]{1,0:T(8,128)(2,1)S(1)}, bf16[48,2048]{1,0:T(8,128)(2,1)S(1)}, u32[]{:S(2)}, u32[]{:S(2)}) collective-permute-start(bf16[48,2048]{1,0:T(8,128)(2,1)S(1)} %get-tuple-element.169), channel_id=1, source_target_pairs={{0,12},{1,13},{2,14},{3,15},{4,8},{5,9},{6,10},{7,11},{8,4},{9,5},... | collective-permute-start | bytes 589832 | tf_op jit(solution)/shard_map/ppermute | solution.py:249
  155.3 2.7 %collective-permute-start.33 = (bf16[48,2048]{1,0:T(8,128)(2,1)S(1)}, bf16[48,2048]{1,0:T(8,128)(2,1)S(1)}, u32[]{:S(2)}, u32[]{:S(2)}) collective-permute-start(bf16[48,2048]{1,0:T(8,128)(2,1)S(1)} %get-tuple-element.170), channel_id=1, source_target_pairs={{0,14},{1,15},{2,12},{3,13},{4,10},{5,11},{6,8},{7,9},{8,6},{9,7},... | collective-permute-start | bytes 589832 | tf_op jit(solution)/shard_map/ppermute | solution.py:249
  158.0 4.5 %forward_half.3 = (bf16[48,2048]{1,0:T(8,128)(2,1)S(1)}, bf16[48,2048]{1,0:T(8,128)(2,1)S(1)}, bf16[96,2048]{1,0:T(8,128)(2,1)S(1)}, bf16[96,2048]{1,0:T(8,128)(2,1)S(1)}, bf16[96,2048]{1,0:T(8,128)(2,1)S(1)}) custom-call(bf16[48,2048]{1,0:T(8,128)(2,1)S(1)} %collective-permute-done.7.refs_0_, bf16[144,2048]{1,0:T(8,128)(2,1)S(1)} %collective-permute-done.23.refs_1_, ...), custom_call_target="tpu_custom_call" | custom-call | flops 1811939328 | bytes 7864320 | tf_op jit(solution)/shard_map/forward_half/pallas_call | solution.py:153
  165.3 2.4 %fusion.1 = bf16[1,1,2048,384]{3,2,1,0:T(8,128)(2,1)} fusion(f32[2048,384]{1,0:T(8,128)S(1)} %fusion.5, bf16[384,2048]{1,0:T(8,128)(2,1)S(1)} %copy-done.10, bf16[384,384]{1,0:T(8,128)(2,1)S(1)} %get-tuple-element.200), kind=kOutput, calls=%fused_computation.4 | convolution fusion | flops 605552640 | bytes 6586368 | tf_op jit(solution)/shard_map/dot_general | solution.py:401
  167.8 4.3 %collective-permute-done.34 = bf16[96,2048]{1,0:T(8,128)(2,1)S(1)} collective-permute-done((bf16[96,2048]{1,0:T(8,128)(2,1)S(1)}, bf16[96,2048]{1,0:T(8,128)(2,1)S(1)}, u32[]{:S(2)}, u32[]{:S(2)}) %collective-permute-start.34) | collective-permute-done | bytes 393248 | tf_op jit(solution)/shard_map/ppermute | solution.py:249
  173.4 2.6 %collective-permute-start.37 = (bf16[48,2048]{1,0:T(8,128)(2,1)S(1)}, bf16[48,2048]{1,0:T(8,128)(2,1)S(1)}, u32[]{:S(2)}, u32[]{:S(2)}) collective-permute-start(bf16[48,2048]{1,0:T(8,128)(2,1)S(1)} %get-tuple-element.176), channel_id=1, source_target_pairs={{0,10},{1,11},{2,8},{3,9},{4,14},{5,15},{6,12},{7,13},{8,2},{9,3},... | collective-permute-start | bytes 589832 | tf_op jit(solution)/shard_map/ppermute | solution.py:249
  178.4 6.8 %collective-permute-done.36.refs_5_ = bf16[48,2048]{1,0:T(8,128)(2,1)S(1)} collective-permute-done((bf16[48,2048]{1,0:T(8,128)(2,1)S(1)}, bf16[48,2048]{1,0:T(8,128)(2,1)S(1)}, u32[]{:S(2)}, u32[]{:S(2)}) %collective-permute-start.36) | collective-permute-done | bytes 196640 | tf_op jit(solution)/shard_map/ppermute | solution.py:249
  185.2 5.4 %collective-permute-done.37.refs_6_ = bf16[48,2048]{1,0:T(8,128)(2,1)S(1)} collective-permute-done((bf16[48,2048]{1,0:T(8,128)(2,1)S(1)}, bf16[48,2048]{1,0:T(8,128)(2,1)S(1)}, u32[]{:S(2)}, u32[]{:S(2)}) %collective-permute-start.37) | collective-permute-done | bytes 196640 | tf_op jit(solution)/shard_map/ppermute | solution.py:249
  195.4 6.4 %collective-permute-done.38.refs_7_ = bf16[48,2048]{1,0:T(8,128)(2,1)S(1)} collective-permute-done((bf16[48,2048]{1,0:T(8,128)(2,1)S(1)}, bf16[48,2048]{1,0:T(8,128)(2,1)S(1)}, u32[]{:S(2)}, u32[]{:S(2)}) %collective-permute-start.38) | collective-permute-done | bytes 196640 | tf_op jit(solution)/shard_map/ppermute | solution.py:249
  205.1 2.3 %collective-permute-start.46 = (bf16[48,2048]{1,0:T(8,128)(2,1)S(1)}, bf16[48,2048]{1,0:T(8,128)(2,1)S(1)}, u32[]{:S(2)}, u32[]{:S(2)}) collective-permute-start(bf16[48,2048]{1,0:T(8,128)(2,1)S(1)} %get-tuple-element.192), channel_id=1, source_target_pairs={{0,6},{1,7},{2,4},{3,5},{4,2},{5,3},{6,0},{7,1},{8,14},{9,15},{10,... | collective-permute-start | bytes 589832 | tf_op jit(solution)/shard_map/ppermute | solution.py:249
  207.5 4.0 %collective-permute-done.44 = bf16[96,2048]{1,0:T(8,128)(2,1)S(1)} collective-permute-done((bf16[96,2048]{1,0:T(8,128)(2,1)S(1)}, bf16[96,2048]{1,0:T(8,128)(2,1)S(1)}, u32[]{:S(2)}, u32[]{:S(2)}) %collective-permute-start.44) | collective-permute-done | bytes 393248 | tf_op jit(solution)/shard_map/ppermute | solution.py:249
  (118 shorter events, 59.0 us)
Async XLA Ops:
  6.5 20.4 %collective-permute-start.5 = (bf16[96,2048]{1,0:T(8,128)(2,1)S(1)}, bf16[96,2048]{1,0:T(8,128)(2,1)S(1)}, u32[]{:S(2)}, u32[]{:S(2)}) collective-permute-start(bf16[96,2048]{1,0:T(8,128)(2,1)S(1)} %get-tuple-element.124), channel_id=1, source_target_pairs={{0,2},{1,3},{2,0},{3,1},{4,6},{5,7},{6,4},{7,5},{8,10},{9,11},{10,... | collective-permute-start | bytes 1179656 | tf_op jit(solution)/shard_map/ppermute | solution.py:249
  9.4 20.2 %collective-permute-start.2 = (bf16[96,2048]{1,0:T(8,128)(2,1)S(1)}, bf16[96,2048]{1,0:T(8,128)(2,1)S(1)}, u32[]{:S(2)}, u32[]{:S(2)}) collective-permute-start(bf16[96,2048]{1,0:T(8,128)(2,1)S(1)} %get-tuple-element.119), channel_id=1, source_target_pairs={{0,8},{1,9},{2,10},{3,11},{4,12},{5,13},{6,14},{7,15},{8,0},{9,1},... | collective-permute-start | bytes 1179656 | tf_op jit(solution)/shard_map/ppermute | solution.py:249
  12.0 17.6 %collective-permute-start.6 = (bf16[96,2048]{1,0:T(8,128)(2,1)S(1)}, bf16[96,2048]{1,0:T(8,128)(2,1)S(1)}, u32[]{:S(2)}, u32[]{:S(2)}) collective-permute-start(bf16[96,2048]{1,0:T(8,128)(2,1)S(1)} %get-tuple-element.125.refs_0_), channel_id=1, source_target_pairs={{0,1},{1,0},{2,3},{3,2},{4,5},{5,4},{6,7},{7,6},{8,9},{9,8},{10,11... | collective-permute-start | bytes 1179656 | tf_op jit(solution)/shard_map/ppermute | solution.py:249
  29.6 18.2 %collective-permute-start.8 = (bf16[96,2048]{1,0:T(8,128)(2,1)S(1)}, bf16[96,2048]{1,0:T(8,128)(2,1)S(1)}, u32[]{:S(2)}, u32[]{:S(2)}) collective-permute-start(bf16[96,2048]{1,0:T(8,128)(2,1)S(1)} %get-tuple-element.126), channel_id=1, source_target_pairs={{0,4},{1,5},{2,6},{3,7},{4,0},{5,1},{6,2},{7,3},{8,12},{9,13},{10,... | collective-permute-start | bytes 1179656 | tf_op jit(solution)/shard_map/ppermute | solution.py:249
  30.3 21.0 %collective-permute-start.3 = (bf16[96,2048]{1,0:T(8,128)(2,1)S(1)}, bf16[96,2048]{1,0:T(8,128)(2,1)S(1)}, u32[]{:S(2)}, u32[]{:S(2)}) collective-permute-start(bf16[96,2048]{1,0:T(8,128)(2,1)S(1)} %get-tuple-element.120), channel_id=1, source_target_pairs={{0,10},{1,11},{2,8},{3,9},{4,14},{5,15},{6,12},{7,13},{8,2},{9,3},... | collective-permute-start | bytes 1179656 | tf_op jit(solution)/shard_map/ppermute | solution.py:249
  33.6 17.7 %collective-permute-start.9 = (bf16[96,2048]{1,0:T(8,128)(2,1)S(1)}, bf16[96,2048]{1,0:T(8,128)(2,1)S(1)}, u32[]{:S(2)}, u32[]{:S(2)}) collective-permute-start(bf16[96,2048]{1,0:T(8,128)(2,1)S(1)} %collective-permute-done.5.refs_1_), channel_id=1, source_target_pairs={{0,1},{1,0},{2,3},{3,2},{4,5},{5,4},{6,7},{7,6},{8,9},{9,8},{10,11... | collective-permute-start | bytes 1179656 | tf_op jit(solution)/shard_map/ppermute | solution.py:249
  35.1 17.4 %collective-permute-start.10 = (bf16[96,2048]{1,0:T(8,128)(2,1)S(1)}, bf16[96,2048]{1,0:T(8,128)(2,1)S(1)}, u32[]{:S(2)}, u32[]{:S(2)}) collective-permute-start(bf16[96,2048]{1,0:T(8,128)(2,1)S(1)} %collective-permute-done.2.refs_4_), channel_id=1, source_target_pairs={{0,1},{1,0},{2,3},{3,2},{4,5},{5,4},{6,7},{7,6},{8,9},{9,8},{10,11... | collective-permute-start | bytes 1179656 | tf_op jit(solution)/shard_map/ppermute | solution.py:249
  52.5 21.4 %collective-permute-start.11 = (bf16[96,2048]{1,0:T(8,128)(2,1)S(1)}, bf16[96,2048]{1,0:T(8,128)(2,1)S(1)}, u32[]{:S(2)}, u32[]{:S(2)}) collective-permute-start(bf16[96,2048]{1,0:T(8,128)(2,1)S(1)} %get-tuple-element.129), channel_id=1, source_target_pairs={{0,6},{1,7},{2,4},{3,5},{4,2},{5,3},{6,0},{7,1},{8,14},{9,15},{10,... | collective-permute-start | bytes 1179656 | tf_op jit(solution)/shard_map/ppermute | solution.py:249
  53.8 17.6 %collective-permute-start.4 = (bf16[96,2048]{1,0:T(8,128)(2,1)S(1)}, bf16[96,2048]{1,0:T(8,128)(2,1)S(1)}, u32[]{:S(2)}, u32[]{:S(2)}) collective-permute-start(bf16[96,2048]{1,0:T(8,128)(2,1)S(1)} %get-tuple-element.121), channel_id=1, source_target_pairs={{0,12},{1,13},{2,14},{3,15},{4,8},{5,9},{6,10},{7,11},{8,4},{9,5},... | collective-permute-start | bytes 1179656 | tf_op jit(solution)/shard_map/ppermute | solution.py:249
  54.5 19.4 %collective-permute-start.12 = (bf16[96,2048]{1,0:T(8,128)(2,1)S(1)}, bf16[96,2048]{1,0:T(8,128)(2,1)S(1)}, u32[]{:S(2)}, u32[]{:S(2)}) collective-permute-start(bf16[96,2048]{1,0:T(8,128)(2,1)S(1)} %collective-permute-done.8.refs_2_), channel_id=1, source_target_pairs={{0,1},{1,0},{2,3},{3,2},{4,5},{5,4},{6,7},{7,6},{8,9},{9,8},{10,11... | collective-permute-start | bytes 1179656 | tf_op jit(solution)/shard_map/ppermute | solution.py:249
  56.0 17.9 %collective-permute-start.13 = (bf16[96,2048]{1,0:T(8,128)(2,1)S(1)}, bf16[96,2048]{1,0:T(8,128)(2,1)S(1)}, u32[]{:S(2)}, u32[]{:S(2)}) collective-permute-start(bf16[96,2048]{1,0:T(8,128)(2,1)S(1)} %collective-permute-done.3.refs_5_), channel_id=1, source_target_pairs={{0,1},{1,0},{2,3},{3,2},{4,5},{5,4},{6,7},{7,6},{8,9},{9,8},{10,11... | collective-permute-start | bytes 1179656 | tf_op jit(solution)/shard_map/ppermute | solution.py:249
  71.4 12.3 %collective-permute-start.15 = (bf16[96,2048]{1,0:T(8,128)(2,1)S(1)}, bf16[96,2048]{1,0:T(8,128)(2,1)S(1)}, u32[]{:S(2)}, u32[]{:S(2)}) collective-permute-start(bf16[96,2048]{1,0:T(8,128)(2,1)S(1)} %get-tuple-element.135), channel_id=1, source_target_pairs={{0,14},{1,15},{2,12},{3,13},{4,10},{5,11},{6,8},{7,9},{8,6},{9,7},... | collective-permute-start | bytes 1179656 | tf_op jit(solution)/shard_map/ppermute | solution.py:249
  73.9 17.2 %collective-permute-start.16 = (bf16[96,2048]{1,0:T(8,128)(2,1)S(1)}, bf16[96,2048]{1,0:T(8,128)(2,1)S(1)}, u32[]{:S(2)}, u32[]{:S(2)}) collective-permute-start(bf16[96,2048]{1,0:T(8,128)(2,1)S(1)} %collective-permute-done.11.refs_3_), channel_id=1, source_target_pairs={{0,1},{1,0},{2,3},{3,2},{4,5},{5,4},{6,7},{7,6},{8,9},{9,8},{10,11... | collective-permute-start | bytes 1179656 | tf_op jit(solution)/shard_map/ppermute | solution.py:249
  75.5 15.6 %collective-permute-start.17 = (bf16[96,2048]{1,0:T(8,128)(2,1)S(1)}, bf16[96,2048]{1,0:T(8,128)(2,1)S(1)}, u32[]{:S(2)}, u32[]{:S(2)}) collective-permute-start(bf16[96,2048]{1,0:T(8,128)(2,1)S(1)} %collective-permute-done.4.refs_6_), channel_id=1, source_target_pairs={{0,1},{1,0},{2,3},{3,2},{4,5},{5,4},{6,7},{7,6},{8,9},{9,8},{10,11... | collective-permute-start | bytes 1179656 | tf_op jit(solution)/shard_map/ppermute | solution.py:249
  76.0 15.1 %collective-permute-start.14 = (bf16[48,2048]{1,0:T(8,128)(2,1)S(1)}, bf16[48,2048]{1,0:T(8,128)(2,1)S(1)}, u32[]{:S(2)}, u32[]{:S(2)}) collective-permute-start(bf16[48,2048]{1,0:T(8,128)(2,1)S(1)} %get-tuple-element.132), channel_id=1, source_target_pairs={{0,2},{1,3},{2,0},{3,1},{4,6},{5,7},{6,4},{7,5},{8,10},{9,11},{10,... | collective-permute-start | bytes 589832 | tf_op jit(solution)/shard_map/ppermute | solution.py:249
  83.7 15.8 %collective-permute-start.20 = (bf16[48,2048]{1,0:T(8,128)(2,1)S(1)}, bf16[48,2048]{1,0:T(8,128)(2,1)S(1)}, u32[]{:S(2)}, u32[]{:S(2)}) collective-permute-start(bf16[48,2048]{1,0:T(8,128)(2,1)S(1)} %get-tuple-element.142), channel_id=1, source_target_pairs={{0,8},{1,9},{2,10},{3,11},{4,12},{5,13},{6,14},{7,15},{8,0},{9,1},... | collective-permute-start | bytes 589832 | tf_op jit(solution)/shard_map/ppermute | solution.py:249
  99.9 13.2 %collective-permute-start.23 = (bf16[144,2048]{1,0:T(8,128)(2,1)S(1)}, bf16[144,2048]{1,0:T(8,128)(2,1)S(1)}, u32[]{:S(2)}, u32[]{:S(2)}) collective-permute-start(bf16[144,2048]{1,0:T(8,128)(2,1)S(1)} %pad_maximum_fusion.1), channel_id=1, source_target_pairs={{0,1},{1,0},{2,3},{3,2},{4,5},{5,4},{6,7},{7,6},{8,9},{9,8},{10,11... | collective-permute-start | bytes 1769480 | tf_op jit(solution)/shard_map/ppermute | solution.py:249
  117.0 12.0 %collective-permute-start.26 = (bf16[96,2048]{1,0:T(8,128)(2,1)S(1)}, bf16[96,2048]{1,0:T(8,128)(2,1)S(1)}, u32[]{:S(2)}, u32[]{:S(2)}) collective-permute-start(bf16[96,2048]{1,0:T(8,128)(2,1)S(1)} %get-tuple-element.156), channel_id=1, source_target_pairs={{0,1},{1,0},{2,3},{3,2},{4,5},{5,4},{6,7},{7,6},{8,9},{9,8},{10,11... | collective-permute-start | bytes 1179656 | tf_op jit(solution)/shard_map/ppermute | solution.py:249
  118.5 16.2 %collective-permute-start.27 = (bf16[96,2048]{1,0:T(8,128)(2,1)S(1)}, bf16[96,2048]{1,0:T(8,128)(2,1)S(1)}, u32[]{:S(2)}, u32[]{:S(2)}) collective-permute-start(bf16[96,2048]{1,0:T(8,128)(2,1)S(1)} %get-tuple-element.158), channel_id=1, source_target_pairs={{0,1},{1,0},{2,3},{3,2},{4,5},{5,4},{6,7},{7,6},{8,9},{9,8},{10,11... | collective-permute-start | bytes 1179656 | tf_op jit(solution)/shard_map/ppermute | solution.py:249
  134.7 16.5 %collective-permute-start.28 = (bf16[192,2048]{1,0:T(8,128)(2,1)S(1)}, bf16[192,2048]{1,0:T(8,128)(2,1)S(1)}, u32[]{:S(2)}, u32[]{:S(2)}) collective-permute-start(bf16[192,2048]{1,0:T(8,128)(2,1)S(1)} %pad_maximum_fusion), channel_id=1, source_target_pairs={{0,1},{1,0},{2,3},{3,2},{4,5},{5,4},{6,7},{7,6},{8,9},{9,8},{10,11... | collective-permute-start | bytes 2359304 | tf_op jit(solution)/shard_map/ppermute | solution.py:249
  136.3 13.0 %collective-permute-start.29 = (bf16[48,2048]{1,0:T(8,128)(2,1)S(1)}, bf16[48,2048]{1,0:T(8,128)(2,1)S(1)}, u32[]{:S(2)}, u32[]{:S(2)}) collective-permute-start(bf16[48,2048]{1,0:T(8,128)(2,1)S(1)} %get-tuple-element.165), channel_id=1, source_target_pairs={{0,8},{1,9},{2,10},{3,11},{4,12},{5,13},{6,14},{7,15},{8,0},{9,1},... | collective-permute-start | bytes 589832 | tf_op jit(solution)/shard_map/ppermute | solution.py:249
  137.6 13.6 %collective-permute-start.30 = (bf16[48,2048]{1,0:T(8,128)(2,1)S(1)}, bf16[48,2048]{1,0:T(8,128)(2,1)S(1)}, u32[]{:S(2)}, u32[]{:S(2)}) collective-permute-start(bf16[48,2048]{1,0:T(8,128)(2,1)S(1)} %get-tuple-element.166), channel_id=1, source_target_pairs={{0,10},{1,11},{2,8},{3,9},{4,14},{5,15},{6,12},{7,13},{8,2},{9,3},... | collective-permute-start | bytes 589832 | tf_op jit(solution)/shard_map/ppermute | solution.py:249
  151.2 16.5 %collective-permute-start.31 = (bf16[96,2048]{1,0:T(8,128)(2,1)S(1)}, bf16[96,2048]{1,0:T(8,128)(2,1)S(1)}, u32[]{:S(2)}, u32[]{:S(2)}) collective-permute-start(bf16[96,2048]{1,0:T(8,128)(2,1)S(1)} %get-tuple-element.167), channel_id=1, source_target_pairs={{0,1},{1,0},{2,3},{3,2},{4,5},{5,4},{6,7},{7,6},{8,9},{9,8},{10,11... | collective-permute-start | bytes 1179656 | tf_op jit(solution)/shard_map/ppermute | solution.py:249
  152.5 15.2 %collective-permute-start.32 = (bf16[48,2048]{1,0:T(8,128)(2,1)S(1)}, bf16[48,2048]{1,0:T(8,128)(2,1)S(1)}, u32[]{:S(2)}, u32[]{:S(2)}) collective-permute-start(bf16[48,2048]{1,0:T(8,128)(2,1)S(1)} %get-tuple-element.169), channel_id=1, source_target_pairs={{0,12},{1,13},{2,14},{3,15},{4,8},{5,9},{6,10},{7,11},{8,4},{9,5},... | collective-permute-start | bytes 589832 | tf_op jit(solution)/shard_map/ppermute | solution.py:249
  155.3 12.4 %collective-permute-start.33 = (bf16[48,2048]{1,0:T(8,128)(2,1)S(1)}, bf16[48,2048]{1,0:T(8,128)(2,1)S(1)}, u32[]{:S(2)}, u32[]{:S(2)}) collective-permute-start(bf16[48,2048]{1,0:T(8,128)(2,1)S(1)} %get-tuple-element.170), channel_id=1, source_target_pairs={{0,14},{1,15},{2,12},{3,13},{4,10},{5,11},{6,8},{7,9},{8,6},{9,7},... | collective-permute-start | bytes 589832 | tf_op jit(solution)/shard_map/ppermute | solution.py:249
  172.0 19.1 %collective-permute-start.35 = (bf16[96,2048]{1,0:T(8,128)(2,1)S(1)}, bf16[96,2048]{1,0:T(8,128)(2,1)S(1)}, u32[]{:S(2)}, u32[]{:S(2)}) collective-permute-start(bf16[96,2048]{1,0:T(8,128)(2,1)S(1)} %get-tuple-element.173), channel_id=1, source_target_pairs={{0,1},{1,0},{2,3},{3,2},{4,5},{5,4},{6,7},{7,6},{8,9},{9,8},{10,11... | collective-permute-start | bytes 1179656 | tf_op jit(solution)/shard_map/ppermute | solution.py:249
  173.3 11.9 %collective-permute-start.36 = (bf16[48,2048]{1,0:T(8,128)(2,1)S(1)}, bf16[48,2048]{1,0:T(8,128)(2,1)S(1)}, u32[]{:S(2)}, u32[]{:S(2)}) collective-permute-start(bf16[48,2048]{1,0:T(8,128)(2,1)S(1)} %get-tuple-element.175), channel_id=1, source_target_pairs={{0,8},{1,9},{2,10},{3,11},{4,12},{5,13},{6,14},{7,15},{8,0},{9,1},... | collective-permute-start | bytes 589832 | tf_op jit(solution)/shard_map/ppermute | solution.py:249
  173.4 17.3 %collective-permute-start.37 = (bf16[48,2048]{1,0:T(8,128)(2,1)S(1)}, bf16[48,2048]{1,0:T(8,128)(2,1)S(1)}, u32[]{:S(2)}, u32[]{:S(2)}) collective-permute-start(bf16[48,2048]{1,0:T(8,128)(2,1)S(1)} %get-tuple-element.176), channel_id=1, source_target_pairs={{0,10},{1,11},{2,8},{3,9},{4,14},{5,15},{6,12},{7,13},{8,2},{9,3},... | collective-permute-start | bytes 589832 | tf_op jit(solution)/shard_map/ppermute | solution.py:249
  176.0 15.2 %collective-permute-start.39 = (bf16[96,2048]{1,0:T(8,128)(2,1)S(1)}, bf16[96,2048]{1,0:T(8,128)(2,1)S(1)}, u32[]{:S(2)}, u32[]{:S(2)}) collective-permute-start(bf16[96,2048]{1,0:T(8,128)(2,1)S(1)} %pad_maximum_fusion.3), channel_id=1, source_target_pairs={{0,1},{1,0},{2,3},{3,2},{4,5},{5,4},{6,7},{7,6},{8,9},{9,8},{10,11... | collective-permute-start | bytes 1179656 | tf_op jit(solution)/shard_map/ppermute | solution.py:249
  177.2 13.9 %collective-permute-start.40 = (bf16[48,2048]{1,0:T(8,128)(2,1)S(1)}, bf16[48,2048]{1,0:T(8,128)(2,1)S(1)}, u32[]{:S(2)}, u32[]{:S(2)}) collective-permute-start(bf16[48,2048]{1,0:T(8,128)(2,1)S(1)} %get-tuple-element.183), channel_id=1, source_target_pairs={{0,6},{1,7},{2,4},{3,5},{4,2},{5,3},{6,0},{7,1},{8,14},{9,15},{10,... | collective-permute-start | bytes 589832 | tf_op jit(solution)/shard_map/ppermute | solution.py:249
  191.2 12.5 %collective-permute-start.41 = (bf16[96,2048]{1,0:T(8,128)(2,1)S(1)}, bf16[96,2048]{1,0:T(8,128)(2,1)S(1)}, u32[]{:S(2)}, u32[]{:S(2)}) collective-permute-start(bf16[96,2048]{1,0:T(8,128)(2,1)S(1)} %get-tuple-element.184), channel_id=1, source_target_pairs={{0,1},{1,0},{2,3},{3,2},{4,5},{5,4},{6,7},{7,6},{8,9},{9,8},{10,11... | collective-permute-start | bytes 1179656 | tf_op jit(solution)/shard_map/ppermute | solution.py:249
  191.5 12.1 %collective-permute-start.42 = (bf16[96,2048]{1,0:T(8,128)(2,1)S(1)}, bf16[96,2048]{1,0:T(8,128)(2,1)S(1)}, u32[]{:S(2)}, u32[]{:S(2)}) collective-permute-start(bf16[96,2048]{1,0:T(8,128)(2,1)S(1)} %pad_maximum_fusion.4), channel_id=1, source_target_pairs={{0,2},{1,3},{2,0},{3,1},{4,6},{5,7},{6,4},{7,5},{8,10},{9,11},{10,... | collective-permute-start | bytes 1179656 | tf_op jit(solution)/shard_map/ppermute | solution.py:249
  (29 other events, 205.4 us)

commit v5 on v4

--- a/solution.py
+++ b/solution.py
@@ -340,8 +340,9 @@
     z_start("f", slots_f, 1)
     meet(("b", 7),)
     z_start("f", slots_f, 4)
+    meet(("x", 3), ("x", 6))
+    x_start(7)
     meet(("b", 7), ("f", 1), ("x", 3), ("x", 6))
-    x_start(7)
     z_start("f", slots_f, 2)
     back_own, kept_own = backward_half(
         [a for i in range(8) for a in held["b", i]], *weights, split
@@ -380,8 +381,9 @@
     give_back("r", back_own, 3)
     meet(("o", 4), ("o", 5))
     give_back("o", out_own, 6)
+    meet(("ox", 3), ("bx", 1))
+    part_start("ox", out_other, 1)
     meet(("o", 4), ("o", 5), ("ox", 3), ("bx", 1), ("r", 3))
-    part_start("ox", out_other, 1)
     give_both(1)
     give_back("r", back_own, 2)
     meet(("o", 6),)
@@ -401,9 +403,9 @@
             terms.append(lax.dot_general(left, kept[b], outer, preferred_element_type=jnp.float32))
         return (terms[0] + terms[1]).astype(jnp.bfloat16)
 
-    grad_gate = weight_term(3, 1, rounds[10])
-    grad_up = weight_term(3, 2, rounds[11])
-    grad_down = weight_term(0, 4, rounds[12])
+    grad_gate = weight_term(3, 1, rounds[11])
+    grad_up = weight_term(3, 2, rounds[12])
+    grad_down = weight_term(0, 4, rounds[13])
 
     back = [a for i in range(8) for a in held["r", i]]
     out = [a for i in range(8) for a in held["o", i]]

time: 218 us -> 218 us (level)
  no operation moved by 1% of the time
where the time goes in v5:
time: 218 us; the launch traced here: 217 us
  waiting for transfers between devices  103 us (47%)
  starting transfers between devices  70.6 us (32%)
  Pallas kernels  27.8 us (13%)
  matrix products  10.3 us (5%)
  local copies, waits for them, and re-layouts  3.49 us (2%)
    ppermute x46, waiting for transfers between devices, to_xor(): lax.ppermute(array, 'expert', [(i, i ^ mask) for i in range(devices)])  102 us
    ppermute x46, starting transfers between devices, to_xor(): lax.ppermute(array, 'expert', [(i, i ^ mask) for i in range(devices)])  70.1 us
    pallas_call x2, Pallas kernels, backward_half(): pl.pallas_call(functools.partial(backward_kernel, n, len(outs)), out_shap...  13.8 us
    dot_general x6, matrix products, weight_term(): lax.dot_general(left, kept[b], outer, preferred_element_type=jnp.float32)  10.3 us
    pallas_call x2, Pallas kernels, forward_half(): pl.pallas_call(functools.partial(forward_kernel, n, len(outs), order or r...  9.06 us
  transfers between devices with their start and end apart: 48, of which 24 were waited for; matrix products, arithmetic and copies ran while one was open for 5% of the time, Pallas kernels for 12%

profile of v5, /device:TPU:0, one launch (start us, length us, event | category | flops | bytes accessed | tf_op | source)
XLA Modules:
  0.0 217.4 jit_solution(3102812963106334946)
XLA Ops:
  6.5 3.0 %collective-permute-start.5 = (bf16[96,2048]{1,0:T(8,128)(2,1)S(1)}, bf16[96,2048]{1,0:T(8,128)(2,1)S(1)}, u32[]{:S(2)}, u32[]{:S(2)}) collective-permute-start(bf16[96,2048]{1,0:T(8,128)(2,1)S(1)} %get-tuple-element.124), channel_id=1, source_target_pairs={{0,2},{1,3},{2,0},{3,1},{4,6},{5,7},{6,4},{7,5},{8,10},{9,11},{10,... | collective-permute-start | bytes 1179656 | tf_op jit(solution)/shard_map/ppermute | solution.py:249
  9.4 2.6 %collective-permute-start.2 = (bf16[96,2048]{1,0:T(8,128)(2,1)S(1)}, bf16[96,2048]{1,0:T(8,128)(2,1)S(1)}, u32[]{:S(2)}, u32[]{:S(2)}) collective-permute-start(bf16[96,2048]{1,0:T(8,128)(2,1)S(1)} %get-tuple-element.119), channel_id=1, source_target_pairs={{0,8},{1,9},{2,10},{3,11},{4,12},{5,13},{6,14},{7,15},{8,0},{9,1},... | collective-permute-start | bytes 1179656 | tf_op jit(solution)/shard_map/ppermute | solution.py:249
  15.5 11.3 %collective-permute-done.7.refs_0_ = bf16[48,2048]{1,0:T(8,128)(2,1)S(1)} collective-permute-done((bf16[48,2048]{1,0:T(8,128)(2,1)S(1)}, bf16[48,2048]{1,0:T(8,128)(2,1)S(1)}, u32[]{:S(2)}, u32[]{:S(2)}) %collective-permute-start.7) | collective-permute-done | bytes 196640 | tf_op jit(solution)/shard_map/ppermute | solution.py:249
  26.8 2.8 %collective-permute-done.2.refs_4_ = bf16[96,2048]{1,0:T(8,128)(2,1)S(1)} collective-permute-done((bf16[96,2048]{1,0:T(8,128)(2,1)S(1)}, bf16[96,2048]{1,0:T(8,128)(2,1)S(1)}, u32[]{:S(2)}, u32[]{:S(2)}) %collective-permute-start.2) | collective-permute-done | bytes 393248 | tf_op jit(solution)/shard_map/ppermute | solution.py:249
  30.3 3.3 %collective-permute-start.3 = (bf16[96,2048]{1,0:T(8,128)(2,1)S(1)}, bf16[96,2048]{1,0:T(8,128)(2,1)S(1)}, u32[]{:S(2)}, u32[]{:S(2)}) collective-permute-start(bf16[96,2048]{1,0:T(8,128)(2,1)S(1)} %get-tuple-element.120), channel_id=1, source_target_pairs={{0,10},{1,11},{2,8},{3,9},{4,14},{5,15},{6,12},{7,13},{8,2},{9,3},... | collective-permute-start | bytes 1179656 | tf_op jit(solution)/shard_map/ppermute | solution.py:249
  35.6 12.2 %collective-permute-done.8.refs_2_ = bf16[96,2048]{1,0:T(8,128)(2,1)S(1)} collective-permute-done((bf16[96,2048]{1,0:T(8,128)(2,1)S(1)}, bf16[96,2048]{1,0:T(8,128)(2,1)S(1)}, u32[]{:S(2)}, u32[]{:S(2)}) %collective-permute-start.8) | collective-permute-done | bytes 393248 | tf_op jit(solution)/shard_map/ppermute | solution.py:249
  47.8 3.5 %collective-permute-done.3.refs_5_ = bf16[96,2048]{1,0:T(8,128)(2,1)S(1)} collective-permute-done((bf16[96,2048]{1,0:T(8,128)(2,1)S(1)}, bf16[96,2048]{1,0:T(8,128)(2,1)S(1)}, u32[]{:S(2)}, u32[]{:S(2)}) %collective-permute-start.3) | collective-permute-done | bytes 393248 | tf_op jit(solution)/shard_map/ppermute | solution.py:249
  56.5 14.9 %collective-permute-done.4.refs_6_ = bf16[96,2048]{1,0:T(8,128)(2,1)S(1)} collective-permute-done((bf16[96,2048]{1,0:T(8,128)(2,1)S(1)}, bf16[96,2048]{1,0:T(8,128)(2,1)S(1)}, u32[]{:S(2)}, u32[]{:S(2)}) %collective-permute-start.4) | collective-permute-done | bytes 393248 | tf_op jit(solution)/shard_map/ppermute | solution.py:249
  71.4 2.5 %collective-permute-start.15 = (bf16[96,2048]{1,0:T(8,128)(2,1)S(1)}, bf16[96,2048]{1,0:T(8,128)(2,1)S(1)}, u32[]{:S(2)}, u32[]{:S(2)}) collective-permute-start(bf16[96,2048]{1,0:T(8,128)(2,1)S(1)} %get-tuple-element.135), channel_id=1, source_target_pairs={{0,14},{1,15},{2,12},{3,13},{4,10},{5,11},{6,8},{7,9},{8,6},{9,7},... | collective-permute-start | bytes 1179656 | tf_op jit(solution)/shard_map/ppermute | solution.py:249
  77.5 6.2 %collective-permute-done.15.refs_7_ = bf16[96,2048]{1,0:T(8,128)(2,1)S(1)} collective-permute-done((bf16[96,2048]{1,0:T(8,128)(2,1)S(1)}, bf16[96,2048]{1,0:T(8,128)(2,1)S(1)}, u32[]{:S(2)}, u32[]{:S(2)}) %collective-permute-start.15) | collective-permute-done | bytes 393248 | tf_op jit(solution)/shard_map/ppermute | solution.py:249
  83.7 7.3 %collective-permute-start.20 = (bf16[48,2048]{1,0:T(8,128)(2,1)S(1)}, bf16[48,2048]{1,0:T(8,128)(2,1)S(1)}, u32[]{:S(2)}, u32[]{:S(2)}) collective-permute-start(bf16[48,2048]{1,0:T(8,128)(2,1)S(1)} %get-tuple-element.142), channel_id=1, source_target_pairs={{0,8},{1,9},{2,10},{3,11},{4,12},{5,13},{6,14},{7,15},{8,0},{9,1},... | collective-permute-start | bytes 589832 | tf_op jit(solution)/shard_map/ppermute | solution.py:249
  92.7 6.8 %backward_half.2 = (bf16[48,2048]{1,0:T(8,128)(2,1)S(1)}, bf16[48,2048]{1,0:T(8,128)(2,1)S(1)}, bf16[96,2048]{1,0:T(8,128)(2,1)S(1)}, bf16[96,2048]{1,0:T(8,128)...) custom-call(bf16[96,2048]{1,0:T(8,128)(2,1)S(1)} %get-tuple-element., ...), custom_call_target="tpu_custom_call" | custom-call | flops 3019898880 | bytes 12582912 | tf_op jit(solution)/shard_map/backward_half/pallas_call | solution.py:203
  101.4 3.7 %collective-permute-start.22 = (bf16[48,2048]{1,0:T(8,128)(2,1)S(1)}, bf16[48,2048]{1,0:T(8,128)(2,1)S(1)}, u32[]{:S(2)}, u32[]{:S(2)}) collective-permute-start(bf16[48,2048]{1,0:T(8,128)(2,1)S(1)} %get-tuple-element.146), channel_id=1, source_target_pairs={{0,10},{1,11},{2,8},{3,9},{4,14},{5,15},{6,12},{7,13},{8,2},{9,3},... | collective-permute-start | bytes 589832 | tf_op jit(solution)/shard_map/ppermute | solution.py:249
  105.1 6.9 %backward_half.3 = (bf16[48,2048]{1,0:T(8,128)(2,1)S(1)}, bf16[48,2048]{1,0:T(8,128)(2,1)S(1)}, bf16[96,2048]{1,0:T(8,128)(2,1)S(1)}, bf16[96,2048]{1,0:T(8,128)...) custom-call(bf16[96,2048]{1,0:T(8,128)(2,1)S(1)} %collective-permute, ...), custom_call_target="tpu_custom_call" | custom-call | flops 3019898880 | bytes 12582912 | tf_op jit(solution)/shard_map/backward_half/pallas_call | solution.py:203
  113.2 3.1 %collective-permute-start.25 = (bf16[48,2048]{1,0:T(8,128)(2,1)S(1)}, bf16[48,2048]{1,0:T(8,128)(2,1)S(1)}, u32[]{:S(2)}, u32[]{:S(2)}) collective-permute-start(bf16[48,2048]{1,0:T(8,128)(2,1)S(1)} %get-tuple-element.152), channel_id=1, source_target_pairs={{0,14},{1,15},{2,12},{3,13},{4,10},{5,11},{6,8},{7,9},{8,6},{9,7},... | collective-permute-start | bytes 589832 | tf_op jit(solution)/shard_map/ppermute | solution.py:249
  119.0 3.2 %collective-permute-done.25.refs_7_ = bf16[48,2048]{1,0:T(8,128)(2,1)S(1)} collective-permute-done((bf16[48,2048]{1,0:T(8,128)(2,1)S(1)}, bf16[48,2048]{1,0:T(8,128)(2,1)S(1)}, u32[]{:S(2)}, u32[]{:S(2)}) %collective-permute-start.25) | collective-permute-done | bytes 196640 | tf_op jit(solution)/shard_map/ppermute | solution.py:249
  124.3 4.5 %forward_half.2 = (bf16[48,2048]{1,0:T(8,128)(2,1)S(1)}, bf16[48,2048]{1,0:T(8,128)(2,1)S(1)}, bf16[96,2048]{1,0:T(8,128)(2,1)S(1)}, bf16[96,2048]{1,0:T(8,128)(2,1)S(1)}, bf16[96,2048]{1,0:T(8,128)(2,1)S(1)}) custom-call(bf16[48,2048]{1,0:T(8,128)(2,1)S(1)} %get-tuple-element.107.refs_0_, bf16[48,2048]{1,0:T(8,128)(2,1)S(1)} %collective-permute-done.14.refs_1_, ...), custom_call_target="tpu_custom_call" | custom-call | flops 1811939328 | bytes 7864320 | tf_op jit(solution)/shard_map/forward_half/pallas_call | solution.py:153
  129.0 5.7 %collective-permute-done.27 = bf16[96,2048]{1,0:T(8,128)(2,1)S(1)} collective-permute-done((bf16[96,2048]{1,0:T(8,128)(2,1)S(1)}, bf16[96,2048]{1,0:T(8,128)(2,1)S(1)}, u32[]{:S(2)}, u32[]{:S(2)}) %collective-permute-start.27) | collective-permute-done | bytes 393248 | tf_op jit(solution)/shard_map/ppermute | solution.py:249
  137.6 2.6 %collective-permute-start.30 = (bf16[48,2048]{1,0:T(8,128)(2,1)S(1)}, bf16[48,2048]{1,0:T(8,128)(2,1)S(1)}, u32[]{:S(2)}, u32[]{:S(2)}) collective-permute-start(bf16[48,2048]{1,0:T(8,128)(2,1)S(1)} %get-tuple-element.166), channel_id=1, source_target_pairs={{0,10},{1,11},{2,8},{3,9},{4,14},{5,15},{6,12},{7,13},{8,2},{9,3},... | collective-permute-start | bytes 589832 | tf_op jit(solution)/shard_map/ppermute | solution.py:249
  141.6 2.3 %fusion = bf16[1,1,2048,384]{3,2,1,0:T(8,128)(2,1)} fusion(f32[2048,384]{1,0:T(8,128)S(1)} %fusion.4, bf16[384,2048]{1,0:T(8,128)(2,1)S(1)} %copy-done.9, bf16[384,384]{1,0:T(8,128)(2,1)S(1)} %get-tuple-element.143), kind=kOutput, calls=%fused_computation.3 | convolution fusion | flops 605552640 | bytes 6586368 | tf_op jit(solution)/shard_map/dot_general | solution.py:403
  143.9 5.4 %collective-permute-done.29.refs_4_ = bf16[48,2048]{1,0:T(8,128)(2,1)S(1)} collective-permute-done((bf16[48,2048]{1,0:T(8,128)(2,1)S(1)}, bf16[48,2048]{1,0:T(8,128)(2,1)S(1)}, u32[]{:S(2)}, u32[]{:S(2)}) %collective-permute-start.29) | collective-permute-done | bytes 196640 | tf_op jit(solution)/shard_map/ppermute | solution.py:249
  152.5 2.8 %collective-permute-start.32 = (bf16[48,2048]{1,0:T(8,128)(2,1)S(1)}, bf16[48,2048]{1,0:T(8,128)(2,1)S(1)}, u32[]{:S(2)}, u32[]{:S(2)}) collective-permute-start(bf16[48,2048]{1,0:T(8,128)(2,1)S(1)} %get-tuple-element.169), channel_id=1, source_target_pairs={{0,12},{1,13},{2,14},{3,15},{4,8},{5,9},{6,10},{7,11},{8,4},{9,5},... | collective-permute-start | bytes 589832 | tf_op jit(solution)/shard_map/ppermute | solution.py:249
  155.3 2.7 %collective-permute-start.33 = (bf16[48,2048]{1,0:T(8,128)(2,1)S(1)}, bf16[48,2048]{1,0:T(8,128)(2,1)S(1)}, u32[]{:S(2)}, u32[]{:S(2)}) collective-permute-start(bf16[48,2048]{1,0:T(8,128)(2,1)S(1)} %get-tuple-element.170), channel_id=1, source_target_pairs={{0,14},{1,15},{2,12},{3,13},{4,10},{5,11},{6,8},{7,9},{8,6},{9,7},... | collective-permute-start | bytes 589832 | tf_op jit(solution)/shard_map/ppermute | solution.py:249
  158.0 4.5 %forward_half.3 = (bf16[48,2048]{1,0:T(8,128)(2,1)S(1)}, bf16[48,2048]{1,0:T(8,128)(2,1)S(1)}, bf16[96,2048]{1,0:T(8,128)(2,1)S(1)}, bf16[96,2048]{1,0:T(8,128)(2,1)S(1)}, bf16[96,2048]{1,0:T(8,128)(2,1)S(1)}) custom-call(bf16[48,2048]{1,0:T(8,128)(2,1)S(1)} %collective-permute-done.7.refs_0_, bf16[144,2048]{1,0:T(8,128)(2,1)S(1)} %collective-permute-done.23.refs_1_, ...), custom_call_target="tpu_custom_call" | custom-call | flops 1811939328 | bytes 7864320 | tf_op jit(solution)/shard_map/forward_half/pallas_call | solution.py:153
  165.3 2.4 %fusion.1 = bf16[1,1,2048,384]{3,2,1,0:T(8,128)(2,1)} fusion(f32[2048,384]{1,0:T(8,128)S(1)} %fusion.5, bf16[384,2048]{1,0:T(8,128)(2,1)S(1)} %copy-done.10, bf16[384,384]{1,0:T(8,128)(2,1)S(1)} %get-tuple-element.200), kind=kOutput, calls=%fused_computation.4 | convolution fusion | flops 605552640 | bytes 6586368 | tf_op jit(solution)/shard_map/dot_general | solution.py:403
  167.8 4.3 %collective-permute-done.34 = bf16[96,2048]{1,0:T(8,128)(2,1)S(1)} collective-permute-done((bf16[96,2048]{1,0:T(8,128)(2,1)S(1)}, bf16[96,2048]{1,0:T(8,128)(2,1)S(1)}, u32[]{:S(2)}, u32[]{:S(2)}) %collective-permute-start.34) | collective-permute-done | bytes 393248 | tf_op jit(solution)/shard_map/ppermute | solution.py:249
  173.4 2.6 %collective-permute-start.37 = (bf16[48,2048]{1,0:T(8,128)(2,1)S(1)}, bf16[48,2048]{1,0:T(8,128)(2,1)S(1)}, u32[]{:S(2)}, u32[]{:S(2)}) collective-permute-start(bf16[48,2048]{1,0:T(8,128)(2,1)S(1)} %get-tuple-element.176), channel_id=1, source_target_pairs={{0,10},{1,11},{2,8},{3,9},{4,14},{5,15},{6,12},{7,13},{8,2},{9,3},... | collective-permute-start | bytes 589832 | tf_op jit(solution)/shard_map/ppermute | solution.py:249
  178.4 5.7 %collective-permute-done.35 = bf16[96,2048]{1,0:T(8,128)(2,1)S(1)} collective-permute-done((bf16[96,2048]{1,0:T(8,128)(2,1)S(1)}, bf16[96,2048]{1,0:T(8,128)(2,1)S(1)}, u32[]{:S(2)}, u32[]{:S(2)}) %collective-permute-start.35) | collective-permute-done | bytes 393248 | tf_op jit(solution)/shard_map/ppermute | solution.py:249
  184.1 5.7 %collective-permute-done.39 = bf16[96,2048]{1,0:T(8,128)(2,1)S(1)} collective-permute-done((bf16[96,2048]{1,0:T(8,128)(2,1)S(1)}, bf16[96,2048]{1,0:T(8,128)(2,1)S(1)}, u32[]{:S(2)}, u32[]{:S(2)}) %collective-permute-start.39) | collective-permute-done | bytes 393248 | tf_op jit(solution)/shard_map/ppermute | solution.py:249
  195.1 6.2 %collective-permute-done.38.refs_7_ = bf16[48,2048]{1,0:T(8,128)(2,1)S(1)} collective-permute-done((bf16[48,2048]{1,0:T(8,128)(2,1)S(1)}, bf16[48,2048]{1,0:T(8,128)(2,1)S(1)}, u32[]{:S(2)}, u32[]{:S(2)}) %collective-permute-start.38) | collective-permute-done | bytes 196640 | tf_op jit(solution)/shard_map/ppermute | solution.py:249
  204.0 2.3 %collective-permute-start.46 = (bf16[48,2048]{1,0:T(8,128)(2,1)S(1)}, bf16[48,2048]{1,0:T(8,128)(2,1)S(1)}, u32[]{:S(2)}, u32[]{:S(2)}) collective-permute-start(bf16[48,2048]{1,0:T(8,128)(2,1)S(1)} %get-tuple-element.192), channel_id=1, source_target_pairs={{0,6},{1,7},{2,4},{3,5},{4,2},{5,3},{6,0},{7,1},{8,14},{9,15},{10,... | collective-permute-start | bytes 589832 | tf_op jit(solution)/shard_map/ppermute | solution.py:249
  206.3 4.8 %collective-permute-done.44 = bf16[96,2048]{1,0:T(8,128)(2,1)S(1)} collective-permute-done((bf16[96,2048]{1,0:T(8,128)(2,1)S(1)}, bf16[96,2048]{1,0:T(8,128)(2,1)S(1)}, u32[]{:S(2)}, u32[]{:S(2)}) %collective-permute-start.44) | collective-permute-done | bytes 393248 | tf_op jit(solution)/shard_map/ppermute | solution.py:249
  (118 shorter events, 58.6 us)
Async XLA Ops:
  6.5 20.4 %collective-permute-start.5 = (bf16[96,2048]{1,0:T(8,128)(2,1)S(1)}, bf16[96,2048]{1,0:T(8,128)(2,1)S(1)}, u32[]{:S(2)}, u32[]{:S(2)}) collective-permute-start(bf16[96,2048]{1,0:T(8,128)(2,1)S(1)} %get-tuple-element.124), channel_id=1, source_target_pairs={{0,2},{1,3},{2,0},{3,1},{4,6},{5,7},{6,4},{7,5},{8,10},{9,11},{10,... | collective-permute-start | bytes 1179656 | tf_op jit(solution)/shard_map/ppermute | solution.py:249
  9.4 20.2 %collective-permute-start.2 = (bf16[96,2048]{1,0:T(8,128)(2,1)S(1)}, bf16[96,2048]{1,0:T(8,128)(2,1)S(1)}, u32[]{:S(2)}, u32[]{:S(2)}) collective-permute-start(bf16[96,2048]{1,0:T(8,128)(2,1)S(1)} %get-tuple-element.119), channel_id=1, source_target_pairs={{0,8},{1,9},{2,10},{3,11},{4,12},{5,13},{6,14},{7,15},{8,0},{9,1},... | collective-permute-start | bytes 1179656 | tf_op jit(solution)/shard_map/ppermute | solution.py:249
  12.0 17.6 %collective-permute-start.6 = (bf16[96,2048]{1,0:T(8,128)(2,1)S(1)}, bf16[96,2048]{1,0:T(8,128)(2,1)S(1)}, u32[]{:S(2)}, u32[]{:S(2)}) collective-permute-start(bf16[96,2048]{1,0:T(8,128)(2,1)S(1)} %get-tuple-element.125.refs_0_), channel_id=1, source_target_pairs={{0,1},{1,0},{2,3},{3,2},{4,5},{5,4},{6,7},{7,6},{8,9},{9,8},{10,11... | collective-permute-start | bytes 1179656 | tf_op jit(solution)/shard_map/ppermute | solution.py:249
  29.6 18.2 %collective-permute-start.8 = (bf16[96,2048]{1,0:T(8,128)(2,1)S(1)}, bf16[96,2048]{1,0:T(8,128)(2,1)S(1)}, u32[]{:S(2)}, u32[]{:S(2)}) collective-permute-start(bf16[96,2048]{1,0:T(8,128)(2,1)S(1)} %get-tuple-element.126), channel_id=1, source_target_pairs={{0,4},{1,5},{2,6},{3,7},{4,0},{5,1},{6,2},{7,3},{8,12},{9,13},{10,... | collective-permute-start | bytes 1179656 | tf_op jit(solution)/shard_map/ppermute | solution.py:249
  30.3 21.0 %collective-permute-start.3 = (bf16[96,2048]{1,0:T(8,128)(2,1)S(1)}, bf16[96,2048]{1,0:T(8,128)(2,1)S(1)}, u32[]{:S(2)}, u32[]{:S(2)}) collective-permute-start(bf16[96,2048]{1,0:T(8,128)(2,1)S(1)} %get-tuple-element.120), channel_id=1, source_target_pairs={{0,10},{1,11},{2,8},{3,9},{4,14},{5,15},{6,12},{7,13},{8,2},{9,3},... | collective-permute-start | bytes 1179656 | tf_op jit(solution)/shard_map/ppermute | solution.py:249
  33.6 17.7 %collective-permute-start.9 = (bf16[96,2048]{1,0:T(8,128)(2,1)S(1)}, bf16[96,2048]{1,0:T(8,128)(2,1)S(1)}, u32[]{:S(2)}, u32[]{:S(2)}) collective-permute-start(bf16[96,2048]{1,0:T(8,128)(2,1)S(1)} %collective-permute-done.5.refs_1_), channel_id=1, source_target_pairs={{0,1},{1,0},{2,3},{3,2},{4,5},{5,4},{6,7},{7,6},{8,9},{9,8},{10,11... | collective-permute-start | bytes 1179656 | tf_op jit(solution)/shard_map/ppermute | solution.py:249
  35.1 17.4 %collective-permute-start.10 = (bf16[96,2048]{1,0:T(8,128)(2,1)S(1)}, bf16[96,2048]{1,0:T(8,128)(2,1)S(1)}, u32[]{:S(2)}, u32[]{:S(2)}) collective-permute-start(bf16[96,2048]{1,0:T(8,128)(2,1)S(1)} %collective-permute-done.2.refs_4_), channel_id=1, source_target_pairs={{0,1},{1,0},{2,3},{3,2},{4,5},{5,4},{6,7},{7,6},{8,9},{9,8},{10,11... | collective-permute-start | bytes 1179656 | tf_op jit(solution)/shard_map/ppermute | solution.py:249
  52.5 21.4 %collective-permute-start.11 = (bf16[96,2048]{1,0:T(8,128)(2,1)S(1)}, bf16[96,2048]{1,0:T(8,128)(2,1)S(1)}, u32[]{:S(2)}, u32[]{:S(2)}) collective-permute-start(bf16[96,2048]{1,0:T(8,128)(2,1)S(1)} %get-tuple-element.129), channel_id=1, source_target_pairs={{0,6},{1,7},{2,4},{3,5},{4,2},{5,3},{6,0},{7,1},{8,14},{9,15},{10,... | collective-permute-start | bytes 1179656 | tf_op jit(solution)/shard_map/ppermute | solution.py:249
  53.8 17.6 %collective-permute-start.4 = (bf16[96,2048]{1,0:T(8,128)(2,1)S(1)}, bf16[96,2048]{1,0:T(8,128)(2,1)S(1)}, u32[]{:S(2)}, u32[]{:S(2)}) collective-permute-start(bf16[96,2048]{1,0:T(8,128)(2,1)S(1)} %get-tuple-element.121), channel_id=1, source_target_pairs={{0,12},{1,13},{2,14},{3,15},{4,8},{5,9},{6,10},{7,11},{8,4},{9,5},... | collective-permute-start | bytes 1179656 | tf_op jit(solution)/shard_map/ppermute | solution.py:249
  54.5 19.4 %collective-permute-start.12 = (bf16[96,2048]{1,0:T(8,128)(2,1)S(1)}, bf16[96,2048]{1,0:T(8,128)(2,1)S(1)}, u32[]{:S(2)}, u32[]{:S(2)}) collective-permute-start(bf16[96,2048]{1,0:T(8,128)(2,1)S(1)} %collective-permute-done.8.refs_2_), channel_id=1, source_target_pairs={{0,1},{1,0},{2,3},{3,2},{4,5},{5,4},{6,7},{7,6},{8,9},{9,8},{10,11... | collective-permute-start | bytes 1179656 | tf_op jit(solution)/shard_map/ppermute | solution.py:249
  56.0 17.9 %collective-permute-start.13 = (bf16[96,2048]{1,0:T(8,128)(2,1)S(1)}, bf16[96,2048]{1,0:T(8,128)(2,1)S(1)}, u32[]{:S(2)}, u32[]{:S(2)}) collective-permute-start(bf16[96,2048]{1,0:T(8,128)(2,1)S(1)} %collective-permute-done.3.refs_5_), channel_id=1, source_target_pairs={{0,1},{1,0},{2,3},{3,2},{4,5},{5,4},{6,7},{7,6},{8,9},{9,8},{10,11... | collective-permute-start | bytes 1179656 | tf_op jit(solution)/shard_map/ppermute | solution.py:249
  71.4 12.3 %collective-permute-start.15 = (bf16[96,2048]{1,0:T(8,128)(2,1)S(1)}, bf16[96,2048]{1,0:T(8,128)(2,1)S(1)}, u32[]{:S(2)}, u32[]{:S(2)}) collective-permute-start(bf16[96,2048]{1,0:T(8,128)(2,1)S(1)} %get-tuple-element.135), channel_id=1, source_target_pairs={{0,14},{1,15},{2,12},{3,13},{4,10},{5,11},{6,8},{7,9},{8,6},{9,7},... | collective-permute-start | bytes 1179656 | tf_op jit(solution)/shard_map/ppermute | solution.py:249
  73.9 17.2 %collective-permute-start.16 = (bf16[96,2048]{1,0:T(8,128)(2,1)S(1)}, bf16[96,2048]{1,0:T(8,128)(2,1)S(1)}, u32[]{:S(2)}, u32[]{:S(2)}) collective-permute-start(bf16[96,2048]{1,0:T(8,128)(2,1)S(1)} %collective-permute-done.11.refs_3_), channel_id=1, source_target_pairs={{0,1},{1,0},{2,3},{3,2},{4,5},{5,4},{6,7},{7,6},{8,9},{9,8},{10,11... | collective-permute-start | bytes 1179656 | tf_op jit(solution)/shard_map/ppermute | solution.py:249
  75.5 15.6 %collective-permute-start.17 = (bf16[96,2048]{1,0:T(8,128)(2,1)S(1)}, bf16[96,2048]{1,0:T(8,128)(2,1)S(1)}, u32[]{:S(2)}, u32[]{:S(2)}) collective-permute-start(bf16[96,2048]{1,0:T(8,128)(2,1)S(1)} %collective-permute-done.4.refs_6_), channel_id=1, source_target_pairs={{0,1},{1,0},{2,3},{3,2},{4,5},{5,4},{6,7},{7,6},{8,9},{9,8},{10,11... | collective-permute-start | bytes 1179656 | tf_op jit(solution)/shard_map/ppermute | solution.py:249
  76.0 15.1 %collective-permute-start.14 = (bf16[48,2048]{1,0:T(8,128)(2,1)S(1)}, bf16[48,2048]{1,0:T(8,128)(2,1)S(1)}, u32[]{:S(2)}, u32[]{:S(2)}) collective-permute-start(bf16[48,2048]{1,0:T(8,128)(2,1)S(1)} %get-tuple-element.132), channel_id=1, source_target_pairs={{0,2},{1,3},{2,0},{3,1},{4,6},{5,7},{6,4},{7,5},{8,10},{9,11},{10,... | collective-permute-start | bytes 589832 | tf_op jit(solution)/shard_map/ppermute | solution.py:249
  83.7 15.8 %collective-permute-start.20 = (bf16[48,2048]{1,0:T(8,128)(2,1)S(1)}, bf16[48,2048]{1,0:T(8,128)(2,1)S(1)}, u32[]{:S(2)}, u32[]{:S(2)}) collective-permute-start(bf16[48,2048]{1,0:T(8,128)(2,1)S(1)} %get-tuple-element.142), channel_id=1, source_target_pairs={{0,8},{1,9},{2,10},{3,11},{4,12},{5,13},{6,14},{7,15},{8,0},{9,1},... | collective-permute-start | bytes 589832 | tf_op jit(solution)/shard_map/ppermute | solution.py:249
  99.9 13.2 %collective-permute-start.23 = (bf16[144,2048]{1,0:T(8,128)(2,1)S(1)}, bf16[144,2048]{1,0:T(8,128)(2,1)S(1)}, u32[]{:S(2)}, u32[]{:S(2)}) collective-permute-start(bf16[144,2048]{1,0:T(8,128)(2,1)S(1)} %pad_maximum_fusion.1), channel_id=1, source_target_pairs={{0,1},{1,0},{2,3},{3,2},{4,5},{5,4},{6,7},{7,6},{8,9},{9,8},{10,11... | collective-permute-start | bytes 1769480 | tf_op jit(solution)/shard_map/ppermute | solution.py:249
  117.0 12.0 %collective-permute-start.26 = (bf16[96,2048]{1,0:T(8,128)(2,1)S(1)}, bf16[96,2048]{1,0:T(8,128)(2,1)S(1)}, u32[]{:S(2)}, u32[]{:S(2)}) collective-permute-start(bf16[96,2048]{1,0:T(8,128)(2,1)S(1)} %get-tuple-element.156), channel_id=1, source_target_pairs={{0,1},{1,0},{2,3},{3,2},{4,5},{5,4},{6,7},{7,6},{8,9},{9,8},{10,11... | collective-permute-start | bytes 1179656 | tf_op jit(solution)/shard_map/ppermute | solution.py:249
  118.5 16.2 %collective-permute-start.27 = (bf16[96,2048]{1,0:T(8,128)(2,1)S(1)}, bf16[96,2048]{1,0:T(8,128)(2,1)S(1)}, u32[]{:S(2)}, u32[]{:S(2)}) collective-permute-start(bf16[96,2048]{1,0:T(8,128)(2,1)S(1)} %get-tuple-element.158), channel_id=1, source_target_pairs={{0,1},{1,0},{2,3},{3,2},{4,5},{5,4},{6,7},{7,6},{8,9},{9,8},{10,11... | collective-permute-start | bytes 1179656 | tf_op jit(solution)/shard_map/ppermute | solution.py:249
  134.7 16.5 %collective-permute-start.28 = (bf16[192,2048]{1,0:T(8,128)(2,1)S(1)}, bf16[192,2048]{1,0:T(8,128)(2,1)S(1)}, u32[]{:S(2)}, u32[]{:S(2)}) collective-permute-start(bf16[192,2048]{1,0:T(8,128)(2,1)S(1)} %pad_maximum_fusion), channel_id=1, source_target_pairs={{0,1},{1,0},{2,3},{3,2},{4,5},{5,4},{6,7},{7,6},{8,9},{9,8},{10,11... | collective-permute-start | bytes 2359304 | tf_op jit(solution)/shard_map/ppermute | solution.py:249
  136.3 13.0 %collective-permute-start.29 = (bf16[48,2048]{1,0:T(8,128)(2,1)S(1)}, bf16[48,2048]{1,0:T(8,128)(2,1)S(1)}, u32[]{:S(2)}, u32[]{:S(2)}) collective-permute-start(bf16[48,2048]{1,0:T(8,128)(2,1)S(1)} %get-tuple-element.165), channel_id=1, source_target_pairs={{0,8},{1,9},{2,10},{3,11},{4,12},{5,13},{6,14},{7,15},{8,0},{9,1},... | collective-permute-start | bytes 589832 | tf_op jit(solution)/shard_map/ppermute | solution.py:249
  137.6 13.6 %collective-permute-start.30 = (bf16[48,2048]{1,0:T(8,128)(2,1)S(1)}, bf16[48,2048]{1,0:T(8,128)(2,1)S(1)}, u32[]{:S(2)}, u32[]{:S(2)}) collective-permute-start(bf16[48,2048]{1,0:T(8,128)(2,1)S(1)} %get-tuple-element.166), channel_id=1, source_target_pairs={{0,10},{1,11},{2,8},{3,9},{4,14},{5,15},{6,12},{7,13},{8,2},{9,3},... | collective-permute-start | bytes 589832 | tf_op jit(solution)/shard_map/ppermute | solution.py:249
  151.2 16.5 %collective-permute-start.31 = (bf16[96,2048]{1,0:T(8,128)(2,1)S(1)}, bf16[96,2048]{1,0:T(8,128)(2,1)S(1)}, u32[]{:S(2)}, u32[]{:S(2)}) collective-permute-start(bf16[96,2048]{1,0:T(8,128)(2,1)S(1)} %get-tuple-element.167), channel_id=1, source_target_pairs={{0,1},{1,0},{2,3},{3,2},{4,5},{5,4},{6,7},{7,6},{8,9},{9,8},{10,11... | collective-permute-start | bytes 1179656 | tf_op jit(solution)/shard_map/ppermute | solution.py:249
  152.5 15.2 %collective-permute-start.32 = (bf16[48,2048]{1,0:T(8,128)(2,1)S(1)}, bf16[48,2048]{1,0:T(8,128)(2,1)S(1)}, u32[]{:S(2)}, u32[]{:S(2)}) collective-permute-start(bf16[48,2048]{1,0:T(8,128)(2,1)S(1)} %get-tuple-element.169), channel_id=1, source_target_pairs={{0,12},{1,13},{2,14},{3,15},{4,8},{5,9},{6,10},{7,11},{8,4},{9,5},... | collective-permute-start | bytes 589832 | tf_op jit(solution)/shard_map/ppermute | solution.py:249
  155.3 12.4 %collective-permute-start.33 = (bf16[48,2048]{1,0:T(8,128)(2,1)S(1)}, bf16[48,2048]{1,0:T(8,128)(2,1)S(1)}, u32[]{:S(2)}, u32[]{:S(2)}) collective-permute-start(bf16[48,2048]{1,0:T(8,128)(2,1)S(1)} %get-tuple-element.170), channel_id=1, source_target_pairs={{0,14},{1,15},{2,12},{3,13},{4,10},{5,11},{6,8},{7,9},{8,6},{9,7},... | collective-permute-start | bytes 589832 | tf_op jit(solution)/shard_map/ppermute | solution.py:249
  172.0 12.1 %collective-permute-start.35 = (bf16[96,2048]{1,0:T(8,128)(2,1)S(1)}, bf16[96,2048]{1,0:T(8,128)(2,1)S(1)}, u32[]{:S(2)}, u32[]{:S(2)}) collective-permute-start(bf16[96,2048]{1,0:T(8,128)(2,1)S(1)} %get-tuple-element.173), channel_id=1, source_target_pairs={{0,1},{1,0},{2,3},{3,2},{4,5},{5,4},{6,7},{7,6},{8,9},{9,8},{10,11... | collective-permute-start | bytes 1179656 | tf_op jit(solution)/shard_map/ppermute | solution.py:249
  173.3 17.7 %collective-permute-start.36 = (bf16[48,2048]{1,0:T(8,128)(2,1)S(1)}, bf16[48,2048]{1,0:T(8,128)(2,1)S(1)}, u32[]{:S(2)}, u32[]{:S(2)}) collective-permute-start(bf16[48,2048]{1,0:T(8,128)(2,1)S(1)} %get-tuple-element.175), channel_id=1, source_target_pairs={{0,8},{1,9},{2,10},{3,11},{4,12},{5,13},{6,14},{7,15},{8,0},{9,1},... | collective-permute-start | bytes 589832 | tf_op jit(solution)/shard_map/ppermute | solution.py:249
  173.4 17.7 %collective-permute-start.37 = (bf16[48,2048]{1,0:T(8,128)(2,1)S(1)}, bf16[48,2048]{1,0:T(8,128)(2,1)S(1)}, u32[]{:S(2)}, u32[]{:S(2)}) collective-permute-start(bf16[48,2048]{1,0:T(8,128)(2,1)S(1)} %get-tuple-element.176), channel_id=1, source_target_pairs={{0,10},{1,11},{2,8},{3,9},{4,14},{5,15},{6,12},{7,13},{8,2},{9,3},... | collective-permute-start | bytes 589832 | tf_op jit(solution)/shard_map/ppermute | solution.py:249
  176.0 13.8 %collective-permute-start.39 = (bf16[96,2048]{1,0:T(8,128)(2,1)S(1)}, bf16[96,2048]{1,0:T(8,128)(2,1)S(1)}, u32[]{:S(2)}, u32[]{:S(2)}) collective-permute-start(bf16[96,2048]{1,0:T(8,128)(2,1)S(1)} %pad_maximum_fusion.3), channel_id=1, source_target_pairs={{0,1},{1,0},{2,3},{3,2},{4,5},{5,4},{6,7},{7,6},{8,9},{9,8},{10,11... | collective-permute-start | bytes 1179656 | tf_op jit(solution)/shard_map/ppermute | solution.py:249
  177.2 13.9 %collective-permute-start.41 = (bf16[48,2048]{1,0:T(8,128)(2,1)S(1)}, bf16[48,2048]{1,0:T(8,128)(2,1)S(1)}, u32[]{:S(2)}, u32[]{:S(2)}) collective-permute-start(bf16[48,2048]{1,0:T(8,128)(2,1)S(1)} %get-tuple-element.186), channel_id=1, source_target_pairs={{0,6},{1,7},{2,4},{3,5},{4,2},{5,3},{6,0},{7,1},{8,14},{9,15},{10,... | collective-permute-start | bytes 589832 | tf_op jit(solution)/shard_map/ppermute | solution.py:249
  189.7 13.4 %collective-permute-start.40 = (bf16[96,2048]{1,0:T(8,128)(2,1)S(1)}, bf16[96,2048]{1,0:T(8,128)(2,1)S(1)}, u32[]{:S(2)}, u32[]{:S(2)}) collective-permute-start(bf16[96,2048]{1,0:T(8,128)(2,1)S(1)} %get-tuple-element.182), channel_id=1, source_target_pairs={{0,1},{1,0},{2,3},{3,2},{4,5},{5,4},{6,7},{7,6},{8,9},{9,8},{10,11... | collective-permute-start | bytes 1179656 | tf_op jit(solution)/shard_map/ppermute | solution.py:249
  191.1 12.0 %collective-permute-start.42 = (bf16[96,2048]{1,0:T(8,128)(2,1)S(1)}, bf16[96,2048]{1,0:T(8,128)(2,1)S(1)}, u32[]{:S(2)}, u32[]{:S(2)}) collective-permute-start(bf16[96,2048]{1,0:T(8,128)(2,1)S(1)} %pad_maximum_fusion.4), channel_id=1, source_target_pairs={{0,2},{1,3},{2,0},{3,1},{4,6},{5,7},{6,4},{7,5},{8,10},{9,11},{10,... | collective-permute-start | bytes 1179656 | tf_op jit(solution)/shard_map/ppermute | solution.py:249
  (29 other events, 207.0 us)

commit v6 on v5

--- a/solution.py
+++ b/solution.py
@@ -388,8 +388,9 @@
     give_back("r", back_own, 2)
     meet(("o", 6),)
     give_back("o", out_own, 7)
+    meet(("ox", 1),)
+    both_start(0)
     meet(("o", 6), ("ox", 1), ("both", 1), ("r", 2))
-    both_start(0)
     give_back("o", out_own, 2)
     give_back("o", out_own, 3)
     give_both(0)

time: 218 us -> 218 us (level)
  no operation moved by 1% of the time
where the time goes in v6:
time: 218 us; the launch traced here: 217 us
  waiting for transfers between devices  102 us (47%)
  starting transfers between devices  71.2 us (33%)
  Pallas kernels  27.8 us (13%)
  matrix products  10.3 us (5%)
  local copies, waits for them, and re-layouts  3.88 us (2%)
    ppermute x46, waiting for transfers between devices, to_xor(): lax.ppermute(array, 'expert', [(i, i ^ mask) for i in range(devices)])  101 us
    ppermute x46, starting transfers between devices, to_xor(): lax.ppermute(array, 'expert', [(i, i ^ mask) for i in range(devices)])  70.6 us
    pallas_call x2, Pallas kernels, backward_half(): pl.pallas_call(functools.partial(backward_kernel, n, len(outs)), out_shap...  13.8 us
    dot_general x6, matrix products, weight_term(): lax.dot_general(left, kept[b], outer, preferred_element_type=jnp.float32)  10.3 us
    pallas_call x2, Pallas kernels, forward_half(): pl.pallas_call(functools.partial(forward_kernel, n, len(outs), order or r...  9.06 us
  transfers between devices with their start and end apart: 48, of which 24 were waited for; matrix products, arithmetic and copies ran while one was open for 5% of the time, Pallas kernels for 12%

profile of v6, /device:TPU:0, one launch (start us, length us, event | category | flops | bytes accessed | tf_op | source)
XLA Modules:
  0.0 217.4 jit_solution(1715142065352369167)
XLA Ops:
  6.5 3.0 %collective-permute-start.5 = (bf16[96,2048]{1,0:T(8,128)(2,1)S(1)}, bf16[96,2048]{1,0:T(8,128)(2,1)S(1)}, u32[]{:S(2)}, u32[]{:S(2)}) collective-permute-start(bf16[96,2048]{1,0:T(8,128)(2,1)S(1)} %get-tuple-element.124), channel_id=1, source_target_pairs={{0,2},{1,3},{2,0},{3,1},{4,6},{5,7},{6,4},{7,5},{8,10},{9,11},{10,... | collective-permute-start | bytes 1179656 | tf_op jit(solution)/shard_map/ppermute | solution.py:249
  9.4 2.6 %collective-permute-start.2 = (bf16[96,2048]{1,0:T(8,128)(2,1)S(1)}, bf16[96,2048]{1,0:T(8,128)(2,1)S(1)}, u32[]{:S(2)}, u32[]{:S(2)}) collective-permute-start(bf16[96,2048]{1,0:T(8,128)(2,1)S(1)} %get-tuple-element.119), channel_id=1, source_target_pairs={{0,8},{1,9},{2,10},{3,11},{4,12},{5,13},{6,14},{7,15},{8,0},{9,1},... | collective-permute-start | bytes 1179656 | tf_op jit(solution)/shard_map/ppermute | solution.py:249
  15.5 11.3 %collective-permute-done.7.refs_0_ = bf16[48,2048]{1,0:T(8,128)(2,1)S(1)} collective-permute-done((bf16[48,2048]{1,0:T(8,128)(2,1)S(1)}, bf16[48,2048]{1,0:T(8,128)(2,1)S(1)}, u32[]{:S(2)}, u32[]{:S(2)}) %collective-permute-start.7) | collective-permute-done | bytes 196640 | tf_op jit(solution)/shard_map/ppermute | solution.py:249
  26.8 2.8 %collective-permute-done.2.refs_4_ = bf16[96,2048]{1,0:T(8,128)(2,1)S(1)} collective-permute-done((bf16[96,2048]{1,0:T(8,128)(2,1)S(1)}, bf16[96,2048]{1,0:T(8,128)(2,1)S(1)}, u32[]{:S(2)}, u32[]{:S(2)}) %collective-permute-start.2) | collective-permute-done | bytes 393248 | tf_op jit(solution)/shard_map/ppermute | solution.py:249
  30.3 3.3 %collective-permute-start.3 = (bf16[96,2048]{1,0:T(8,128)(2,1)S(1)}, bf16[96,2048]{1,0:T(8,128)(2,1)S(1)}, u32[]{:S(2)}, u32[]{:S(2)}) collective-permute-start(bf16[96,2048]{1,0:T(8,128)(2,1)S(1)} %get-tuple-element.120), channel_id=1, source_target_pairs={{0,10},{1,11},{2,8},{3,9},{4,14},{5,15},{6,12},{7,13},{8,2},{9,3},... | collective-permute-start | bytes 1179656 | tf_op jit(solution)/shard_map/ppermute | solution.py:249
  35.6 12.2 %collective-permute-done.8.refs_2_ = bf16[96,2048]{1,0:T(8,128)(2,1)S(1)} collective-permute-done((bf16[96,2048]{1,0:T(8,128)(2,1)S(1)}, bf16[96,2048]{1,0:T(8,128)(2,1)S(1)}, u32[]{:S(2)}, u32[]{:S(2)}) %collective-permute-start.8) | collective-permute-done | bytes 393248 | tf_op jit(solution)/shard_map/ppermute | solution.py:249
  47.8 3.5 %collective-permute-done.3.refs_5_ = bf16[96,2048]{1,0:T(8,128)(2,1)S(1)} collective-permute-done((bf16[96,2048]{1,0:T(8,128)(2,1)S(1)}, bf16[96,2048]{1,0:T(8,128)(2,1)S(1)}, u32[]{:S(2)}, u32[]{:S(2)}) %collective-permute-start.3) | collective-permute-done | bytes 393248 | tf_op jit(solution)/shard_map/ppermute | solution.py:249
  56.5 14.9 %collective-permute-done.4.refs_6_ = bf16[96,2048]{1,0:T(8,128)(2,1)S(1)} collective-permute-done((bf16[96,2048]{1,0:T(8,128)(2,1)S(1)}, bf16[96,2048]{1,0:T(8,128)(2,1)S(1)}, u32[]{:S(2)}, u32[]{:S(2)}) %collective-permute-start.4) | collective-permute-done | bytes 393248 | tf_op jit(solution)/shard_map/ppermute | solution.py:249
  71.4 2.5 %collective-permute-start.15 = (bf16[96,2048]{1,0:T(8,128)(2,1)S(1)}, bf16[96,2048]{1,0:T(8,128)(2,1)S(1)}, u32[]{:S(2)}, u32[]{:S(2)}) collective-permute-start(bf16[96,2048]{1,0:T(8,128)(2,1)S(1)} %get-tuple-element.135), channel_id=1, source_target_pairs={{0,14},{1,15},{2,12},{3,13},{4,10},{5,11},{6,8},{7,9},{8,6},{9,7},... | collective-permute-start | bytes 1179656 | tf_op jit(solution)/shard_map/ppermute | solution.py:249
  77.5 6.2 %collective-permute-done.15.refs_7_ = bf16[96,2048]{1,0:T(8,128)(2,1)S(1)} collective-permute-done((bf16[96,2048]{1,0:T(8,128)(2,1)S(1)}, bf16[96,2048]{1,0:T(8,128)(2,1)S(1)}, u32[]{:S(2)}, u32[]{:S(2)}) %collective-permute-start.15) | collective-permute-done | bytes 393248 | tf_op jit(solution)/shard_map/ppermute | solution.py:249
  83.7 7.3 %collective-permute-start.20 = (bf16[48,2048]{1,0:T(8,128)(2,1)S(1)}, bf16[48,2048]{1,0:T(8,128)(2,1)S(1)}, u32[]{:S(2)}, u32[]{:S(2)}) collective-permute-start(bf16[48,2048]{1,0:T(8,128)(2,1)S(1)} %get-tuple-element.142), channel_id=1, source_target_pairs={{0,8},{1,9},{2,10},{3,11},{4,12},{5,13},{6,14},{7,15},{8,0},{9,1},... | collective-permute-start | bytes 589832 | tf_op jit(solution)/shard_map/ppermute | solution.py:249
  92.7 6.8 %backward_half.2 = (bf16[48,2048]{1,0:T(8,128)(2,1)S(1)}, bf16[48,2048]{1,0:T(8,128)(2,1)S(1)}, bf16[96,2048]{1,0:T(8,128)(2,1)S(1)}, bf16[96,2048]{1,0:T(8,128)...) custom-call(bf16[96,2048]{1,0:T(8,128)(2,1)S(1)} %get-tuple-element., ...), custom_call_target="tpu_custom_call" | custom-call | flops 3019898880 | bytes 12582912 | tf_op jit(solution)/shard_map/backward_half/pallas_call | solution.py:203
  101.4 3.7 %collective-permute-start.22 = (bf16[48,2048]{1,0:T(8,128)(2,1)S(1)}, bf16[48,2048]{1,0:T(8,128)(2,1)S(1)}, u32[]{:S(2)}, u32[]{:S(2)}) collective-permute-start(bf16[48,2048]{1,0:T(8,128)(2,1)S(1)} %get-tuple-element.146), channel_id=1, source_target_pairs={{0,10},{1,11},{2,8},{3,9},{4,14},{5,15},{6,12},{7,13},{8,2},{9,3},... | collective-permute-start | bytes 589832 | tf_op jit(solution)/shard_map/ppermute | solution.py:249
  105.1 6.9 %backward_half.3 = (bf16[48,2048]{1,0:T(8,128)(2,1)S(1)}, bf16[48,2048]{1,0:T(8,128)(2,1)S(1)}, bf16[96,2048]{1,0:T(8,128)(2,1)S(1)}, bf16[96,2048]{1,0:T(8,128)...) custom-call(bf16[96,2048]{1,0:T(8,128)(2,1)S(1)} %collective-permute, ...), custom_call_target="tpu_custom_call" | custom-call | flops 3019898880 | bytes 12582912 | tf_op jit(solution)/shard_map/backward_half/pallas_call | solution.py:203
  113.2 3.1 %collective-permute-start.25 = (bf16[48,2048]{1,0:T(8,128)(2,1)S(1)}, bf16[48,2048]{1,0:T(8,128)(2,1)S(1)}, u32[]{:S(2)}, u32[]{:S(2)}) collective-permute-start(bf16[48,2048]{1,0:T(8,128)(2,1)S(1)} %get-tuple-element.152), channel_id=1, source_target_pairs={{0,14},{1,15},{2,12},{3,13},{4,10},{5,11},{6,8},{7,9},{8,6},{9,7},... | collective-permute-start | bytes 589832 | tf_op jit(solution)/shard_map/ppermute | solution.py:249
  119.0 3.2 %collective-permute-done.25.refs_7_ = bf16[48,2048]{1,0:T(8,128)(2,1)S(1)} collective-permute-done((bf16[48,2048]{1,0:T(8,128)(2,1)S(1)}, bf16[48,2048]{1,0:T(8,128)(2,1)S(1)}, u32[]{:S(2)}, u32[]{:S(2)}) %collective-permute-start.25) | collective-permute-done | bytes 196640 | tf_op jit(solution)/shard_map/ppermute | solution.py:249
  124.3 4.5 %forward_half.2 = (bf16[48,2048]{1,0:T(8,128)(2,1)S(1)}, bf16[48,2048]{1,0:T(8,128)(2,1)S(1)}, bf16[96,2048]{1,0:T(8,128)(2,1)S(1)}, bf16[96,2048]{1,0:T(8,128)(2,1)S(1)}, bf16[96,2048]{1,0:T(8,128)(2,1)S(1)}) custom-call(bf16[48,2048]{1,0:T(8,128)(2,1)S(1)} %get-tuple-element.107.refs_0_, bf16[48,2048]{1,0:T(8,128)(2,1)S(1)} %collective-permute-done.14.refs_1_, ...), custom_call_target="tpu_custom_call" | custom-call | flops 1811939328 | bytes 7864320 | tf_op jit(solution)/shard_map/forward_half/pallas_call | solution.py:153
  129.0 5.7 %collective-permute-done.27 = bf16[96,2048]{1,0:T(8,128)(2,1)S(1)} collective-permute-done((bf16[96,2048]{1,0:T(8,128)(2,1)S(1)}, bf16[96,2048]{1,0:T(8,128)(2,1)S(1)}, u32[]{:S(2)}, u32[]{:S(2)}) %collective-permute-start.27) | collective-permute-done | bytes 393248 | tf_op jit(solution)/shard_map/ppermute | solution.py:249
  137.6 2.6 %collective-permute-start.30 = (bf16[48,2048]{1,0:T(8,128)(2,1)S(1)}, bf16[48,2048]{1,0:T(8,128)(2,1)S(1)}, u32[]{:S(2)}, u32[]{:S(2)}) collective-permute-start(bf16[48,2048]{1,0:T(8,128)(2,1)S(1)} %get-tuple-element.166), channel_id=1, source_target_pairs={{0,10},{1,11},{2,8},{3,9},{4,14},{5,15},{6,12},{7,13},{8,2},{9,3},... | collective-permute-start | bytes 589832 | tf_op jit(solution)/shard_map/ppermute | solution.py:249
  143.9 5.4 %collective-permute-done.29.refs_4_ = bf16[48,2048]{1,0:T(8,128)(2,1)S(1)} collective-permute-done((bf16[48,2048]{1,0:T(8,128)(2,1)S(1)}, bf16[48,2048]{1,0:T(8,128)(2,1)S(1)}, u32[]{:S(2)}, u32[]{:S(2)}) %collective-permute-start.29) | collective-permute-done | bytes 196640 | tf_op jit(solution)/shard_map/ppermute | solution.py:249
  152.5 2.8 %collective-permute-start.32 = (bf16[48,2048]{1,0:T(8,128)(2,1)S(1)}, bf16[48,2048]{1,0:T(8,128)(2,1)S(1)}, u32[]{:S(2)}, u32[]{:S(2)}) collective-permute-start(bf16[48,2048]{1,0:T(8,128)(2,1)S(1)} %get-tuple-element.169), channel_id=1, source_target_pairs={{0,12},{1,13},{2,14},{3,15},{4,8},{5,9},{6,10},{7,11},{8,4},{9,5},... | collective-permute-start | bytes 589832 | tf_op jit(solution)/shard_map/ppermute | solution.py:249
  155.3 2.7 %collective-permute-start.33 = (bf16[48,2048]{1,0:T(8,128)(2,1)S(1)}, bf16[48,2048]{1,0:T(8,128)(2,1)S(1)}, u32[]{:S(2)}, u32[]{:S(2)}) collective-permute-start(bf16[48,2048]{1,0:T(8,128)(2,1)S(1)} %get-tuple-element.170), channel_id=1, source_target_pairs={{0,14},{1,15},{2,12},{3,13},{4,10},{5,11},{6,8},{7,9},{8,6},{9,7},... | collective-permute-start | bytes 589832 | tf_op jit(solution)/shard_map/ppermute | solution.py:249
  158.0 4.5 %forward_half.3 = (bf16[48,2048]{1,0:T(8,128)(2,1)S(1)}, bf16[48,2048]{1,0:T(8,128)(2,1)S(1)}, bf16[96,2048]{1,0:T(8,128)(2,1)S(1)}, bf16[96,2048]{1,0:T(8,128)(2,1)S(1)}, bf16[96,2048]{1,0:T(8,128)(2,1)S(1)}) custom-call(bf16[48,2048]{1,0:T(8,128)(2,1)S(1)} %collective-permute-done.7.refs_0_, bf16[144,2048]{1,0:T(8,128)(2,1)S(1)} %collective-permute-done.23.refs_1_, ...), custom_call_target="tpu_custom_call" | custom-call | flops 1811939328 | bytes 7864320 | tf_op jit(solution)/shard_map/forward_half/pallas_call | solution.py:153
  165.3 2.4 %fusion.1 = bf16[1,1,2048,384]{3,2,1,0:T(8,128)(2,1)} fusion(f32[2048,384]{1,0:T(8,128)S(1)} %fusion.5, bf16[384,2048]{1,0:T(8,128)(2,1)S(1)} %copy-done.10, bf16[384,384]{1,0:T(8,128)(2,1)S(1)} %get-tuple-element.200), kind=kOutput, calls=%fused_computation.4 | convolution fusion | flops 605552640 | bytes 6586368 | tf_op jit(solution)/shard_map/dot_general | solution.py:404
  167.8 4.3 %collective-permute-done.34 = bf16[96,2048]{1,0:T(8,128)(2,1)S(1)} collective-permute-done((bf16[96,2048]{1,0:T(8,128)(2,1)S(1)}, bf16[96,2048]{1,0:T(8,128)(2,1)S(1)}, u32[]{:S(2)}, u32[]{:S(2)}) %collective-permute-start.34) | collective-permute-done | bytes 393248 | tf_op jit(solution)/shard_map/ppermute | solution.py:249
  174.2 2.9 %collective-permute-start.40 = (bf16[48,2048]{1,0:T(8,128)(2,1)S(1)}, bf16[48,2048]{1,0:T(8,128)(2,1)S(1)}, u32[]{:S(2)}, u32[]{:S(2)}) collective-permute-start(bf16[48,2048]{1,0:T(8,128)(2,1)S(1)} %get-tuple-element.183), channel_id=1, source_target_pairs={{0,10},{1,11},{2,8},{3,9},{4,14},{5,15},{6,12},{7,13},{8,2},{9,3},... | collective-permute-start | bytes 589832 | tf_op jit(solution)/shard_map/ppermute | solution.py:249
  181.0 3.1 %collective-permute-done.35 = bf16[96,2048]{1,0:T(8,128)(2,1)S(1)} collective-permute-done((bf16[96,2048]{1,0:T(8,128)(2,1)S(1)}, bf16[96,2048]{1,0:T(8,128)(2,1)S(1)}, u32[]{:S(2)}, u32[]{:S(2)}) %collective-permute-start.35) | collective-permute-done | bytes 393248 | tf_op jit(solution)/shard_map/ppermute | solution.py:249
  184.1 5.7 %collective-permute-done.36 = bf16[96,2048]{1,0:T(8,128)(2,1)S(1)} collective-permute-done((bf16[96,2048]{1,0:T(8,128)(2,1)S(1)}, bf16[96,2048]{1,0:T(8,128)(2,1)S(1)}, u32[]{:S(2)}, u32[]{:S(2)}) %collective-permute-start.36) | collective-permute-done | bytes 393248 | tf_op jit(solution)/shard_map/ppermute | solution.py:249
  192.9 7.8 %collective-permute-done.43.refs_7_ = bf16[48,2048]{1,0:T(8,128)(2,1)S(1)} collective-permute-done((bf16[48,2048]{1,0:T(8,128)(2,1)S(1)}, bf16[48,2048]{1,0:T(8,128)(2,1)S(1)}, u32[]{:S(2)}, u32[]{:S(2)}) %collective-permute-start.43) | collective-permute-done | bytes 196640 | tf_op jit(solution)/shard_map/ppermute | solution.py:249
  203.8 2.4 %collective-permute-start.46 = (bf16[48,2048]{1,0:T(8,128)(2,1)S(1)}, bf16[48,2048]{1,0:T(8,128)(2,1)S(1)}, u32[]{:S(2)}, u32[]{:S(2)}) collective-permute-start(bf16[48,2048]{1,0:T(8,128)(2,1)S(1)} %get-tuple-element.192), channel_id=1, source_target_pairs={{0,6},{1,7},{2,4},{3,5},{4,2},{5,3},{6,0},{7,1},{8,14},{9,15},{10,... | collective-permute-start | bytes 589832 | tf_op jit(solution)/shard_map/ppermute | solution.py:249
  206.2 3.1 %collective-permute-done.38 = bf16[96,2048]{1,0:T(8,128)(2,1)S(1)} collective-permute-done((bf16[96,2048]{1,0:T(8,128)(2,1)S(1)}, bf16[96,2048]{1,0:T(8,128)(2,1)S(1)}, u32[]{:S(2)}, u32[]{:S(2)}) %collective-permute-start.38) | collective-permute-done | bytes 393248 | tf_op jit(solution)/shard_map/ppermute | solution.py:249
  212.6 3.0 %collective-permute-done.46.refs_4_ = bf16[48,2048]{1,0:T(8,128)(2,1)S(1)} collective-permute-done((bf16[48,2048]{1,0:T(8,128)(2,1)S(1)}, bf16[48,2048]{1,0:T(8,128)(2,1)S(1)}, u32[]{:S(2)}, u32[]{:S(2)}) %collective-permute-start.46) | collective-permute-done | bytes 196640 | tf_op jit(solution)/shard_map/ppermute | solution.py:249
  (118 shorter events, 60.3 us)
Async XLA Ops:
  6.5 20.4 %collective-permute-start.5 = (bf16[96,2048]{1,0:T(8,128)(2,1)S(1)}, bf16[96,2048]{1,0:T(8,128)(2,1)S(1)}, u32[]{:S(2)}, u32[]{:S(2)}) collective-permute-start(bf16[96,2048]{1,0:T(8,128)(2,1)S(1)} %get-tuple-element.124), channel_id=1, source_target_pairs={{0,2},{1,3},{2,0},{3,1},{4,6},{5,7},{6,4},{7,5},{8,10},{9,11},{10,... | collective-permute-start | bytes 1179656 | tf_op jit(solution)/shard_map/ppermute | solution.py:249
  9.4 20.2 %collective-permute-start.2 = (bf16[96,2048]{1,0:T(8,128)(2,1)S(1)}, bf16[96,2048]{1,0:T(8,128)(2,1)S(1)}, u32[]{:S(2)}, u32[]{:S(2)}) collective-permute-start(bf16[96,2048]{1,0:T(8,128)(2,1)S(1)} %get-tuple-element.119), channel_id=1, source_target_pairs={{0,8},{1,9},{2,10},{3,11},{4,12},{5,13},{6,14},{7,15},{8,0},{9,1},... | collective-permute-start | bytes 1179656 | tf_op jit(solution)/shard_map/ppermute | solution.py:249
  12.0 17.6 %collective-permute-start.6 = (bf16[96,2048]{1,0:T(8,128)(2,1)S(1)}, bf16[96,2048]{1,0:T(8,128)(2,1)S(1)}, u32[]{:S(2)}, u32[]{:S(2)}) collective-permute-start(bf16[96,2048]{1,0:T(8,128)(2,1)S(1)} %get-tuple-element.125.refs_0_), channel_id=1, source_target_pairs={{0,1},{1,0},{2,3},{3,2},{4,5},{5,4},{6,7},{7,6},{8,9},{9,8},{10,11... | collective-permute-start | bytes 1179656 | tf_op jit(solution)/shard_map/ppermute | solution.py:249
  14.9 11.9 %collective-permute-start.7 = (bf16[48,2048]{1,0:T(8,128)(2,1)S(1)}, bf16[48,2048]{1,0:T(8,128)(2,1)S(1)}, u32[]{:S(2)}, u32[]{:S(2)}) collective-permute-start(bf16[48,2048]{1,0:T(8,128)(2,1)S(1)} %get-tuple-element.107.refs_0_), channel_id=1, source_target_pairs={{0,1},{1,0},{2,3},{3,2},{4,5},{5,4},{6,7},{7,6},{8,9},{9,8},{10,11... | collective-permute-start | bytes 589832 | tf_op jit(solution)/shard_map/ppermute | solution.py:249
  29.6 18.2 %collective-permute-start.8 = (bf16[96,2048]{1,0:T(8,128)(2,1)S(1)}, bf16[96,2048]{1,0:T(8,128)(2,1)S(1)}, u32[]{:S(2)}, u32[]{:S(2)}) collective-permute-start(bf16[96,2048]{1,0:T(8,128)(2,1)S(1)} %get-tuple-element.126), channel_id=1, source_target_pairs={{0,4},{1,5},{2,6},{3,7},{4,0},{5,1},{6,2},{7,3},{8,12},{9,13},{10,... | collective-permute-start | bytes 1179656 | tf_op jit(solution)/shard_map/ppermute | solution.py:249
  30.3 21.0 %collective-permute-start.3 = (bf16[96,2048]{1,0:T(8,128)(2,1)S(1)}, bf16[96,2048]{1,0:T(8,128)(2,1)S(1)}, u32[]{:S(2)}, u32[]{:S(2)}) collective-permute-start(bf16[96,2048]{1,0:T(8,128)(2,1)S(1)} %get-tuple-element.120), channel_id=1, source_target_pairs={{0,10},{1,11},{2,8},{3,9},{4,14},{5,15},{6,12},{7,13},{8,2},{9,3},... | collective-permute-start | bytes 1179656 | tf_op jit(solution)/shard_map/ppermute | solution.py:249
  33.6 17.7 %collective-permute-start.9 = (bf16[96,2048]{1,0:T(8,128)(2,1)S(1)}, bf16[96,2048]{1,0:T(8,128)(2,1)S(1)}, u32[]{:S(2)}, u32[]{:S(2)}) collective-permute-start(bf16[96,2048]{1,0:T(8,128)(2,1)S(1)} %collective-permute-done.5.refs_1_), channel_id=1, source_target_pairs={{0,1},{1,0},{2,3},{3,2},{4,5},{5,4},{6,7},{7,6},{8,9},{9,8},{10,11... | collective-permute-start | bytes 1179656 | tf_op jit(solution)/shard_map/ppermute | solution.py:249
  35.1 17.4 %collective-permute-start.10 = (bf16[96,2048]{1,0:T(8,128)(2,1)S(1)}, bf16[96,2048]{1,0:T(8,128)(2,1)S(1)}, u32[]{:S(2)}, u32[]{:S(2)}) collective-permute-start(bf16[96,2048]{1,0:T(8,128)(2,1)S(1)} %collective-permute-done.2.refs_4_), channel_id=1, source_target_pairs={{0,1},{1,0},{2,3},{3,2},{4,5},{5,4},{6,7},{7,6},{8,9},{9,8},{10,11... | collective-permute-start | bytes 1179656 | tf_op jit(solution)/shard_map/ppermute | solution.py:249
  52.5 21.4 %collective-permute-start.11 = (bf16[96,2048]{1,0:T(8,128)(2,1)S(1)}, bf16[96,2048]{1,0:T(8,128)(2,1)S(1)}, u32[]{:S(2)}, u32[]{:S(2)}) collective-permute-start(bf16[96,2048]{1,0:T(8,128)(2,1)S(1)} %get-tuple-element.129), channel_id=1, source_target_pairs={{0,6},{1,7},{2,4},{3,5},{4,2},{5,3},{6,0},{7,1},{8,14},{9,15},{10,... | collective-permute-start | bytes 1179656 | tf_op jit(solution)/shard_map/ppermute | solution.py:249
  53.8 17.6 %collective-permute-start.4 = (bf16[96,2048]{1,0:T(8,128)(2,1)S(1)}, bf16[96,2048]{1,0:T(8,128)(2,1)S(1)}, u32[]{:S(2)}, u32[]{:S(2)}) collective-permute-start(bf16[96,2048]{1,0:T(8,128)(2,1)S(1)} %get-tuple-element.121), channel_id=1, source_target_pairs={{0,12},{1,13},{2,14},{3,15},{4,8},{5,9},{6,10},{7,11},{8,4},{9,5},... | collective-permute-start | bytes 1179656 | tf_op jit(solution)/shard_map/ppermute | solution.py:249
  54.5 19.4 %collective-permute-start.12 = (bf16[96,2048]{1,0:T(8,128)(2,1)S(1)}, bf16[96,2048]{1,0:T(8,128)(2,1)S(1)}, u32[]{:S(2)}, u32[]{:S(2)}) collective-permute-start(bf16[96,2048]{1,0:T(8,128)(2,1)S(1)} %collective-permute-done.8.refs_2_), channel_id=1, source_target_pairs={{0,1},{1,0},{2,3},{3,2},{4,5},{5,4},{6,7},{7,6},{8,9},{9,8},{10,11... | collective-permute-start | bytes 1179656 | tf_op jit(solution)/shard_map/ppermute | solution.py:249
  56.0 17.9 %collective-permute-start.13 = (bf16[96,2048]{1,0:T(8,128)(2,1)S(1)}, bf16[96,2048]{1,0:T(8,128)(2,1)S(1)}, u32[]{:S(2)}, u32[]{:S(2)}) collective-permute-start(bf16[96,2048]{1,0:T(8,128)(2,1)S(1)} %collective-permute-done.3.refs_5_), channel_id=1, source_target_pairs={{0,1},{1,0},{2,3},{3,2},{4,5},{5,4},{6,7},{7,6},{8,9},{9,8},{10,11... | collective-permute-start | bytes 1179656 | tf_op jit(solution)/shard_map/ppermute | solution.py:249
  71.4 12.3 %collective-permute-start.15 = (bf16[96,2048]{1,0:T(8,128)(2,1)S(1)}, bf16[96,2048]{1,0:T(8,128)(2,1)S(1)}, u32[]{:S(2)}, u32[]{:S(2)}) collective-permute-start(bf16[96,2048]{1,0:T(8,128)(2,1)S(1)} %get-tuple-element.135), channel_id=1, source_target_pairs={{0,14},{1,15},{2,12},{3,13},{4,10},{5,11},{6,8},{7,9},{8,6},{9,7},... | collective-permute-start | bytes 1179656 | tf_op jit(solution)/shard_map/ppermute | solution.py:249
  73.9 17.2 %collective-permute-start.16 = (bf16[96,2048]{1,0:T(8,128)(2,1)S(1)}, bf16[96,2048]{1,0:T(8,128)(2,1)S(1)}, u32[]{:S(2)}, u32[]{:S(2)}) collective-permute-start(bf16[96,2048]{1,0:T(8,128)(2,1)S(1)} %collective-permute-done.11.refs_3_), channel_id=1, source_target_pairs={{0,1},{1,0},{2,3},{3,2},{4,5},{5,4},{6,7},{7,6},{8,9},{9,8},{10,11... | collective-permute-start | bytes 1179656 | tf_op jit(solution)/shard_map/ppermute | solution.py:249
  75.5 15.6 %collective-permute-start.17 = (bf16[96,2048]{1,0:T(8,128)(2,1)S(1)}, bf16[96,2048]{1,0:T(8,128)(2,1)S(1)}, u32[]{:S(2)}, u32[]{:S(2)}) collective-permute-start(bf16[96,2048]{1,0:T(8,128)(2,1)S(1)} %collective-permute-done.4.refs_6_), channel_id=1, source_target_pairs={{0,1},{1,0},{2,3},{3,2},{4,5},{5,4},{6,7},{7,6},{8,9},{9,8},{10,11... | collective-permute-start | bytes 1179656 | tf_op jit(solution)/shard_map/ppermute | solution.py:249
  76.0 15.1 %collective-permute-start.14 = (bf16[48,2048]{1,0:T(8,128)(2,1)S(1)}, bf16[48,2048]{1,0:T(8,128)(2,1)S(1)}, u32[]{:S(2)}, u32[]{:S(2)}) collective-permute-start(bf16[48,2048]{1,0:T(8,128)(2,1)S(1)} %get-tuple-element.132), channel_id=1, source_target_pairs={{0,2},{1,3},{2,0},{3,1},{4,6},{5,7},{6,4},{7,5},{8,10},{9,11},{10,... | collective-permute-start | bytes 589832 | tf_op jit(solution)/shard_map/ppermute | solution.py:249
  83.7 15.8 %collective-permute-start.20 = (bf16[48,2048]{1,0:T(8,128)(2,1)S(1)}, bf16[48,2048]{1,0:T(8,128)(2,1)S(1)}, u32[]{:S(2)}, u32[]{:S(2)}) collective-permute-start(bf16[48,2048]{1,0:T(8,128)(2,1)S(1)} %get-tuple-element.142), channel_id=1, source_target_pairs={{0,8},{1,9},{2,10},{3,11},{4,12},{5,13},{6,14},{7,15},{8,0},{9,1},... | collective-permute-start | bytes 589832 | tf_op jit(solution)/shard_map/ppermute | solution.py:249
  99.9 13.2 %collective-permute-start.23 = (bf16[144,2048]{1,0:T(8,128)(2,1)S(1)}, bf16[144,2048]{1,0:T(8,128)(2,1)S(1)}, u32[]{:S(2)}, u32[]{:S(2)}) collective-permute-start(bf16[144,2048]{1,0:T(8,128)(2,1)S(1)} %pad_maximum_fusion.1), channel_id=1, source_target_pairs={{0,1},{1,0},{2,3},{3,2},{4,5},{5,4},{6,7},{7,6},{8,9},{9,8},{10,11... | collective-permute-start | bytes 1769480 | tf_op jit(solution)/shard_map/ppermute | solution.py:249
  117.0 12.0 %collective-permute-start.26 = (bf16[96,2048]{1,0:T(8,128)(2,1)S(1)}, bf16[96,2048]{1,0:T(8,128)(2,1)S(1)}, u32[]{:S(2)}, u32[]{:S(2)}) collective-permute-start(bf16[96,2048]{1,0:T(8,128)(2,1)S(1)} %get-tuple-element.156), channel_id=1, source_target_pairs={{0,1},{1,0},{2,3},{3,2},{4,5},{5,4},{6,7},{7,6},{8,9},{9,8},{10,11... | collective-permute-start | bytes 1179656 | tf_op jit(solution)/shard_map/ppermute | solution.py:249
  118.5 16.2 %collective-permute-start.27 = (bf16[96,2048]{1,0:T(8,128)(2,1)S(1)}, bf16[96,2048]{1,0:T(8,128)(2,1)S(1)}, u32[]{:S(2)}, u32[]{:S(2)}) collective-permute-start(bf16[96,2048]{1,0:T(8,128)(2,1)S(1)} %get-tuple-element.158), channel_id=1, source_target_pairs={{0,1},{1,0},{2,3},{3,2},{4,5},{5,4},{6,7},{7,6},{8,9},{9,8},{10,11... | collective-permute-start | bytes 1179656 | tf_op jit(solution)/shard_map/ppermute | solution.py:249
  134.7 16.5 %collective-permute-start.28 = (bf16[192,2048]{1,0:T(8,128)(2,1)S(1)}, bf16[192,2048]{1,0:T(8,128)(2,1)S(1)}, u32[]{:S(2)}, u32[]{:S(2)}) collective-permute-start(bf16[192,2048]{1,0:T(8,128)(2,1)S(1)} %pad_maximum_fusion), channel_id=1, source_target_pairs={{0,1},{1,0},{2,3},{3,2},{4,5},{5,4},{6,7},{7,6},{8,9},{9,8},{10,11... | collective-permute-start | bytes 2359304 | tf_op jit(solution)/shard_map/ppermute | solution.py:249
  136.3 13.0 %collective-permute-start.29 = (bf16[48,2048]{1,0:T(8,128)(2,1)S(1)}, bf16[48,2048]{1,0:T(8,128)(2,1)S(1)}, u32[]{:S(2)}, u32[]{:S(2)}) collective-permute-start(bf16[48,2048]{1,0:T(8,128)(2,1)S(1)} %get-tuple-element.165), channel_id=1, source_target_pairs={{0,8},{1,9},{2,10},{3,11},{4,12},{5,13},{6,14},{7,15},{8,0},{9,1},... | collective-permute-start | bytes 589832 | tf_op jit(solution)/shard_map/ppermute | solution.py:249
  137.6 13.6 %collective-permute-start.30 = (bf16[48,2048]{1,0:T(8,128)(2,1)S(1)}, bf16[48,2048]{1,0:T(8,128)(2,1)S(1)}, u32[]{:S(2)}, u32[]{:S(2)}) collective-permute-start(bf16[48,2048]{1,0:T(8,128)(2,1)S(1)} %get-tuple-element.166), channel_id=1, source_target_pairs={{0,10},{1,11},{2,8},{3,9},{4,14},{5,15},{6,12},{7,13},{8,2},{9,3},... | collective-permute-start | bytes 589832 | tf_op jit(solution)/shard_map/ppermute | solution.py:249
  151.2 16.5 %collective-permute-start.31 = (bf16[96,2048]{1,0:T(8,128)(2,1)S(1)}, bf16[96,2048]{1,0:T(8,128)(2,1)S(1)}, u32[]{:S(2)}, u32[]{:S(2)}) collective-permute-start(bf16[96,2048]{1,0:T(8,128)(2,1)S(1)} %get-tuple-element.167), channel_id=1, source_target_pairs={{0,1},{1,0},{2,3},{3,2},{4,5},{5,4},{6,7},{7,6},{8,9},{9,8},{10,11... | collective-permute-start | bytes 1179656 | tf_op jit(solution)/shard_map/ppermute | solution.py:249
  152.5 15.2 %collective-permute-start.32 = (bf16[48,2048]{1,0:T(8,128)(2,1)S(1)}, bf16[48,2048]{1,0:T(8,128)(2,1)S(1)}, u32[]{:S(2)}, u32[]{:S(2)}) collective-permute-start(bf16[48,2048]{1,0:T(8,128)(2,1)S(1)} %get-tuple-element.169), channel_id=1, source_target_pairs={{0,12},{1,13},{2,14},{3,15},{4,8},{5,9},{6,10},{7,11},{8,4},{9,5},... | collective-permute-start | bytes 589832 | tf_op jit(solution)/shard_map/ppermute | solution.py:249
  155.3 12.4 %collective-permute-start.33 = (bf16[48,2048]{1,0:T(8,128)(2,1)S(1)}, bf16[48,2048]{1,0:T(8,128)(2,1)S(1)}, u32[]{:S(2)}, u32[]{:S(2)}) collective-permute-start(bf16[48,2048]{1,0:T(8,128)(2,1)S(1)} %get-tuple-element.170), channel_id=1, source_target_pairs={{0,14},{1,15},{2,12},{3,13},{4,10},{5,11},{6,8},{7,9},{8,6},{9,7},... | collective-permute-start | bytes 589832 | tf_op jit(solution)/shard_map/ppermute | solution.py:249
  172.0 12.1 %collective-permute-start.35 = (bf16[96,2048]{1,0:T(8,128)(2,1)S(1)}, bf16[96,2048]{1,0:T(8,128)(2,1)S(1)}, u32[]{:S(2)}, u32[]{:S(2)}) collective-permute-start(bf16[96,2048]{1,0:T(8,128)(2,1)S(1)} %get-tuple-element.173), channel_id=1, source_target_pairs={{0,1},{1,0},{2,3},{3,2},{4,5},{5,4},{6,7},{7,6},{8,9},{9,8},{10,11... | collective-permute-start | bytes 1179656 | tf_op jit(solution)/shard_map/ppermute | solution.py:249
  173.2 16.6 %collective-permute-start.36 = (bf16[96,2048]{1,0:T(8,128)(2,1)S(1)}, bf16[96,2048]{1,0:T(8,128)(2,1)S(1)}, u32[]{:S(2)}, u32[]{:S(2)}) collective-permute-start(bf16[96,2048]{1,0:T(8,128)(2,1)S(1)} %pad_maximum_fusion.3), channel_id=1, source_target_pairs={{0,1},{1,0},{2,3},{3,2},{4,5},{5,4},{6,7},{7,6},{8,9},{9,8},{10,11... | collective-permute-start | bytes 1179656 | tf_op jit(solution)/shard_map/ppermute | solution.py:249
  174.2 16.8 %collective-permute-start.39 = (bf16[48,2048]{1,0:T(8,128)(2,1)S(1)}, bf16[48,2048]{1,0:T(8,128)(2,1)S(1)}, u32[]{:S(2)}, u32[]{:S(2)}) collective-permute-start(bf16[48,2048]{1,0:T(8,128)(2,1)S(1)} %get-tuple-element.182), channel_id=1, source_target_pairs={{0,8},{1,9},{2,10},{3,11},{4,12},{5,13},{6,14},{7,15},{8,0},{9,1},... | collective-permute-start | bytes 589832 | tf_op jit(solution)/shard_map/ppermute | solution.py:249
  174.2 16.8 %collective-permute-start.40 = (bf16[48,2048]{1,0:T(8,128)(2,1)S(1)}, bf16[48,2048]{1,0:T(8,128)(2,1)S(1)}, u32[]{:S(2)}, u32[]{:S(2)}) collective-permute-start(bf16[48,2048]{1,0:T(8,128)(2,1)S(1)} %get-tuple-element.183), channel_id=1, source_target_pairs={{0,10},{1,11},{2,8},{3,9},{4,14},{5,15},{6,12},{7,13},{8,2},{9,3},... | collective-permute-start | bytes 589832 | tf_op jit(solution)/shard_map/ppermute | solution.py:249
  177.2 15.4 %collective-permute-start.41 = (bf16[48,2048]{1,0:T(8,128)(2,1)S(1)}, bf16[48,2048]{1,0:T(8,128)(2,1)S(1)}, u32[]{:S(2)}, u32[]{:S(2)}) collective-permute-start(bf16[48,2048]{1,0:T(8,128)(2,1)S(1)} %get-tuple-element.185), channel_id=1, source_target_pairs={{0,6},{1,7},{2,4},{3,5},{4,2},{5,3},{6,0},{7,1},{8,14},{9,15},{10,... | collective-permute-start | bytes 589832 | tf_op jit(solution)/shard_map/ppermute | solution.py:249
  203.8 11.8 %collective-permute-start.46 = (bf16[48,2048]{1,0:T(8,128)(2,1)S(1)}, bf16[48,2048]{1,0:T(8,128)(2,1)S(1)}, u32[]{:S(2)}, u32[]{:S(2)}) collective-permute-start(bf16[48,2048]{1,0:T(8,128)(2,1)S(1)} %get-tuple-element.192), channel_id=1, source_target_pairs={{0,6},{1,7},{2,4},{3,5},{4,2},{5,3},{6,0},{7,1},{8,14},{9,15},{10,... | collective-permute-start | bytes 589832 | tf_op jit(solution)/shard_map/ppermute | solution.py:249
  (29 other events, 206.4 us)
